TPU v7x, 32 devices: a whole 2x2x4 slice. The times are simulated.
32 devices in a mesh: grp: 2 (over y), vec: 4 (over z), walk: 2 (over x), orb: 2 (over core).
Axes of the slice: x: 2, y: 2, z: 4, core: 2. Of those that a mesh axis runs over, the one named last changes fastest.
Arguments:
- walkers: bfloat16 [32, 512, 128], P(('grp', 'walk'), 'orb'), parts along dimension 0, may hold values from -3 to 3
- inv_intersection: bfloat16 [32, 128, 128], P(('grp', 'walk')), parts along dimension 0, may hold values from -0.5 to 0.5
- trial: bfloat16 [512, 128], replicated, may hold values from -0.25 to 0.25
- vectors: bfloat16 [32, 512, 512], P('vec', 'orb')
- aux_field: float32 [32, 32], P(('grp', 'walk'), 'vec'), parts along dimension 0, may hold values from -5 to 5
- log_weight: float32 [32], P(('grp', 'walk')), parts along dimension 0, may hold values from -4 to 4
- copy_list: int32 [32], P(('grp', 'walk')), parts along dimension 0, may hold values from 0 to 15
Outputs:
- walkers_out: bfloat16 [32, 512, 128], P(('grp', 'walk'), 'orb'), parts along dimension 0
- weights_out: float32 [32], P(('grp', 'walk')), parts along dimension 0
There are 2 independent parts, one for each index of `grp`. A program takes and returns all parts, laid end to end along the dimension named above; an argument that names none is the same for every part. Nothing has to cross between parts.
Inputs may be any that keep to these rules, and one draw needn't show every extreme that they name: `copy_list`: the walker, within the same ensemble, whose copy fills the slot.
All inputs are finite; a program needn't handle non-finite values.
Results may differ from a plain program's by a relative error of at most 0.008.
Values may be sent and summed in bfloat16 or wider, within the bound.
No kernel may reach another device: no remote copies, remote signals or barrier semaphores. Data moves between devices by JAX's collectives and lax.ppermute only.
A program may use at most 64 MiB of HBM per device.

v0:
```python
from functools import partial
import math

import jax
import jax.numpy as jnp
from jax import lax
from jax.sharding import PartitionSpec as P

ORDER = 6


step_root = math.sqrt(0.08)


def fold_rows(operator, carry, piece, start):
    return jnp.einsum("wnm,wme->wne", operator, piece, preferred_element_type=jnp.float32)


def per_device(walkers, inv_intersection, trial, vectors, aux_field, log_weight, copy_list):
    green = jnp.einsum(
        "wne,wef->wnf", walkers, inv_intersection, preferred_element_type=jnp.float32
    ).astype(jnp.bfloat16)
    mixed = jnp.einsum("gnm,me->gne", vectors, trial, preferred_element_type=jnp.float32).astype(
        jnp.bfloat16
    )
    partial_bias = jnp.einsum("wne,gne->wg", green, mixed, preferred_element_type=jnp.float32)
    bias = lax.psum(partial_bias, "orb")
    shift = -step_root * bias
    field = aux_field - shift
    own_factor = jnp.sum(aux_field * shift - 0.5 * shift * shift, axis=1)
    new_log = log_weight + lax.psum(own_factor, "vec")
    weighted = (field * step_root).astype(jnp.bfloat16)
    local_operator = jnp.einsum(
        "wg,gnm->wnm", weighted, vectors, preferred_element_type=jnp.float32
    )
    operator = lax.psum(local_operator, "vec").astype(jnp.bfloat16)
    running = walkers.astype(jnp.float32)
    folder = partial(fold_rows, operator)
    operand = walkers
    for degree in range(1, ORDER + 1):
        initial = jnp.zeros(running.shape, jnp.float32)
        summed = folder(initial, lax.all_gather(operand, "orb", axis=1, tiled=True), jnp.int32(0))
        new_term = (summed / degree).astype(jnp.bfloat16)
        running = running + new_term.astype(jnp.float32)
        if degree < ORDER:
            operand = new_term
    propagated = running.astype(jnp.bfloat16)
    every_walker = lax.all_gather(propagated, "walk", axis=0, tiled=True)
    every_log = lax.all_gather(new_log, "walk", axis=0, tiled=True)
    return (every_walker[copy_list], every_log[copy_list])


def solution(mesh):
    return jax.shard_map(
        per_device,
        mesh=mesh,
        in_specs=(
            P(("grp", "walk"), "orb", None),
            P(("grp", "walk"), None, None),
            P(),
            P("vec", "orb", None),
            P(("grp", "walk"), "vec"),
            P(("grp", "walk")),
            P(("grp", "walk")),
        ),
        out_specs=(P(("grp", "walk"), "orb", None), P(("grp", "walk"))),
        check_vma=False,
    )
```

profile of v0, /device:TPU:0, one launch (start us, length us, event | category | flops | bytes accessed | tf_op | source)
XLA Modules:
  0.0 276.8 jit_solution(15812537913773210420)
XLA Ops:
  7.2 0.0 copy-start
  7.2 0.0 copy-start.3
  7.2 0.0 all-gather.8.cloned.1.call-start
  7.2 0.7 all-gather.8.cloned.1.call-update
  7.9 0.0 all-gather.10.cloned.1.call-start
  8.0 1.4 convolution_convert_fusion.1
  9.4 0.4 copy.23
  9.8 0.0 copy-start.4
  9.8 1.5 convolution_convert_fusion.2
  11.3 1.4 copy.24
  12.7 0.4 convolution_bitcast_fusion
  13.2 2.6 psum.21
  15.8 3.3 %fusion = f32[8,256,512]{2,0,1:T(8,128)} fusion(bf16[8,256,512]{2,1,0:T(8,128)(2,1)S(1)} %copy-done, f32[8,8]{1,0:T(8,128)S(1)} %copy-done.4, f32[8,8]{1,0:T(8,128)S(1)} %psum.21), kind=kOutput, calls=%fused_computation.2 | convolution fusion | flops 16777472 | bytes 6291968 | tf_op jit(solution)/shard_map/wg,gnm->wnm/dot_general | solution.py:33
  19.1 0.1 subtract_reduce_fusion
  19.2 150.7 %all-reduce.3 = (bf16[8,256,512]{2,0,1:T(8,128)(2,1)}, f32[8]{0:T(128)S(1)}) all-reduce(f32[8,256,512]{2,0,1:T(8,128)} %fusion, f32[8]{0:T(128)S(1)} %subtract_reduce_fusion), channel_id=1, replica_groups=mesh['grp'=2,'vec'=4,'walk'=2,'orb'=2] {'vec'}, use_global_device_ids=true, to_apply=%region_1.0 | all-reduce | flops 1048584 | bytes 6291520 | tf_op jit(solution)/shard_map/psum | solution.py:36
  169.9 4.0 %convolution_convert_fusion = bf16[8,256,128]{2,1,0:T(8,128)(2,1)} fusion(bf16[8,512,128]{2,1,0:T(8,128)(2,1)} %all-gather.8.cloned.1.call-done, bf16[8,256,512]{2,0,1:T(8,128)(2,1)} %get-tuple-element.2), kind=kOutput, calls=%fused_computation.9 | convolution fusion | flops 268697600 | bytes 3670016 | tf_op jit(solution)/shard_map/wnm,wme->wne/dot_general | solution.py:16
  173.9 0.0 all-gather.10.cloned.1.call-update
  173.9 0.0 all-gather.12.cloned.1.call-start
  173.9 8.3 %all-gather.10.cloned.1.call-done = bf16[8,512,128]{2,1,0:T(8,128)(2,1)} async-done(((bf16[8,256,128]{2,1,0:T(8,128)(2,1)}), bf16[8,512,128]{2,1,0:T(8,128)(2,1)}) %all-gather.10.cloned.1.call-update) | async-done | bytes 1048592 | tf_op jit(solution)/shard_map/all_gather | solution.py:42
  182.2 4.1 %fusion.2 = bf16[8,256,128]{2,1,0:T(8,128)(2,1)} fusion(bf16[8,512,128]{2,1,0:T(8,128)(2,1)} %all-gather.10.cloned.1.call-done, bf16[8,256,512]{2,0,1:T(8,128)(2,1)} %get-tuple-element.2), kind=kOutput, calls=%fused_computation.11 | convolution fusion | flops 268959744 | bytes 3670016 | tf_op jit(solution)/shard_map/wnm,wme->wne/dot_general | solution.py:16
  186.3 0.0 all-gather.12.cloned.1.call-update
  186.3 0.0 all-gather.14.cloned.1.call-start
  186.4 10.3 %all-gather.12.cloned.1.call-done = bf16[8,512,128]{2,1,0:T(8,128)(2,1)} async-done(((bf16[8,256,128]{2,1,0:T(8,128)(2,1)}), bf16[8,512,128]{2,1,0:T(8,128)(2,1)}) %all-gather.12.cloned.1.call-update) | async-done | bytes 1048592 | tf_op jit(solution)/shard_map/all_gather | solution.py:42
  196.7 4.1 %fusion.3 = bf16[8,256,128]{2,1,0:T(8,128)(2,1)} fusion(bf16[8,512,128]{2,1,0:T(8,128)(2,1)} %all-gather.12.cloned.1.call-done, bf16[8,256,512]{2,0,1:T(8,128)(2,1)} %get-tuple-element.2), kind=kOutput, calls=%fused_computation.12 | convolution fusion | flops 268959744 | bytes 3670016 | tf_op jit(solution)/shard_map/wnm,wme->wne/dot_general | solution.py:16
  200.7 0.0 all-gather.14.cloned.1.call-update
  200.7 0.0 all-gather.16.cloned.1.call-start
  200.8 10.3 %all-gather.14.cloned.1.call-done = bf16[8,512,128]{2,1,0:T(8,128)(2,1)} async-done(((bf16[8,256,128]{2,1,0:T(8,128)(2,1)}), bf16[8,512,128]{2,1,0:T(8,128)(2,1)}) %all-gather.14.cloned.1.call-update) | async-done | bytes 1048592 | tf_op jit(solution)/shard_map/all_gather | solution.py:42
  211.1 4.0 %fusion.4 = bf16[8,256,128]{2,1,0:T(8,128)(2,1)} fusion(bf16[8,512,128]{2,1,0:T(8,128)(2,1)} %all-gather.14.cloned.1.call-done, bf16[8,256,512]{2,0,1:T(8,128)(2,1)} %get-tuple-element.2), kind=kOutput, calls=%fused_computation.13 | convolution fusion | flops 268959744 | bytes 3670016 | tf_op jit(solution)/shard_map/wnm,wme->wne/dot_general | solution.py:16
  215.1 0.0 all-gather.16.cloned.1.call-update
  215.2 0.0 copy-start.1
  215.2 0.0 copy-start.2
  215.2 0.0 all-gather.18.cloned.1.call-start
  215.2 10.3 %all-gather.16.cloned.1.call-done = bf16[8,512,128]{2,1,0:T(8,128)(2,1)} async-done(((bf16[8,256,128]{2,1,0:T(8,128)(2,1)}), bf16[8,512,128]{2,1,0:T(8,128)(2,1)}) %all-gather.16.cloned.1.call-update) | async-done | bytes 1048592 | tf_op jit(solution)/shard_map/all_gather | solution.py:42
  225.5 4.0 %fusion.5 = bf16[8,256,128]{2,1,0:T(8,128)(2,1)} fusion(bf16[8,512,128]{2,1,0:T(8,128)(2,1)} %all-gather.16.cloned.1.call-done, bf16[8,256,512]{2,0,1:T(8,128)(2,1)} %get-tuple-element.2), kind=kOutput, calls=%fused_computation.14 | convolution fusion | flops 268959744 | bytes 3670016 | tf_op jit(solution)/shard_map/wnm,wme->wne/dot_general | solution.py:16
  229.6 0.0 all-gather.18.cloned.1.call-update
  229.6 0.0 copy-start.7
  229.6 0.0 copy-start.5
  229.6 0.0 copy-start.6
  229.6 0.0 all-gather.20.cloned.1.call-start
  229.7 10.3 %all-gather.18.cloned.1.call-done = bf16[8,512,128]{2,1,0:T(8,128)(2,1)} async-done(((bf16[8,256,128]{2,1,0:T(8,128)(2,1)}), bf16[8,512,128]{2,1,0:T(8,128)(2,1)}) %all-gather.18.cloned.1.call-update) | async-done | bytes 1048592 | tf_op jit(solution)/shard_map/all_gather | solution.py:42
  239.9 4.7 %fusion.9 = bf16[8,256,128]{2,1,0:T(8,128)(2,1)} fusion(bf16[8,512,128]{2,1,0:T(8,128)(2,1)} %all-gather.18.cloned.1.call-done, bf16[8,256,128]{2,1,0:T(8,128)(2,1)} %fusion.5, bf16[8,256,128]{2,1,0:T(8,128)(2,1)} %fusion.4, bf16[8,256,128]{2,1,0:T(8,128)(2,1)} %fusion.3, bf16[8,256,128]{2,1,0:T(8,128)(2,1)} %fusion.2, ...), kind=kOutput, calls=%fused_computation.18 | convolution fusion | flops 272629760 | bytes 6815744 | tf_op jit(solution)/shard_map/wnm,wme->wne/dot_general | solution.py:16
  244.7 0.0 all-gather.20.cloned.1.call-update
  244.7 0.6 dynamic-slice
  246.0 0.1 add_dynamic-update-slice_fusion
  246.1 4.9 %all-reduce = f32[16]{0:T(128)S(1)} all-reduce(f32[16]{0:T(128)S(1)} %add_dynamic-update-slice_fusion), channel_id=1, replica_groups=mesh['grp'=2,'vec'=4,'walk'=2,'orb'=2] {'walk'}, use_global_device_ids=true, to_apply=%add | all-reduce | flops 16 | bytes 128
  251.0 1.2 gather_fusion.1
  252.2 15.2 %all-gather.20.cloned.1.call-done = bf16[16,256,128]{2,1,0:T(8,128)(2,1)} async-done(((bf16[8,256,128]{2,1,0:T(8,128)(2,1)}), bf16[16,256,128]{2,1,0:T(8,128)(2,1)}) %all-gather.20.cloned.1.call-update) | async-done | bytes 1048592 | tf_op jit(solution)/shard_map/all_gather | solution.py:48
  267.3 2.6 gather_fusion
  (12 shorter events, 0.0 us)
Async XLA Ops:
  7.2 2.6 copy-start
  7.2 2.6 copy-start.3
  7.2 162.7 %all-gather.8.cloned.1.call-start = ((), (), s32[]{:S(2)}) async-start(), calls=%async_computation | async-start | bytes 1572864 | tf_op jit(solution)/shard_map/all_gather | solution.py:42
  7.9 174.3 %all-gather.10.cloned.1.call-start = ((), (), s32[]{:S(2)}) async-start(), calls=%async_computation.1 | async-start | bytes 1572864 | tf_op jit(solution)/shard_map/all_gather | solution.py:42
  9.8 6.0 %copy-start.4 = (f32[8,8]{1,0:T(8,128)S(1)}, f32[8,8]{1,0:T(8,128)}, u32[]{:S(2)}) copy-start(f32[8,8]{1,0:T(8,128)} %param.11) | copy-start | bytes 772
  173.9 22.8 %all-gather.12.cloned.1.call-start = ((), (), s32[]{:S(2)}) async-start(), calls=%async_computation.2 | async-start | bytes 1572864 | tf_op jit(solution)/shard_map/all_gather | solution.py:42
  186.3 24.8 %all-gather.14.cloned.1.call-start = ((), (), s32[]{:S(2)}) async-start(), calls=%async_computation.3 | async-start | bytes 1572864 | tf_op jit(solution)/shard_map/all_gather | solution.py:42
  200.7 24.8 %all-gather.16.cloned.1.call-start = ((), (), s32[]{:S(2)}) async-start(), calls=%async_computation.4 | async-start | bytes 1572864 | tf_op jit(solution)/shard_map/all_gather | solution.py:42
  215.2 24.8 %copy-start.1 = (bf16[8,256,128]{2,1,0:T(8,128)(2,1)S(1)}, bf16[8,256,128]{2,1,0:T(8,128)(2,1)}, u32[]{:S(2)}) copy-start(bf16[8,256,128]{2,1,0:T(8,128)(2,1)} %param.7) | copy-start | bytes 1572868
  215.2 24.8 %copy-start.2 = (bf16[8,256,128]{2,1,0:T(8,128)(2,1)S(1)}, bf16[8,256,128]{2,1,0:T(8,128)(2,1)}, u32[]{:S(2)}) copy-start(bf16[8,256,128]{2,1,0:T(8,128)(2,1)} %convolution_convert_fusion) | copy-start | bytes 1572868
  215.2 24.8 %all-gather.18.cloned.1.call-start = ((), (), s32[]{:S(2)}) async-start(), calls=%async_computation.5 | async-start | bytes 1572864 | tf_op jit(solution)/shard_map/all_gather | solution.py:42
  229.6 15.1 %copy-start.7 = (u32[32]{0:T(128)S(1)}, u32[32]{0:T(128)}, u32[]{:S(2)}) copy-start(u32[32]{0:T(128)} %constant.31) | copy-start | bytes 388
  229.6 16.4 %copy-start.5 = (f32[8]{0:T(128)S(1)}, f32[8]{0:T(128)}, u32[]{:S(2)}) copy-start(f32[8]{0:T(128)} %param.12) | copy-start | bytes 100
  229.6 21.4 %copy-start.6 = (s32[8]{0:T(128)S(1)}, s32[8]{0:T(128)}, u32[]{:S(2)}) copy-start(s32[8]{0:T(128)} %param.13) | copy-start | bytes 100
  229.6 37.7 %all-gather.20.cloned.1.call-start = ((), (), s32[]{:S(2)}) async-start(), calls=%async_computation.6 | async-start | bytes 1572864 | tf_op jit(solution)/shard_map/all_gather | solution.py:48
Sparse Core Ops, SparseCore 0:
  9.5 11.7 all-gather.7
  174.0 8.1 all-gather.9
  186.4 10.1 all-gather.11
  200.9 10.1 all-gather.13
  215.3 10.1 all-gather.15
  229.7 10.1 all-gather.17
  244.8 22.4 all-gather.19
where the time goes:
time: 277 us
  blocking collectives  158 us (57%)
  waiting for transfers between devices  65.4 us (24%)
  matrix products  31.5 us (11%)
  between operations  14.9 us (5%)
  local copies, waits for them, and re-layouts  6.25 us (2%)
    psum x1, blocking collectives, per_device(): operator = lax.psum(local_operator, 'vec').astype(jnp.bfloat16)  151 us
    all_gather x6, waiting for transfers between devices, per_device(): lax.all_gather(operand, 'orb', axis=1, tiled=True)  49.4 us
    dot_general x6, matrix products, fold_rows(): jnp.einsum('wnm,wme->wne', operator, piece, preferred_element_type=jnp.fl...  24.9 us
    all_gather x1, waiting for transfers between devices, per_device(): every_walker = lax.all_gather(propagated, 'walk', axis=0, tiled=True)  15.2 us
  transfers between devices with their start and end apart: 7, of which 6 were waited for; matrix products, arithmetic and copies ran while one was open for 4% of the time, Pallas kernels for 0%

commit v1 on v0

--- a/solution.py
+++ b/solution.py
@@ -4,19 +4,40 @@
 import jax
 import jax.numpy as jnp
 from jax import lax
+from jax.experimental import pallas as pl
+from jax.experimental.pallas import tpu as pltpu
 from jax.sharding import PartitionSpec as P
 
 ORDER = 6
-
+LANE = 128
 
 step_root = math.sqrt(0.08)
+
+VMEM = pltpu.VMEM
+SMEM = pltpu.SMEM
+
+
+def in_vmem():
+    return pl.BlockSpec(memory_space=VMEM)
+
+
+def in_smem():
+    return pl.BlockSpec(memory_space=SMEM)
+
+
+def in_any():
+    return pl.BlockSpec(memory_space=pl.ANY)
+
+
+def mm(a, b):
+    return jnp.dot(a, b, preferred_element_type=jnp.float32)
 
 
 def fold_rows(operator, carry, piece, start):
     return jnp.einsum("wnm,wme->wne", operator, piece, preferred_element_type=jnp.float32)
 
 
-def per_device(walkers, inv_intersection, trial, vectors, aux_field, log_weight, copy_list):
+def general_device(walkers, inv_intersection, trial, vectors, aux_field, log_weight, copy_list):
     green = jnp.einsum(
         "wne,wef->wnf", walkers, inv_intersection, preferred_element_type=jnp.float32
     ).astype(jnp.bfloat16)
@@ -50,19 +71,343 @@
     return (every_walker[copy_list], every_log[copy_list])
 
 
+def bias_kernel(walkers_hbm, inv_hbm, trial_hbm, vec_hbm, out_ref,
+                walkers_ref, inv_ref, trial_ref, vec_ref, green_ref, sems):
+    n_walk = walkers_hbm.shape[0]
+    n_vec = vec_hbm.shape[0]
+    copies = [
+        pltpu.make_async_copy(walkers_hbm, walkers_ref, sems.at[0]),
+        pltpu.make_async_copy(inv_hbm, inv_ref, sems.at[1]),
+        pltpu.make_async_copy(trial_hbm, trial_ref, sems.at[2]),
+    ]
+    vec_copies = [
+        pltpu.make_async_copy(vec_hbm.at[g], vec_ref.at[g], sems.at[3 + g]) for g in range(n_vec)
+    ]
+    for copy in copies + vec_copies:
+        copy.start()
+    copies[0].wait()
+    copies[1].wait()
+    for w in range(n_walk):
+        green_ref[w] = mm(walkers_ref[w], inv_ref[w]).astype(jnp.bfloat16).astype(jnp.float32)
+    copies[2].wait()
+    trial = trial_ref[...]
+    lane = lax.broadcasted_iota(jnp.int32, (n_walk, n_vec), 1)
+    total = jnp.zeros((n_walk, n_vec), jnp.float32)
+    for g in range(n_vec):
+        vec_copies[g].wait()
+        mixed = mm(vec_ref[g], trial).astype(jnp.bfloat16).astype(jnp.float32)
+        rows = [jnp.sum(green_ref[w] * mixed, axis=0, keepdims=True) for w in range(n_walk)]
+        column = jnp.sum(jnp.concatenate(rows, axis=0), axis=1, keepdims=True)
+        total = total + jnp.where(lane == g, column, 0.0)
+    out_ref[...] = total
+
+
+def partial_bias_of(walkers, inv, trial, vectors):
+    n_walk, n_vec = walkers.shape[0], vectors.shape[0]
+    return pl.pallas_call(
+        bias_kernel,
+        out_shape=jax.ShapeDtypeStruct((n_walk, n_vec), jnp.float32),
+        in_specs=[in_any()] * 4,
+        out_specs=in_vmem(),
+        scratch_shapes=[
+            VMEM(walkers.shape, walkers.dtype),
+            VMEM(inv.shape, inv.dtype),
+            VMEM(trial.shape, trial.dtype),
+            VMEM(vectors.shape, vectors.dtype),
+            VMEM(walkers.shape, jnp.float32),
+            pltpu.SemaphoreType.DMA((3 + n_vec,)),
+        ],
+        name="bias",
+    )(walkers, inv, trial, vectors)
+
+
+def operator_kernel(n_line, n_orb, group, place_ref, source_ref, bias0, bias1, bias2, bias3, aux_ref,
+                    vec_hbm, factor_ref, *rest):
+    piece_refs = rest[:n_line]
+    vec_ref, field_ref, weight_ref, sems = rest[n_line:]
+    n_walk, n_vec = bias0.shape
+    n_rows, n_cols = vec_hbm.shape[1:]
+    half = n_rows // 2
+    vec_copies = [
+        pltpu.make_async_copy(
+            vec_hbm.at[:, pl.ds(j * group, group)], vec_ref.at[:, pl.ds(j * group, group)], sems.at[j]
+        )
+        for j in range(n_rows // group)
+    ]
+    for copy in vec_copies:
+        copy.start()
+    z, o = place_ref[0], place_ref[1]
+    own = bias0[...] + bias1[...]
+    other = bias2[...] + bias3[...]
+    shift = -step_root * jnp.concatenate([own, other], axis=0)
+    aux = aux_ref[...]
+    field_ref[...] = (aux - shift) * step_root
+    factor_ref[...] = jnp.sum(aux * shift - 0.5 * shift * shift, axis=1, keepdims=True)
+    n_z = n_line // n_orb
+    for k in range(n_line):
+        to_z = lax.rem(z + k // n_orb, n_z)
+        to_o = lax.rem(o + k % n_orb, n_orb)
+        row = source_ref[to_z * n_orb + to_o]
+        weight_ref[pl.ds(k, 1), :] = field_ref[pl.ds(row, 1), :]
+    weighted = weight_ref[...].astype(jnp.bfloat16)
+    rows_of = lax.broadcasted_iota(jnp.int32, (n_line * group, n_line), 0) // group
+    pick = (rows_of == lax.broadcasted_iota(jnp.int32, (n_line * group, n_line), 1))
+    tall = mm(pick.astype(jnp.float32).astype(jnp.bfloat16), weighted).astype(jnp.bfloat16)
+    cols_of = lax.broadcasted_iota(jnp.int32, (n_vec, n_vec * group), 1) // group
+    spread = (cols_of == lax.broadcasted_iota(jnp.int32, (n_vec, n_vec * group), 0))
+    wide = mm(tall, spread.astype(jnp.float32).astype(jnp.bfloat16))
+    row_in = lax.rem(lax.broadcasted_iota(jnp.int32, wide.shape, 0), group)
+    col_in = lax.rem(lax.broadcasted_iota(jnp.int32, wide.shape, 1), group)
+    spreader = jnp.where(row_in == col_in, wide, 0.0).astype(jnp.bfloat16)
+
+    def block(row, col_block):
+        col = pl.multiple_of(lax.rem(col_block, n_cols // LANE) * LANE, LANE)
+        stack = vec_ref[:, pl.ds(row, group), pl.ds(col, LANE)]
+        return mm(spreader, stack.reshape(n_vec * group, LANE)).reshape(n_line, group, LANE)
+
+    first = o * (n_rows // LANE)
+    for copy in vec_copies:
+        copy.wait()
+    rest_rows = 4 * half
+    for k in range(n_line):
+        piece_refs[k][pl.ds(rest_rows, 16), :] = jnp.zeros((16, LANE), jnp.bfloat16)
+    diag_rows = [jnp.zeros((1, LANE), jnp.float32) for _ in range(n_line)]
+    for j in range(half // group):
+        low = j * group
+        upper = block(low, first)
+        lower = block(half + low, first + 1)
+        i_at = low + lax.broadcasted_iota(jnp.int32, (group, LANE), 0)
+        j_at = lax.broadcasted_iota(jnp.int32, (group, LANE), 1)
+        next0 = block(low, first + 1)
+        next1 = block(half + low, first + 2)
+        extra = block(pl.multiple_of(o * half, half) + low, first + 2 + o)
+        for k in range(n_line):
+            merged = jnp.where(i_at <= j_at, upper[k], lower[k])
+            diag_rows[k] = diag_rows[k] + jnp.sum(
+                jnp.where(i_at == j_at, lower[k], 0.0), axis=0, keepdims=True
+            )
+            piece_refs[k][pl.ds(low, group), :] = merged.astype(jnp.bfloat16)
+            piece_refs[k][pl.ds(half + low, group), :] = next0[k].astype(jnp.bfloat16)
+            piece_refs[k][pl.ds(2 * half + low, group), :] = next1[k].astype(jnp.bfloat16)
+            piece_refs[k][pl.ds(3 * half + low, group), :] = extra[k].astype(jnp.bfloat16)
+    for k in range(n_line):
+        piece_refs[k][pl.ds(rest_rows, 16), :] = jnp.broadcast_to(
+            diag_rows[k], (16, LANE)
+        ).astype(jnp.bfloat16)
+
+
+def partial_operators(place, source, biases, aux, vectors, n_line, n_orb):
+    n_walk, n_vec = biases[0].shape
+    n_rows = vectors.shape[1]
+    group = 2 * LANE // n_vec
+    piece = jax.ShapeDtypeStruct((2 * n_rows + 16, LANE), jnp.bfloat16)
+    return pl.pallas_call(
+        partial(operator_kernel, n_line, n_orb, group),
+        out_shape=[jax.ShapeDtypeStruct((2 * n_walk, 1), jnp.float32)] + [piece] * n_line,
+        in_specs=[in_smem(), in_smem()] + [in_vmem()] * 5 + [in_any()],
+        out_specs=[in_vmem()] * (1 + n_line),
+        scratch_shapes=[
+            VMEM(vectors.shape, vectors.dtype),
+            VMEM((2 * n_walk, n_vec), jnp.float32),
+            VMEM((n_line, n_vec), jnp.float32),
+            pltpu.SemaphoreType.DMA((n_rows // group,)),
+        ],
+        name="operators",
+    )(place, source, *biases, aux, vectors)
+
+
+def taylor_kernel(n_z, flags_ref, *refs):
+    same, flip = refs[:n_z], refs[n_z : 2 * n_z]
+    own_ref, orb_ref, walk_ref, far_ref, mine_ref, other_ref, op_ref, term_ref, sum_ref = refs[2 * n_z :]
+    half = LANE
+
+    def total(pieces):
+        result = pieces[0][...].astype(jnp.float32)
+        for piece in pieces[1:]:
+            result = result + piece[...].astype(jnp.float32)
+        return result
+
+    i_at = lax.broadcasted_iota(jnp.int32, (LANE, LANE), 0)
+    j_at = lax.broadcasted_iota(jnp.int32, (LANE, LANE), 1)
+
+    def put(bi, bj, value):
+        op_ref[pl.ds(bi * LANE, LANE), pl.ds(bj * LANE, LANE)] = value.astype(jnp.bfloat16)
+
+    def put_pair(bi, bj, value):
+        put(bi, bj, value)
+        put(bj, bi, value.T)
+
+    extras = []
+    for base, pieces in ((0, same), (2, flip)):
+        sums = total(pieces)
+        merged = sums[:half]
+        turned = merged.T
+        put(base, base, jnp.where(i_at <= j_at, merged, turned))
+        second = jnp.where(i_at > j_at, merged, turned)
+        put(base + 1, base + 1, jnp.where(i_at == j_at, sums[4 * half : 4 * half + 1], second))
+        put_pair(base, base + 1, sums[half : 2 * half])
+        put_pair(base + 1, (base + 2) % 4, sums[2 * half : 3 * half])
+        extras.append(sums[3 * half : 4 * half])
+    lowest = flags_ref[0] == 0
+    across = extras[1].T
+    put_pair(0, 2, jnp.where(lowest, extras[0], across))
+    put_pair(1, 3, jnp.where(lowest, across, extras[0]))
+
+    here = flags_ref[1] == 1
+    rows = own_ref.shape[0]
+    term_ref[pl.ds(0, rows), :] = jnp.where(here, own_ref[...], walk_ref[...])
+    term_ref[pl.ds(rows, rows), :] = jnp.where(here, orb_ref[...], far_ref[...])
+    sum_ref[...] = term_ref[...].astype(jnp.float32)
+    for degree in range(1, ORDER + 1):
+        product = mm(op_ref[...], term_ref[...])
+        term = (product / degree).astype(jnp.bfloat16)
+        sum_ref[...] += term.astype(jnp.float32)
+        if degree < ORDER:
+            term_ref[...] = term
+    mine_ref[...] = sum_ref[pl.ds(0, rows), :].astype(jnp.bfloat16)
+    other_ref[...] = sum_ref[pl.ds(rows, rows), :].astype(jnp.bfloat16)
+
+
+def taylor(flags, same, flip, candidates):
+    rows, width = candidates[0].shape
+    out = jax.ShapeDtypeStruct((rows, width), jnp.bfloat16)
+    return pl.pallas_call(
+        partial(taylor_kernel, len(same)),
+        out_shape=[out, out],
+        in_specs=[in_smem()] + [in_vmem()] * (len(same) + len(flip) + 4),
+        out_specs=[in_vmem()] * 2,
+        scratch_shapes=[
+            VMEM((2 * rows, 2 * rows), jnp.bfloat16),
+            VMEM((2 * rows, width), jnp.bfloat16),
+            VMEM((2 * rows, width), jnp.float32),
+        ],
+        name="taylor",
+    )(flags, *same, *flip, *candidates)
+
+
+def place_kernel(n_line, n_orb, place_ref, *refs):
+    pieces, out_ref, sems = refs[:n_line], refs[n_line], refs[n_line + 1]
+    z, o = place_ref[0], place_ref[1]
+    n_z = n_line // n_orb
+    copies = []
+    for k in range(n_line):
+        from_z = lax.rem(z + n_z - k // n_orb, n_z)
+        from_o = lax.rem(o + n_orb - k % n_orb, n_orb)
+        copies.append(
+            pltpu.make_async_copy(pieces[k], out_ref.at[from_z * n_orb + from_o], sems.at[k])
+        )
+    for copy in copies:
+        copy.start()
+    for copy in copies:
+        copy.wait()
+
+
+def put_in_place(place, pieces, n_orb):
+    n_line = len(pieces)
+    return pl.pallas_call(
+        partial(place_kernel, n_line, n_orb),
+        out_shape=jax.ShapeDtypeStruct((n_line,) + pieces[0].shape, pieces[0].dtype),
+        in_specs=[in_smem()] + [in_any()] * n_line,
+        out_specs=in_any(),
+        scratch_shapes=[pltpu.SemaphoreType.DMA((n_line,))],
+        name="place",
+    )(place, *pieces)
+
+
+def moved(value, axes, sizes, steps):
+    perm = []
+    for a in range(sizes[0]):
+        for b in range(sizes[1]):
+            to = ((a + steps[0]) % sizes[0]) * sizes[1] + (b + steps[1]) % sizes[1]
+            perm.append((a * sizes[1] + b, to))
+    return lax.ppermute(value, axes, perm)
+
+
+def slot_device(n_z, n_x, n_o, walkers, inv_intersection, trial, vectors, aux_field, log_weight, copy_list):
+    n_walk = walkers.shape[0]
+    n_line = n_z * n_o
+    z, x, o = lax.axis_index("vec"), lax.axis_index("walk"), lax.axis_index("orb")
+    line = partial(moved, axes=("vec", "orb"), sizes=(n_z, n_o))
+    near = partial(moved, axes=("walk", "orb"), sizes=(n_x, n_o))
+
+    packed = jnp.concatenate(
+        [aux_field, log_weight[None, :], copy_list.astype(jnp.float32)[None, :]], axis=0
+    )
+    far = near(packed, steps=(1, 0))
+    far_copy = far[n_walk + 1].astype(jnp.int32)
+    aux_both = jnp.concatenate([aux_field, far[:n_walk]], axis=0)
+    log_both = jnp.concatenate([log_weight, far[n_walk]], axis=0)
+    source = copy_list % n_walk + n_walk * (copy_list // n_walk != x).astype(jnp.int32)
+    place = jnp.stack([z, o]).astype(jnp.int32)
+
+    own_bias = partial_bias_of(walkers, inv_intersection, trial, vectors)
+    biases = [own_bias] + [near(own_bias, steps=s) for s in ((0, 1), (1, 0), (1, 1))]
+
+    def walker_at(index):
+        return lax.dynamic_index_in_dim(walkers, index % n_walk, 0, keepdims=False)
+
+    slot = z * n_o + o
+    mate = z * n_o + (n_o - 1 - o)
+    candidates = [
+        walker_at(copy_list[slot]),
+        near(walker_at(copy_list[mate]), steps=(0, 1)),
+        near(walker_at(far_copy[slot]), steps=(1, 0)),
+        near(walker_at(far_copy[mate]), steps=(1, 1)),
+    ]
+
+    factor, *pieces = partial_operators(place, source, biases, aux_both, vectors, n_line, n_o)
+    steps = [(k // n_o, k % n_o) for k in range(n_line)]
+    arrived = [pieces[0]] + [line(pieces[k], steps=steps[k]) for k in range(1, n_line)]
+    same = [arrived[k] for k in range(n_line) if steps[k][1] == 0]
+    flip = [arrived[k] for k in range(n_line) if steps[k][1] == 1]
+    factors = [factor] + [line(factor, steps=(d, 0)) for d in range(1, n_z)]
+    new_log = log_both + ((factors[0] + factors[2]) + (factors[1] + factors[3]))[:, 0]
+    weights_out = new_log[source]
+
+    flags = jnp.stack([o, (copy_list[slot] // n_walk == x).astype(jnp.int32)]).astype(jnp.int32)
+    mine, other = taylor(flags, same, flip, candidates)
+    landed = []
+    for k in range(n_line):
+        half = mine if steps[k][1] == 0 else other
+        landed.append(half if k == 0 else line(half, steps=steps[k]))
+    return put_in_place(place, landed, n_o), weights_out
+
+
+def suits(mesh, walkers, trial, vectors):
+    n_z, n_x, n_o = mesh.shape["vec"], mesh.shape["walk"], mesh.shape["orb"]
+    per_device = walkers.shape[0] // (mesh.shape["grp"] * n_x)
+    local_vectors = vectors.shape[0] // n_z
+    return (
+        n_o == 2
+        and n_x == 2
+        and n_z == 4
+        and per_device == n_z * n_o
+        and local_vectors == per_device
+        and vectors.shape[1] == 4 * LANE
+        and trial.shape[1] == LANE
+    )
+
+
 def solution(mesh):
-    return jax.shard_map(
-        per_device,
-        mesh=mesh,
-        in_specs=(
-            P(("grp", "walk"), "orb", None),
-            P(("grp", "walk"), None, None),
-            P(),
-            P("vec", "orb", None),
-            P(("grp", "walk"), "vec"),
-            P(("grp", "walk")),
-            P(("grp", "walk")),
-        ),
-        out_specs=(P(("grp", "walk"), "orb", None), P(("grp", "walk"))),
-        check_vma=False,
-    )
+    def step(walkers, inv_intersection, trial, vectors, aux_field, log_weight, copy_list):
+        if suits(mesh, walkers, trial, vectors):
+            body = partial(slot_device, mesh.shape["vec"], mesh.shape["walk"], mesh.shape["orb"])
+        else:
+            body = general_device
+        return jax.shard_map(
+            body,
+            mesh=mesh,
+            in_specs=(
+                P(("grp", "walk"), "orb", None),
+                P(("grp", "walk"), None, None),
+                P(),
+                P("vec", "orb", None),
+                P(("grp", "walk"), "vec"),
+                P(("grp", "walk")),
+                P(("grp", "walk")),
+            ),
+            out_specs=(P(("grp", "walk"), "orb", None), P(("grp", "walk"))),
+            check_vma=False,
+        )(walkers, inv_intersection, trial, vectors, aux_field, log_weight, copy_list)
+
+    return step

time: 277 us -> 91.6 us (0.33)
  blocking collectives: 158 us -> 0 us
  waiting for transfers between devices: 65.4 us -> 10.2 us
  starting transfers between devices: 0.29 us -> 32.7 us
  matrix products: 31.5 us -> 0 us
  Pallas kernels: 0 us -> 31.1 us
  between operations: 14.9 us -> 9.08 us
  other arithmetic: 0.23 us -> 3.23 us
    psum x2 -> x0, blocking collectives: 153 us -> none  [the longest x1 151 us: per_device(): operator = lax.psum(local_operator, 'vec').astype(jnp.bfloat16)]
    all_gather x7 -> x0, waiting for transfers between devices: 64.6 us -> none  [the longest x6 49.4 us: per_device(): lax.all_gather(operand, 'orb', axis=1, tiled=True)]
    ppermute x0 -> x24, starting transfers between devices: none -> 32.7 us  [moved(): return lax.ppermute(value, axes, perm)]
    dot_general x10 -> x0, matrix products: 31.5 us -> none  [the longest x6 24.9 us: fold_rows(): jnp.einsum('wnm,wme->wne', operator, piece, preferred_element_type=jnp.fl...]
    pallas_call x0 -> x4, Pallas kernels: none -> 31.1 us  [the longest x1 17.7 us: put_in_place(): pl.pallas_call(partial(place_kernel, n_line, n_orb), out_shape=jax.ShapeD...]
    ppermute x0 -> x24, waiting for transfers between devices: none -> 10.2 us  [moved(): return lax.ppermute(value, axes, perm)]
    unnamed x1 -> x0, blocking collectives: 4.91 us -> none
  transfers between devices with their start and end apart: 7 -> 24, of which waited for: 6 -> 8; matrix products, arithmetic and copies ran while one was open for 4% -> 7% of each run, Pallas kernels for 0% -> 5%
where the time goes in v1:
time: 91.6 us; the launch traced here: 91.3 us
  starting transfers between devices  32.7 us (36%)
  Pallas kernels  31.1 us (34%)
  waiting for transfers between devices  10.2 us (11%)
  between operations  9.08 us (10%)
  local copies, waits for them, and re-layouts  4.94 us (5%)
  other arithmetic  3.23 us (4%)
    ppermute x24, starting transfers between devices, moved(): return lax.ppermute(value, axes, perm)  32.7 us
    pallas_call x1, Pallas kernels, put_in_place(): pl.pallas_call(partial(place_kernel, n_line, n_orb), out_shape=jax.ShapeD...  17.7 us
    ppermute x24, waiting for transfers between devices, moved(): return lax.ppermute(value, axes, perm)  10.2 us
    pallas_call x1, Pallas kernels, partial_bias_of(): pl.pallas_call(bias_kernel, out_shape=jax.ShapeDtypeStruct((n_walk, n_vec...  4.85 us
    pallas_call x1, Pallas kernels, taylor(): pl.pallas_call(partial(taylor_kernel, len(same)), out_shape=[out, out], i...  4.35 us
    pallas_call x1, Pallas kernels, partial_operators(): pl.pallas_call(partial(operator_kernel, n_line, n_orb, group), out_shape=...  4.16 us
    unnamed x48, local copies, waits for them, and re-layouts  1.9 us
  transfers between devices with their start and end apart: 24, of which 8 were waited for; matrix products, arithmetic and copies ran while one was open for 7% of the time, Pallas kernels for 5%

profile of v1, /device:TPU:0, one launch (start us, length us, event | category | flops | bytes accessed | tf_op | source)
XLA Modules:
  0.0 91.3 jit_solution(12856515834071299466)
XLA Ops:
  0.7 4.8 %bias.1.bias0 = f32[8,8]{1,0:T(8,128)} custom-call(bf16[8,256,128]{2,1,0:T(8,128)(2,1)} %walkers_hbm.1, bf16[8,128,128]{2,1,0:T(8,128)(2,1)} %inv_hbm.1, bf16[512,128]{1,0:T(8,128)(2,1)} %trial_hbm.1, bf16[8,256,512]{2,1,0:T(8,128)(2,1)} %vec_hbm.3), custom_call_target="tpu_custom_call" | custom-call | tf_op jit(solution)/shard_map/bias/pallas_call | solution.py:107
  5.5 0.6 collective-permute-start
  6.1 2.5 %collective-permute-start.1 = (f32[8,8]{1,0:T(8,128)}, f32[8,8]{1,0:T(8,128)S(1)}, u32[]{:S(2)}, u32[]{:S(2)}) collective-permute-start(f32[8,8]{1,0:T(8,128)} %bias.1.bias0), channel_id=1, source_target_pairs={{0,2},{1,3},{2,0},{3,1},{4,6},{5,7},{6,4},{7,5},{8,10},{9,11},{10,... | collective-permute-start | bytes 776 | tf_op jit(solution)/shard_map/ppermute | solution.py:323
  8.6 0.0 collective-permute-start.2
  8.7 0.6 compare_select_fusion
  9.2 1.8 %collective-permute-start.3 = (f32[10,8]{1,0:T(8,128)S(1)}, f32[10,8]{1,0:T(8,128)S(1)}, u32[]{:S(2)}, u32[]{:S(2)}) collective-permute-start(f32[10,8]{1,0:T(8,128)S(1)} %pad_maximum_fusion), channel_id=1, source_target_pairs={{0,2},{1,3},{2,0},{3,1},{4,6},{5,7},{6,4},{7,5},{8,10},{9,11},{10,... | collective-permute-start | bytes 968 | tf_op jit(solution)/shard_map/ppermute | solution.py:323
  11.1 0.7 fusion.2
  15.4 0.6 pad_add_fusion.place_ref
  16.0 0.6 constant_dynamic-slice_fusion
  20.4 0.6 pad_maximum_fusion.1.aux_ref
  21.1 0.5 copy-done.20
  21.6 4.2 %operators.1 = (f32[16,1]{1,0:T(8,128)}, bf16[528,128]{1,0:T(8,128)(2,1)}, bf16[528,128]{1,0:T(8,128)(2,1)}, bf16[528,128]{1,0:T(8,128)(2,1)}, bf16[528,128]{1,0...) custom-call(s32[2]{0:T(128)} %pad_add_fusion.place_ref, ...), custom_call_target="tpu_custom_call" | custom-call | tf_op jit(solution)/shard_map/operators/pallas_call | solution.py:204
  25.8 1.6 %collective-permute-start.4 = (bf16[528,128]{1,0:T(8,128)(2,1)}, bf16[528,128]{1,0:T(8,128)(2,1)S(1)}, u32[]{:S(2)}, u32[]{:S(2)}) collective-permute-start(bf16[528,128]{1,0:T(8,128)(2,1)} %get-tuple-element.14), channel_id=1, source_target_pairs={{0,4},{1,5},{4,8},{5,9},{8,12},{9,13},{12,0},{13,1},{2,6},{3,7},{6... | collective-permute-start | bytes 405512 | tf_op jit(solution)/shard_map/ppermute | solution.py:323
  27.4 2.6 %collective-permute-start.5 = (bf16[528,128]{1,0:T(8,128)(2,1)}, bf16[528,128]{1,0:T(8,128)(2,1)S(1)}, u32[]{:S(2)}, u32[]{:S(2)}) collective-permute-start(bf16[528,128]{1,0:T(8,128)(2,1)} %get-tuple-element.15), channel_id=1, source_target_pairs={{0,8},{1,9},{4,12},{5,13},{8,0},{9,1},{12,4},{13,5},{2,10},{3,11},... | collective-permute-start | bytes 405512 | tf_op jit(solution)/shard_map/ppermute | solution.py:323
  30.0 0.6 dynamic-slice_bitcast_fusion
  30.7 0.5 collective-permute-start.12
  31.2 1.3 %collective-permute-start.13 = (bf16[256,128]{1,0:T(8,128)(2,1)S(1)}, bf16[256,128]{1,0:T(8,128)(2,1)S(1)}, u32[]{:S(2)}, u32[]{:S(2)}) collective-permute-start(bf16[256,128]{1,0:T(8,128)(2,1)S(1)} %get-tuple-element.26), channel_id=1, source_target_pairs={{0,3},{1,2},{2,1},{3,0},{4,7},{5,6},{6,5},{7,4},{8,11},{9,10},{10,... | collective-permute-start | bytes 196616 | tf_op jit(solution)/shard_map/ppermute | solution.py:323
  33.2 1.4 %collective-permute-start.6 = (bf16[528,128]{1,0:T(8,128)(2,1)}, bf16[528,128]{1,0:T(8,128)(2,1)S(1)}, u32[]{:S(2)}, u32[]{:S(2)}) collective-permute-start(bf16[528,128]{1,0:T(8,128)(2,1)} %get-tuple-element.16), channel_id=1, source_target_pairs={{0,12},{1,13},{4,0},{5,1},{8,4},{9,5},{12,8},{13,9},{2,14},{3,15},... | collective-permute-start | bytes 405512 | tf_op jit(solution)/shard_map/ppermute | solution.py:323
  34.6 1.0 %collective-permute-done.12.refs_10_ = bf16[256,128]{1,0:T(8,128)(2,1)S(1)} collective-permute-done((bf16[256,128]{1,0:T(8,128)(2,1)S(1)}, bf16[256,128]{1,0:T(8,128)(2,1)S(1)}, u32[]{:S(2)}, u32[]{:S(2)}) %collective-permute-start.12) | collective-permute-done | bytes 65568 | tf_op jit(solution)/shard_map/ppermute | solution.py:323
  35.6 0.5 collective-permute-done.13.refs_11_
  36.1 0.4 collective-permute-start.8
  36.5 1.2 %collective-permute-start.9 = (bf16[528,128]{1,0:T(8,128)(2,1)}, bf16[528,128]{1,0:T(8,128)(2,1)S(1)}, u32[]{:S(2)}, u32[]{:S(2)}) collective-permute-start(bf16[528,128]{1,0:T(8,128)(2,1)} %get-tuple-element.19), channel_id=1, source_target_pairs={{0,9},{1,8},{4,13},{5,12},{8,1},{9,0},{12,5},{13,4},{2,11},{3,10},... | collective-permute-start | bytes 405512 | tf_op jit(solution)/shard_map/ppermute | solution.py:323
  37.8 1.7 %collective-permute-done.5.refs_2_ = bf16[528,128]{1,0:T(8,128)(2,1)S(1)} collective-permute-done((bf16[528,128]{1,0:T(8,128)(2,1)}, bf16[528,128]{1,0:T(8,128)(2,1)S(1)}, u32[]{:S(2)}, u32[]{:S(2)}) %collective-permute-start.5) | collective-permute-done | bytes 135200 | tf_op jit(solution)/shard_map/ppermute | solution.py:323
  39.4 3.1 %collective-permute-start.10 = (bf16[528,128]{1,0:T(8,128)(2,1)}, bf16[528,128]{1,0:T(8,128)(2,1)S(1)}, u32[]{:S(2)}, u32[]{:S(2)}) collective-permute-start(bf16[528,128]{1,0:T(8,128)(2,1)} %get-tuple-element.20), channel_id=1, source_target_pairs={{0,13},{1,12},{4,1},{5,0},{8,5},{9,4},{12,9},{13,8},{2,15},{3,14},... | collective-permute-start | bytes 405512 | tf_op jit(solution)/shard_map/ppermute | solution.py:323
  42.6 0.6 pad_add_fusion.1.flags_ref
  43.2 2.0 %collective-permute-done.6.refs_3_ = bf16[528,128]{1,0:T(8,128)(2,1)S(1)} collective-permute-done((bf16[528,128]{1,0:T(8,128)(2,1)}, bf16[528,128]{1,0:T(8,128)(2,1)S(1)}, u32[]{:S(2)}, u32[]{:S(2)}) %collective-permute-start.6) | collective-permute-done | bytes 135200 | tf_op jit(solution)/shard_map/ppermute | solution.py:323
  45.2 3.5 %collective-permute-start.22 = (f32[16,1]{1,0:T(8,128)}, f32[16,1]{1,0:T(8,128)S(1)}, u32[]{:S(2)}, u32[]{:S(2)}) collective-permute-start(f32[16,1]{1,0:T(8,128)} %get-tuple-element.23), channel_id=1, source_target_pairs={{0,4},{1,5},{4,8},{5,9},{8,12},{9,13},{12,0},{13,1},{2,6},{3,7},{6... | collective-permute-start | bytes 200 | tf_op jit(solution)/shard_map/ppermute | solution.py:323
  48.7 0.3 collective-permute-start.23
  49.0 1.8 %collective-permute-start.21 = (f32[16,1]{1,0:T(8,128)}, f32[16,1]{1,0:T(8,128)S(1)}, u32[]{:S(2)}, u32[]{:S(2)}) collective-permute-start(f32[16,1]{1,0:T(8,128)} %get-tuple-element.23), channel_id=1, source_target_pairs={{0,8},{1,9},{4,12},{5,13},{8,0},{9,1},{12,4},{13,5},{2,10},{3,11},... | collective-permute-start | bytes 200 | tf_op jit(solution)/shard_map/ppermute | solution.py:323
  50.8 0.2 collective-permute-done.9.refs_6_
  51.1 0.6 copy-done.6
  51.7 0.0 copy-done.7
  51.7 4.3 %taylor.1 = (bf16[256,128]{1,0:T(8,128)(2,1)}, bf16[256,128]{1,0:T(8,128)(2,1)}) custom-call(s32[2]{0:T(128)} %pad_add_fusion.1.flags_ref, bf16[528,128]{1,0:T(8,128)(2,1)} %get-tuple-element.13.refs_0_, bf16[528,128]{1,0:T(8,128)(2,1)} %copy-done.1, bf16[528,128]{1,0:T(8,128)(2,1)} %copy-done.2, bf16[528,128]{1,0:T(8,128)(2,1)} %copy-done.3, ...), custom_call_target="tpu_custom_call" | custom-call | tf_op jit(solution)/shard_map/taylor/pallas_call | solution.py:274
  56.1 1.1 %collective-permute-start.14 = (bf16[256,128]{1,0:T(8,128)(2,1)}, bf16[256,128]{1,0:T(8,128)(2,1)S(1)}, u32[]{:S(2)}, u32[]{:S(2)}) collective-permute-start(bf16[256,128]{1,0:T(8,128)(2,1)} %get-tuple-element.22), channel_id=1, source_target_pairs={{0,1},{1,0},{4,5},{5,4},{8,9},{9,8},{12,13},{13,12},{2,3},{3,2},{6... | collective-permute-start | bytes 196616 | tf_op jit(solution)/shard_map/ppermute | solution.py:323
  57.1 2.5 %collective-permute-start.15 = (bf16[256,128]{1,0:T(8,128)(2,1)}, bf16[256,128]{1,0:T(8,128)(2,1)S(1)}, u32[]{:S(2)}, u32[]{:S(2)}) collective-permute-start(bf16[256,128]{1,0:T(8,128)(2,1)} %get-tuple-element.21.refs_0_), channel_id=1, source_target_pairs={{0,4},{1,5},{4,8},{5,9},{8,12},{9,13},{12,0},{13,1},{2,6},{3,7},{6... | collective-permute-start | bytes 196616 | tf_op jit(solution)/shard_map/ppermute | solution.py:323
  59.7 0.8 add_reduce_fusion
  60.5 0.1 collective-permute-start.16
  60.6 1.6 %collective-permute-start.17 = (bf16[256,128]{1,0:T(8,128)(2,1)}, bf16[256,128]{1,0:T(8,128)(2,1)S(1)}, u32[]{:S(2)}, u32[]{:S(2)}) collective-permute-start(bf16[256,128]{1,0:T(8,128)(2,1)} %get-tuple-element.21.refs_0_), channel_id=1, source_target_pairs={{0,8},{1,9},{4,12},{5,13},{8,0},{9,1},{12,4},{13,5},{2,10},{3,11},... | collective-permute-start | bytes 196616 | tf_op jit(solution)/shard_map/ppermute | solution.py:323
  62.2 0.8 collective-permute-start.18
  63.0 3.7 %collective-permute-start.19 = (bf16[256,128]{1,0:T(8,128)(2,1)}, bf16[256,128]{1,0:T(8,128)(2,1)S(1)}, u32[]{:S(2)}, u32[]{:S(2)}) collective-permute-start(bf16[256,128]{1,0:T(8,128)(2,1)} %get-tuple-element.21.refs_0_), channel_id=1, source_target_pairs={{0,12},{1,13},{4,0},{5,1},{8,4},{9,5},{12,8},{13,9},{2,14},{3,15},... | collective-permute-start | bytes 196616 | tf_op jit(solution)/shard_map/ppermute | solution.py:323
  66.7 0.1 collective-permute-start.20
  66.8 0.1 maximum_add_fusion
  66.9 1.2 %gather_fusion = f32[8]{0:T(128)} fusion(f32[16]{0:T(128)S(1)} %maximum_add_fusion, s32[1024]{0:T(1024)S(1)} %pad_clamp_fusion), kind=kCustom, calls=%fused_computation | custom fusion | bytes 96 | tf_op jit(solution)/shard_map/gather | solution.py:365
  68.0 2.6 %collective-permute-done.17.refs_4_ = bf16[256,128]{1,0:T(8,128)(2,1)S(1)} collective-permute-done((bf16[256,128]{1,0:T(8,128)(2,1)}, bf16[256,128]{1,0:T(8,128)(2,1)S(1)}, u32[]{:S(2)}, u32[]{:S(2)}) %collective-permute-start.17) | collective-permute-done | bytes 65568 | tf_op jit(solution)/shard_map/ppermute | solution.py:323
  70.7 0.7 collective-permute-done.18.refs_5_
  71.4 1.5 %collective-permute-done.20.refs_7_ = bf16[256,128]{1,0:T(8,128)(2,1)S(1)} collective-permute-done((bf16[256,128]{1,0:T(8,128)(2,1)}, bf16[256,128]{1,0:T(8,128)(2,1)S(1)}, u32[]{:S(2)}, u32[]{:S(2)}) %collective-permute-start.20) | collective-permute-done | bytes 65568 | tf_op jit(solution)/shard_map/ppermute | solution.py:323
  72.9 0.6 copy-done.17
  73.5 17.7 %place.1 = bf16[8,256,128]{2,1,0:T(8,128)(2,1)} custom-call(s32[2]{0:T(128)} %pad_add_fusion.place_ref, bf16[256,128]{1,0:T(8,128)(2,1)} %get-tuple-element.21.refs_0_, bf16[256,128]{1,0:T(8,128)(2,1)} %copy-done.11, bf16[256,128]{1,0:T(8,128)(2,1)} %copy-done.12, bf16[256,128]{1,0:T(8,128)(2,1)} %copy-done.13, bf16[256,128]{1,0:T(8,128)(2,1)} %copy-done.14, ...), custom_call_target="tpu_custom_call" | custom-call | tf_op jit(solution)/shard_map/place/pallas_call | solution.py:307
  (66 shorter events, 0.2 us)
Async XLA Ops:
  0.6 29.4 %copy-start = (bf16[8,256,128]{2,1,0:T(8,128)(2,1)S(1)}, bf16[8,256,128]{2,1,0:T(8,128)(2,1)}, u32[]{:S(2)}) copy-start(bf16[8,256,128]{2,1,0:T(8,128)(2,1)} %walkers_hbm.1) | copy-start | bytes 1572868
  0.6 8.0 %copy-start.19 = (s32[8]{0:T(128)S(1)}, s32[8]{0:T(128)}, u32[]{:S(2)}) copy-start(s32[8]{0:T(128)} %param.13) | copy-start | bytes 100
  0.7 8.6 %copy-start.23 = (f32[8]{0:T(128)S(1)}, f32[8]{0:T(128)}, u32[]{:S(2)}) copy-start(f32[8]{0:T(128)} %param.12) | copy-start | bytes 100
  0.7 8.6 %copy-start.18 = (f32[8,8]{1,0:T(8,128)S(1)}, f32[8,8]{1,0:T(8,128)}, u32[]{:S(2)}) copy-start(f32[8,8]{1,0:T(8,128)} %param.11) | copy-start | bytes 772
  5.5 15.5 %collective-permute-start = (f32[8,8]{1,0:T(8,128)}, f32[8,8]{1,0:T(8,128)S(1)}, u32[]{:S(2)}, u32[]{:S(2)}) collective-permute-start(f32[8,8]{1,0:T(8,128)} %bias.1.bias0), channel_id=1, source_target_pairs={{0,1},{1,0},{2,3},{3,2},{4,5},{5,4},{6,7},{7,6},{8,9},{9,8},{10,11... | collective-permute-start | bytes 776 | tf_op jit(solution)/shard_map/ppermute | solution.py:323
  6.1 14.9 %collective-permute-start.1 = (f32[8,8]{1,0:T(8,128)}, f32[8,8]{1,0:T(8,128)S(1)}, u32[]{:S(2)}, u32[]{:S(2)}) collective-permute-start(f32[8,8]{1,0:T(8,128)} %bias.1.bias0), channel_id=1, source_target_pairs={{0,2},{1,3},{2,0},{3,1},{4,6},{5,7},{6,4},{7,5},{8,10},{9,11},{10,... | collective-permute-start | bytes 776 | tf_op jit(solution)/shard_map/ppermute | solution.py:323
  8.6 12.4 %collective-permute-start.2 = (f32[8,8]{1,0:T(8,128)}, f32[8,8]{1,0:T(8,128)S(1)}, u32[]{:S(2)}, u32[]{:S(2)}) collective-permute-start(f32[8,8]{1,0:T(8,128)} %bias.1.bias0), channel_id=1, source_target_pairs={{0,3},{1,2},{2,1},{3,0},{4,7},{5,6},{6,5},{7,4},{8,11},{9,10},{10,... | collective-permute-start | bytes 776 | tf_op jit(solution)/shard_map/ppermute | solution.py:323
  9.2 6.8 %collective-permute-start.3 = (f32[10,8]{1,0:T(8,128)S(1)}, f32[10,8]{1,0:T(8,128)S(1)}, u32[]{:S(2)}, u32[]{:S(2)}) collective-permute-start(f32[10,8]{1,0:T(8,128)S(1)} %pad_maximum_fusion), channel_id=1, source_target_pairs={{0,2},{1,3},{2,0},{3,1},{4,6},{5,7},{6,4},{7,5},{8,10},{9,11},{10,... | collective-permute-start | bytes 968 | tf_op jit(solution)/shard_map/ppermute | solution.py:323
  21.0 0.6 copy-start.20
  21.0 0.6 copy-start.21
  21.1 0.6 copy-start.22
  25.8 10.7 %collective-permute-start.4 = (bf16[528,128]{1,0:T(8,128)(2,1)}, bf16[528,128]{1,0:T(8,128)(2,1)S(1)}, u32[]{:S(2)}, u32[]{:S(2)}) collective-permute-start(bf16[528,128]{1,0:T(8,128)(2,1)} %get-tuple-element.14), channel_id=1, source_target_pairs={{0,4},{1,5},{4,8},{5,9},{8,12},{9,13},{12,0},{13,1},{2,6},{3,7},{6... | collective-permute-start | bytes 405512 | tf_op jit(solution)/shard_map/ppermute | solution.py:323
  27.4 12.0 %collective-permute-start.5 = (bf16[528,128]{1,0:T(8,128)(2,1)}, bf16[528,128]{1,0:T(8,128)(2,1)S(1)}, u32[]{:S(2)}, u32[]{:S(2)}) collective-permute-start(bf16[528,128]{1,0:T(8,128)(2,1)} %get-tuple-element.15), channel_id=1, source_target_pairs={{0,8},{1,9},{4,12},{5,13},{8,0},{9,1},{12,4},{13,5},{2,10},{3,11},... | collective-permute-start | bytes 405512 | tf_op jit(solution)/shard_map/ppermute | solution.py:323
  30.7 2.5 %collective-permute-start.11 = (bf16[256,128]{1,0:T(8,128)(2,1)S(1)}, bf16[256,128]{1,0:T(8,128)(2,1)S(1)}, u32[]{:S(2)}, u32[]{:S(2)}) collective-permute-start(bf16[256,128]{1,0:T(8,128)(2,1)S(1)} %get-tuple-element.27), channel_id=1, source_target_pairs={{0,1},{1,0},{2,3},{3,2},{4,5},{5,4},{6,7},{7,6},{8,9},{9,8},{10,11... | collective-permute-start | bytes 196616 | tf_op jit(solution)/shard_map/ppermute | solution.py:323
  30.7 5.0 %collective-permute-start.12 = (bf16[256,128]{1,0:T(8,128)(2,1)S(1)}, bf16[256,128]{1,0:T(8,128)(2,1)S(1)}, u32[]{:S(2)}, u32[]{:S(2)}) collective-permute-start(bf16[256,128]{1,0:T(8,128)(2,1)S(1)} %get-tuple-element.29), channel_id=1, source_target_pairs={{0,2},{1,3},{2,0},{3,1},{4,6},{5,7},{6,4},{7,5},{8,10},{9,11},{10,... | collective-permute-start | bytes 196616 | tf_op jit(solution)/shard_map/ppermute | solution.py:323
  31.2 4.9 %collective-permute-start.13 = (bf16[256,128]{1,0:T(8,128)(2,1)S(1)}, bf16[256,128]{1,0:T(8,128)(2,1)S(1)}, u32[]{:S(2)}, u32[]{:S(2)}) collective-permute-start(bf16[256,128]{1,0:T(8,128)(2,1)S(1)} %get-tuple-element.26), channel_id=1, source_target_pairs={{0,3},{1,2},{2,1},{3,0},{4,7},{5,6},{6,5},{7,4},{8,11},{9,10},{10,... | collective-permute-start | bytes 196616 | tf_op jit(solution)/shard_map/ppermute | solution.py:323
  33.2 17.8 %copy-start.8 = (bf16[256,128]{1,0:T(8,128)(2,1)}, bf16[256,128]{1,0:T(8,128)(2,1)S(1)}, u32[]{:S(2)}) copy-start(bf16[256,128]{1,0:T(8,128)(2,1)S(1)} %collective-permute-done.11.refs_9_) | copy-start | bytes 196612
  33.2 12.0 %collective-permute-start.6 = (bf16[528,128]{1,0:T(8,128)(2,1)}, bf16[528,128]{1,0:T(8,128)(2,1)S(1)}, u32[]{:S(2)}, u32[]{:S(2)}) collective-permute-start(bf16[528,128]{1,0:T(8,128)(2,1)} %get-tuple-element.16), channel_id=1, source_target_pairs={{0,12},{1,13},{4,0},{5,1},{8,4},{9,5},{12,8},{13,9},{2,14},{3,15},... | collective-permute-start | bytes 405512 | tf_op jit(solution)/shard_map/ppermute | solution.py:323
  35.6 15.4 %copy-start.9 = (bf16[256,128]{1,0:T(8,128)(2,1)}, bf16[256,128]{1,0:T(8,128)(2,1)S(1)}, u32[]{:S(2)}) copy-start(bf16[256,128]{1,0:T(8,128)(2,1)S(1)} %collective-permute-done.12.refs_10_) | copy-start | bytes 196612
  35.6 13.1 %collective-permute-start.7 = (bf16[528,128]{1,0:T(8,128)(2,1)}, bf16[528,128]{1,0:T(8,128)(2,1)S(1)}, u32[]{:S(2)}, u32[]{:S(2)}) collective-permute-start(bf16[528,128]{1,0:T(8,128)(2,1)} %get-tuple-element.17), channel_id=1, source_target_pairs={{0,1},{1,0},{4,5},{5,4},{8,9},{9,8},{12,13},{13,12},{2,3},{3,2},{6... | collective-permute-start | bytes 405512 | tf_op jit(solution)/shard_map/ppermute | solution.py:323
  36.1 14.9 %copy-start.10 = (bf16[256,128]{1,0:T(8,128)(2,1)}, bf16[256,128]{1,0:T(8,128)(2,1)S(1)}, u32[]{:S(2)}) copy-start(bf16[256,128]{1,0:T(8,128)(2,1)S(1)} %collective-permute-done.13.refs_11_) | copy-start | bytes 196612
  36.1 12.9 %collective-permute-start.8 = (bf16[528,128]{1,0:T(8,128)(2,1)}, bf16[528,128]{1,0:T(8,128)(2,1)S(1)}, u32[]{:S(2)}, u32[]{:S(2)}) collective-permute-start(bf16[528,128]{1,0:T(8,128)(2,1)} %get-tuple-element.18), channel_id=1, source_target_pairs={{0,5},{1,4},{4,9},{5,8},{8,13},{9,12},{12,1},{13,0},{2,7},{3,6},{6... | collective-permute-start | bytes 405512 | tf_op jit(solution)/shard_map/ppermute | solution.py:323
  36.5 14.5 %copy-start.1 = (bf16[528,128]{1,0:T(8,128)(2,1)}, bf16[528,128]{1,0:T(8,128)(2,1)S(1)}, u32[]{:S(2)}) copy-start(bf16[528,128]{1,0:T(8,128)(2,1)S(1)} %collective-permute-done.4.refs_1_) | copy-start | bytes 405508
  36.5 14.5 %collective-permute-start.9 = (bf16[528,128]{1,0:T(8,128)(2,1)}, bf16[528,128]{1,0:T(8,128)(2,1)S(1)}, u32[]{:S(2)}, u32[]{:S(2)}) collective-permute-start(bf16[528,128]{1,0:T(8,128)(2,1)} %get-tuple-element.19), channel_id=1, source_target_pairs={{0,9},{1,8},{4,13},{5,12},{8,1},{9,0},{12,5},{13,4},{2,11},{3,10},... | collective-permute-start | bytes 405512 | tf_op jit(solution)/shard_map/ppermute | solution.py:323
  39.4 11.6 %copy-start.2 = (bf16[528,128]{1,0:T(8,128)(2,1)}, bf16[528,128]{1,0:T(8,128)(2,1)S(1)}, u32[]{:S(2)}) copy-start(bf16[528,128]{1,0:T(8,128)(2,1)S(1)} %collective-permute-done.5.refs_2_) | copy-start | bytes 405508
  39.4 11.6 %collective-permute-start.10 = (bf16[528,128]{1,0:T(8,128)(2,1)}, bf16[528,128]{1,0:T(8,128)(2,1)S(1)}, u32[]{:S(2)}, u32[]{:S(2)}) collective-permute-start(bf16[528,128]{1,0:T(8,128)(2,1)} %get-tuple-element.20), channel_id=1, source_target_pairs={{0,13},{1,12},{4,1},{5,0},{8,5},{9,4},{12,9},{13,8},{2,15},{3,14},... | collective-permute-start | bytes 405512 | tf_op jit(solution)/shard_map/ppermute | solution.py:323
  45.2 5.9 %copy-start.3 = (bf16[528,128]{1,0:T(8,128)(2,1)}, bf16[528,128]{1,0:T(8,128)(2,1)S(1)}, u32[]{:S(2)}) copy-start(bf16[528,128]{1,0:T(8,128)(2,1)S(1)} %collective-permute-done.6.refs_3_) | copy-start | bytes 405508
  45.2 14.5 %collective-permute-start.22 = (f32[16,1]{1,0:T(8,128)}, f32[16,1]{1,0:T(8,128)S(1)}, u32[]{:S(2)}, u32[]{:S(2)}) collective-permute-start(f32[16,1]{1,0:T(8,128)} %get-tuple-element.23), channel_id=1, source_target_pairs={{0,4},{1,5},{4,8},{5,9},{8,12},{9,13},{12,0},{13,1},{2,6},{3,7},{6... | collective-permute-start | bytes 200 | tf_op jit(solution)/shard_map/ppermute | solution.py:323
  48.7 2.4 %copy-start.4 = (bf16[528,128]{1,0:T(8,128)(2,1)}, bf16[528,128]{1,0:T(8,128)(2,1)S(1)}, u32[]{:S(2)}) copy-start(bf16[528,128]{1,0:T(8,128)(2,1)S(1)} %collective-permute-done.7.refs_4_) | copy-start | bytes 405508
  48.7 11.0 %collective-permute-start.23 = (f32[16,1]{1,0:T(8,128)}, f32[16,1]{1,0:T(8,128)S(1)}, u32[]{:S(2)}, u32[]{:S(2)}) collective-permute-start(f32[16,1]{1,0:T(8,128)} %get-tuple-element.23), channel_id=1, source_target_pairs={{0,12},{1,13},{4,0},{5,1},{8,4},{9,5},{12,8},{13,9},{2,14},{3,15},... | collective-permute-start | bytes 200 | tf_op jit(solution)/shard_map/ppermute | solution.py:323
  49.0 2.1 %copy-start.5 = (bf16[528,128]{1,0:T(8,128)(2,1)}, bf16[528,128]{1,0:T(8,128)(2,1)S(1)}, u32[]{:S(2)}) copy-start(bf16[528,128]{1,0:T(8,128)(2,1)S(1)} %collective-permute-done.8.refs_5_) | copy-start | bytes 405508
  49.0 10.7 %collective-permute-start.21 = (f32[16,1]{1,0:T(8,128)}, f32[16,1]{1,0:T(8,128)S(1)}, u32[]{:S(2)}, u32[]{:S(2)}) collective-permute-start(f32[16,1]{1,0:T(8,128)} %get-tuple-element.23), channel_id=1, source_target_pairs={{0,8},{1,9},{4,12},{5,13},{8,0},{9,1},{12,4},{13,5},{2,10},{3,11},... | collective-permute-start | bytes 200 | tf_op jit(solution)/shard_map/ppermute | solution.py:323
  51.0 0.7 copy-start.6
  51.0 0.7 copy-start.7
  56.1 6.9 %collective-permute-start.14 = (bf16[256,128]{1,0:T(8,128)(2,1)}, bf16[256,128]{1,0:T(8,128)(2,1)S(1)}, u32[]{:S(2)}, u32[]{:S(2)}) collective-permute-start(bf16[256,128]{1,0:T(8,128)(2,1)} %get-tuple-element.22), channel_id=1, source_target_pairs={{0,1},{1,0},{4,5},{5,4},{8,9},{9,8},{12,13},{13,12},{2,3},{3,2},{6... | collective-permute-start | bytes 196616 | tf_op jit(solution)/shard_map/ppermute | solution.py:323
  57.1 9.6 %collective-permute-start.15 = (bf16[256,128]{1,0:T(8,128)(2,1)}, bf16[256,128]{1,0:T(8,128)(2,1)S(1)}, u32[]{:S(2)}, u32[]{:S(2)}) collective-permute-start(bf16[256,128]{1,0:T(8,128)(2,1)} %get-tuple-element.21.refs_0_), channel_id=1, source_target_pairs={{0,4},{1,5},{4,8},{5,9},{8,12},{9,13},{12,0},{13,1},{2,6},{3,7},{6... | collective-permute-start | bytes 196616 | tf_op jit(solution)/shard_map/ppermute | solution.py:323
  60.5 7.6 %collective-permute-start.16 = (bf16[256,128]{1,0:T(8,128)(2,1)}, bf16[256,128]{1,0:T(8,128)(2,1)S(1)}, u32[]{:S(2)}, u32[]{:S(2)}) collective-permute-start(bf16[256,128]{1,0:T(8,128)(2,1)} %get-tuple-element.22), channel_id=1, source_target_pairs={{0,5},{1,4},{4,9},{5,8},{8,13},{9,12},{12,1},{13,0},{2,7},{3,6},{6... | collective-permute-start | bytes 196616 | tf_op jit(solution)/shard_map/ppermute | solution.py:323
  60.6 10.1 %collective-permute-start.17 = (bf16[256,128]{1,0:T(8,128)(2,1)}, bf16[256,128]{1,0:T(8,128)(2,1)S(1)}, u32[]{:S(2)}, u32[]{:S(2)}) collective-permute-start(bf16[256,128]{1,0:T(8,128)(2,1)} %get-tuple-element.21.refs_0_), channel_id=1, source_target_pairs={{0,8},{1,9},{4,12},{5,13},{8,0},{9,1},{12,4},{13,5},{2,10},{3,11},... | collective-permute-start | bytes 196616 | tf_op jit(solution)/shard_map/ppermute | solution.py:323
  62.2 9.2 %collective-permute-start.18 = (bf16[256,128]{1,0:T(8,128)(2,1)}, bf16[256,128]{1,0:T(8,128)(2,1)S(1)}, u32[]{:S(2)}, u32[]{:S(2)}) collective-permute-start(bf16[256,128]{1,0:T(8,128)(2,1)} %get-tuple-element.22), channel_id=1, source_target_pairs={{0,9},{1,8},{4,13},{5,12},{8,1},{9,0},{12,5},{13,4},{2,11},{3,10},... | collective-permute-start | bytes 196616 | tf_op jit(solution)/shard_map/ppermute | solution.py:323
  63.0 9.9 %copy-start.11 = (bf16[256,128]{1,0:T(8,128)(2,1)}, bf16[256,128]{1,0:T(8,128)(2,1)S(1)}, u32[]{:S(2)}) copy-start(bf16[256,128]{1,0:T(8,128)(2,1)S(1)} %collective-permute-done.14.refs_1_) | copy-start | bytes 196612
  63.0 8.4 %collective-permute-start.19 = (bf16[256,128]{1,0:T(8,128)(2,1)}, bf16[256,128]{1,0:T(8,128)(2,1)S(1)}, u32[]{:S(2)}, u32[]{:S(2)}) collective-permute-start(bf16[256,128]{1,0:T(8,128)(2,1)} %get-tuple-element.21.refs_0_), channel_id=1, source_target_pairs={{0,12},{1,13},{4,0},{5,1},{8,4},{9,5},{12,8},{13,9},{2,14},{3,15},... | collective-permute-start | bytes 196616 | tf_op jit(solution)/shard_map/ppermute | solution.py:323
  66.7 6.1 %copy-start.12 = (bf16[256,128]{1,0:T(8,128)(2,1)}, bf16[256,128]{1,0:T(8,128)(2,1)S(1)}, u32[]{:S(2)}) copy-start(bf16[256,128]{1,0:T(8,128)(2,1)S(1)} %collective-permute-done.15.refs_2_) | copy-start | bytes 196612
  66.7 6.1 %collective-permute-start.20 = (bf16[256,128]{1,0:T(8,128)(2,1)}, bf16[256,128]{1,0:T(8,128)(2,1)S(1)}, u32[]{:S(2)}, u32[]{:S(2)}) collective-permute-start(bf16[256,128]{1,0:T(8,128)(2,1)} %get-tuple-element.22), channel_id=1, source_target_pairs={{0,13},{1,12},{4,1},{5,0},{8,5},{9,4},{12,9},{13,8},{2,15},{3,14},... | collective-permute-start | bytes 196616 | tf_op jit(solution)/shard_map/ppermute | solution.py:323
  68.0 4.8 %copy-start.13 = (bf16[256,128]{1,0:T(8,128)(2,1)}, bf16[256,128]{1,0:T(8,128)(2,1)S(1)}, u32[]{:S(2)}) copy-start(bf16[256,128]{1,0:T(8,128)(2,1)S(1)} %collective-permute-done.16.refs_3_) | copy-start | bytes 196612
  70.7 2.2 %copy-start.14 = (bf16[256,128]{1,0:T(8,128)(2,1)}, bf16[256,128]{1,0:T(8,128)(2,1)S(1)}, u32[]{:S(2)}) copy-start(bf16[256,128]{1,0:T(8,128)(2,1)S(1)} %collective-permute-done.17.refs_4_) | copy-start | bytes 196612
  71.4 1.5 %copy-start.15 = (bf16[256,128]{1,0:T(8,128)(2,1)}, bf16[256,128]{1,0:T(8,128)(2,1)S(1)}, u32[]{:S(2)}) copy-start(bf16[256,128]{1,0:T(8,128)(2,1)S(1)} %collective-permute-done.18.refs_5_) | copy-start | bytes 196612
  71.4 1.5 %copy-start.16 = (bf16[256,128]{1,0:T(8,128)(2,1)}, bf16[256,128]{1,0:T(8,128)(2,1)S(1)}, u32[]{:S(2)}) copy-start(bf16[256,128]{1,0:T(8,128)(2,1)S(1)} %collective-permute-done.19.refs_6_) | copy-start | bytes 196612
  72.9 0.6 copy-start.17

commit v2 on v0

--- a/solution.py
+++ b/solution.py
@@ -4,19 +4,40 @@
 import jax
 import jax.numpy as jnp
 from jax import lax
+from jax.experimental import pallas as pl
+from jax.experimental.pallas import tpu as pltpu
 from jax.sharding import PartitionSpec as P
 
 ORDER = 6
-
+LANE = 128
 
 step_root = math.sqrt(0.08)
+
+VMEM = pltpu.VMEM
+SMEM = pltpu.SMEM
+
+
+def in_vmem():
+    return pl.BlockSpec(memory_space=VMEM)
+
+
+def in_smem():
+    return pl.BlockSpec(memory_space=SMEM)
+
+
+def in_any():
+    return pl.BlockSpec(memory_space=pl.ANY)
+
+
+def mm(a, b):
+    return jnp.dot(a, b, preferred_element_type=jnp.float32)
 
 
 def fold_rows(operator, carry, piece, start):
     return jnp.einsum("wnm,wme->wne", operator, piece, preferred_element_type=jnp.float32)
 
 
-def per_device(walkers, inv_intersection, trial, vectors, aux_field, log_weight, copy_list):
+def general_device(walkers, inv_intersection, trial, vectors, aux_field, log_weight, copy_list):
     green = jnp.einsum(
         "wne,wef->wnf", walkers, inv_intersection, preferred_element_type=jnp.float32
     ).astype(jnp.bfloat16)
@@ -50,19 +71,409 @@
     return (every_walker[copy_list], every_log[copy_list])
 
 
+def bias_kernel(aux_ref, log_ref, walkers_hbm, inv_hbm, trial_hbm, vec_hbm, out_ref,
+                walkers_ref, inv_ref, trial_ref, vec_ref, green_ref, sems):
+    n_walk = walkers_hbm.shape[0]
+    n_vec = vec_hbm.shape[0]
+    copies = [
+        pltpu.make_async_copy(walkers_hbm, walkers_ref, sems.at[0]),
+        pltpu.make_async_copy(inv_hbm, inv_ref, sems.at[1]),
+        pltpu.make_async_copy(trial_hbm, trial_ref, sems.at[2]),
+    ]
+    vec_copies = [
+        pltpu.make_async_copy(vec_hbm.at[g], vec_ref.at[g], sems.at[3 + g]) for g in range(n_vec)
+    ]
+    for copy in copies + vec_copies:
+        copy.start()
+    out_ref[...] = jnp.zeros_like(out_ref)
+    out_ref[pl.ds(n_walk, n_walk), :] = aux_ref[...]
+    out_ref[pl.ds(2 * n_walk, 1), :] = log_ref[...]
+    copies[0].wait()
+    copies[1].wait()
+    for w in range(n_walk):
+        green_ref[w] = mm(walkers_ref[w], inv_ref[w]).astype(jnp.bfloat16).astype(jnp.float32)
+    copies[2].wait()
+    trial = trial_ref[...]
+    lane = lax.broadcasted_iota(jnp.int32, (n_walk, n_vec), 1)
+    total = jnp.zeros((n_walk, n_vec), jnp.float32)
+    for g in range(n_vec):
+        vec_copies[g].wait()
+        mixed = mm(vec_ref[g], trial).astype(jnp.bfloat16).astype(jnp.float32)
+        rows = [jnp.sum(green_ref[w] * mixed, axis=0, keepdims=True) for w in range(n_walk)]
+        column = jnp.sum(jnp.concatenate(rows, axis=0), axis=1, keepdims=True)
+        total = total + jnp.where(lane == g, column, 0.0)
+    out_ref[pl.ds(0, n_walk), :] = total
+
+
+def partial_bias_of(aux, log_weight, walkers, inv, trial, vectors):
+    n_walk, n_vec = aux.shape
+    return pl.pallas_call(
+        bias_kernel,
+        out_shape=jax.ShapeDtypeStruct((3 * n_walk, n_vec), jnp.float32),
+        in_specs=[in_vmem()] * 2 + [in_any()] * 4,
+        out_specs=in_vmem(),
+        scratch_shapes=[
+            VMEM(walkers.shape, walkers.dtype),
+            VMEM(inv.shape, inv.dtype),
+            VMEM(trial.shape, trial.dtype),
+            VMEM(vectors.shape, vectors.dtype),
+            VMEM(walkers.shape, jnp.float32),
+            pltpu.SemaphoreType.DMA((3 + n_vec,)),
+        ],
+        name="bias",
+    )(aux, log_weight[None, :], walkers, inv, trial, vectors)
+
+
+def operator_kernel(n_z, n_o, group, copy_ref, own_ref, orb_ref, walk_ref, far_ref, here_hbm, mate_hbm,
+                    factor_ref, log_ref, *rest):
+    piece_refs = rest[:n_z]
+    vec_ref, field_ref, weight_ref, sems = rest[n_z:]
+    n_walk = own_ref.shape[0] // 3
+    n_vec = own_ref.shape[1]
+    size = here_hbm.shape[2]
+    n_rows = here_hbm.shape[1]
+    n_block = size // LANE
+    z, x, o = lax.axis_index("vec"), lax.axis_index("walk"), lax.axis_index("orb")
+
+    def block_copy(b, source):
+        rows = pl.ds(b * LANE % n_rows, LANE)
+        cols = pl.ds(b * LANE, size - b * LANE)
+        return pltpu.make_async_copy(
+            source.at[:, rows, cols], vec_ref.at[:, pl.ds(b * LANE, LANE), cols], sems.at[b]
+        )
+
+    for b in range(n_block):
+        mine = o == b * LANE // n_rows
+
+        @pl.when(mine)
+        def _():
+            block_copy(b, here_hbm).start()
+
+        @pl.when(jnp.logical_not(mine))
+        def _():
+            block_copy(b, mate_hbm).start()
+
+    bias = jnp.concatenate(
+        [own_ref[pl.ds(0, n_walk), :] + orb_ref[pl.ds(0, n_walk), :],
+         walk_ref[pl.ds(0, n_walk), :] + far_ref[pl.ds(0, n_walk), :]], axis=0
+    )
+    aux = jnp.concatenate([own_ref[pl.ds(n_walk, n_walk), :], walk_ref[pl.ds(n_walk, n_walk), :]], axis=0)
+    shift = -step_root * bias
+    field_ref[...] = (aux - shift) * step_root
+    factor_ref[...] = jnp.sum(aux * shift - 0.5 * shift * shift, axis=1, keepdims=True)
+    for side, ref in enumerate((own_ref, walk_ref)):
+        square = (n_walk, n_walk)
+        eye = lax.broadcasted_iota(jnp.int32, square, 0) == lax.broadcasted_iota(jnp.int32, square, 1)
+        log_ref[pl.ds(side * n_walk, n_walk), :] = jnp.sum(
+            jnp.where(eye, ref[pl.ds(2 * n_walk, 1), :], 0.0), axis=1, keepdims=True
+        )
+    for k in range(n_z):
+        source = copy_ref[jnp.bitwise_xor(z, k) * n_o + o]
+        row = lax.rem(source, n_walk) + n_walk * (lax.div(source, n_walk) != x).astype(jnp.int32)
+        weight_ref[pl.ds(k, 1), :] = field_ref[pl.ds(row, 1), :]
+    weighted = weight_ref[...].astype(jnp.bfloat16)
+    tall_shape = (n_z * group, n_z)
+    pick = lax.broadcasted_iota(jnp.int32, tall_shape, 0) // group == lax.broadcasted_iota(
+        jnp.int32, tall_shape, 1
+    )
+    tall = mm(pick.astype(jnp.float32).astype(jnp.bfloat16), weighted).astype(jnp.bfloat16)
+    wide_shape = (n_vec, n_vec * group)
+    spread = lax.broadcasted_iota(jnp.int32, wide_shape, 1) // group == lax.broadcasted_iota(
+        jnp.int32, wide_shape, 0
+    )
+    wide = mm(tall, spread.astype(jnp.float32).astype(jnp.bfloat16))
+    row_in = lax.rem(lax.broadcasted_iota(jnp.int32, wide.shape, 0), group)
+    col_in = lax.rem(lax.broadcasted_iota(jnp.int32, wide.shape, 1), group)
+    spreader = jnp.where(row_in == col_in, wide, 0.0).astype(jnp.bfloat16)
+
+    half = n_block // 2
+    offsets, at = {}, half * LANE
+    for i in range(n_block):
+        for j in range(i + 1, n_block):
+            offsets[(i, j)] = at
+            at += LANE
+    lane = lax.broadcasted_iota(jnp.int32, (group, LANE), 1)
+    line = lax.broadcasted_iota(jnp.int32, (group, LANE), 0)
+    kept = {}
+    for i in range(n_block):
+        if i < n_block:
+            block_copy(i, here_hbm).wait()
+        diagonal = [jnp.zeros((1, LANE), jnp.float32) for _ in range(n_z)]
+        for step in range(LANE // group):
+            low = i * LANE + step * group
+            stack = vec_ref[:, pl.ds(low, group), pl.ds(i * LANE, size - i * LANE)]
+            value = mm(spreader, stack.reshape(n_vec * group, size - i * LANE))
+            value = value.reshape(n_z, group, size - i * LANE)
+            row_at = line + step * group
+            for k in range(n_z):
+                first = value[k, :, :LANE]
+                spot = pl.ds((i // 2) * LANE + step * group, group)
+                if i % 2 == 0:
+                    kept[(k, step)] = first
+                else:
+                    merged = jnp.where(row_at <= lane, kept[(k, step)], first)
+                    piece_refs[k][spot, :] = merged.astype(jnp.bfloat16)
+                    diagonal[k] = diagonal[k] + jnp.sum(
+                        jnp.where(row_at == lane, first, 0.0), axis=0, keepdims=True
+                    )
+                for j in range(i + 1, n_block):
+                    spot = pl.ds(offsets[(i, j)] + step * group, group)
+                    part = value[k, :, (j - i) * LANE : (j - i + 1) * LANE]
+                    piece_refs[k][spot, :] = part.astype(jnp.bfloat16)
+        if i % 2 == 1:
+            for k in range(n_z):
+                piece_refs[k][pl.ds(at + (i // 2) * 16, 16), :] = jnp.broadcast_to(
+                    diagonal[k], (16, LANE)
+                ).astype(jnp.bfloat16)
+
+
+def piece_rows(size):
+    n_block = size // LANE
+    return (n_block // 2 + n_block * (n_block - 1) // 2) * LANE + n_block // 2 * 16
+
+
+def partial_operators(copy_list, packs, vectors, mate_vectors, n_z, n_o):
+    n_walk, n_vec = packs[0].shape[0] // 3, packs[0].shape[1]
+    size = vectors.shape[2]
+    group = 2 * LANE // n_vec
+    piece = jax.ShapeDtypeStruct((piece_rows(size), LANE), jnp.bfloat16)
+    column = jax.ShapeDtypeStruct((2 * n_walk, 1), jnp.float32)
+    return pl.pallas_call(
+        partial(operator_kernel, n_z, n_o, group),
+        out_shape=[column, column] + [piece] * n_z,
+        in_specs=[in_smem()] + [in_vmem()] * 4 + [in_any()] * 2,
+        out_specs=[in_vmem()] * (2 + n_z),
+        scratch_shapes=[
+            VMEM((n_vec, size, size), vectors.dtype),
+            VMEM((2 * n_walk, n_vec), jnp.float32),
+            VMEM((n_z, n_vec), jnp.float32),
+            pltpu.SemaphoreType.DMA((size // LANE,)),
+        ],
+        name="operators",
+    )(copy_list, *packs, vectors, mate_vectors)
+
+
+def source_kernel(n_o, copy_ref, far_ref, walkers_hbm, own_out, orb_out, walk_out, diag_out, sems):
+    n_walk = walkers_hbm.shape[0]
+    z, o = lax.axis_index("vec"), lax.axis_index("orb")
+    slot, mate = z * n_o + o, z * n_o + (n_o - 1 - o)
+    wanted = [
+        (copy_ref, slot, own_out), (copy_ref, mate, orb_out), (far_ref, slot, walk_out), (far_ref, mate, diag_out)
+    ]
+    copies = [
+        pltpu.make_async_copy(walkers_hbm.at[lax.rem(ref[at], n_walk)], out, sems.at[i])
+        for i, (ref, at, out) in enumerate(wanted)
+    ]
+    for copy in copies:
+        copy.start()
+    for copy in copies:
+        copy.wait()
+
+
+def source_walkers(copy_list, far_copy, walkers, n_o):
+    out = jax.ShapeDtypeStruct(walkers.shape[1:], walkers.dtype)
+    return pl.pallas_call(
+        partial(source_kernel, n_o),
+        out_shape=[out] * 4,
+        in_specs=[in_smem()] * 2 + [in_any()],
+        out_specs=[in_vmem()] * 4,
+        scratch_shapes=[pltpu.SemaphoreType.DMA((4,))],
+        name="sources",
+    )(copy_list, far_copy, walkers)
+
+
+def weights_kernel(copy_ref, log_ref, f0, f1, f2, f3, out_ref):
+    n_both = log_ref.shape[0]
+    n_walk = n_both // 2
+    x = lax.axis_index("walk")
+    new_log = log_ref[...] + ((f0[...] + f1[...]) + (f2[...] + f3[...]))
+    source = copy_ref[...]
+    row = lax.rem(source, n_walk) + n_walk * (lax.div(source, n_walk) != x).astype(jnp.int32)
+    shape = (n_both, source.shape[1])
+    at = lax.broadcasted_iota(jnp.int32, shape, 0)
+    out_ref[...] = jnp.sum(
+        jnp.where(at == jnp.broadcast_to(row, shape), jnp.broadcast_to(new_log, shape), 0.0),
+        axis=0, keepdims=True,
+    )
+
+
+def slot_weights(copy_list, log_column, factors):
+    return pl.pallas_call(
+        weights_kernel,
+        out_shape=jax.ShapeDtypeStruct((1,) + copy_list.shape, jnp.float32),
+        in_specs=[in_vmem()] * 6,
+        out_specs=in_vmem(),
+        name="weights",
+    )(copy_list[None, :], log_column, *factors)[0]
+
+
+def taylor_kernel(n_z, n_o, copy_ref, *refs):
+    pieces = refs[:n_z]
+    own_ref, orb_ref, walk_ref, far_ref, mine_ref, other_ref, op_ref, term_ref, sum_ref = refs[n_z:]
+    z, x, o = lax.axis_index("vec"), lax.axis_index("walk"), lax.axis_index("orb")
+    n_walk = copy_ref.shape[0]
+    n_block = op_ref.shape[0] // LANE
+    i_at = lax.broadcasted_iota(jnp.int32, (LANE, LANE), 0)
+    j_at = lax.broadcasted_iota(jnp.int32, (LANE, LANE), 1)
+
+    def total(start, count):
+        result = pieces[0][pl.ds(start, count), :].astype(jnp.float32)
+        for piece in pieces[1:]:
+            result = result + piece[pl.ds(start, count), :].astype(jnp.float32)
+        return result
+
+    def put(i, j, value):
+        op_ref[pl.ds(i * LANE, LANE), pl.ds(j * LANE, LANE)] = value.astype(jnp.bfloat16)
+
+    at = n_block // 2 * LANE
+    for i in range(n_block):
+        for j in range(i + 1, n_block):
+            value = total(at, LANE)
+            put(i, j, value)
+            put(j, i, value.T)
+            at += LANE
+    for pair in range(n_block // 2):
+        merged = total(pair * LANE, LANE)
+        diagonal = total(at + pair * 16, 16)[:1]
+        turned = merged.T
+        put(2 * pair, 2 * pair, jnp.where(i_at <= j_at, merged, turned))
+        second = jnp.where(i_at > j_at, merged, turned)
+        put(2 * pair + 1, 2 * pair + 1, jnp.where(i_at == j_at, diagonal, second))
+
+    here = lax.div(copy_ref[z * n_o + o], n_walk) == x
+    rows = own_ref.shape[0]
+    top = pl.ds(pl.multiple_of(o * rows, rows), rows)
+    bottom = pl.ds(pl.multiple_of((1 - o) * rows, rows), rows)
+    term_ref[top, :] = jnp.where(here, own_ref[...], walk_ref[...])
+    term_ref[bottom, :] = jnp.where(here, orb_ref[...], far_ref[...])
+    sum_ref[...] = term_ref[...].astype(jnp.float32)
+    for degree in range(1, ORDER + 1):
+        product = mm(op_ref[...], term_ref[...])
+        term = (product / degree).astype(jnp.bfloat16)
+        sum_ref[...] += term.astype(jnp.float32)
+        if degree < ORDER:
+            term_ref[...] = term
+    mine_ref[...] = sum_ref[top, :].astype(jnp.bfloat16)
+    other_ref[...] = sum_ref[bottom, :].astype(jnp.bfloat16)
+
+
+def taylor(copy_list, pieces, candidates, n_o):
+    rows, width = candidates[0].shape
+    size = n_o * rows
+    out = jax.ShapeDtypeStruct((rows, width), jnp.bfloat16)
+    return pl.pallas_call(
+        partial(taylor_kernel, len(pieces), n_o),
+        out_shape=[out, out],
+        in_specs=[in_smem()] + [in_vmem()] * (len(pieces) + 4),
+        out_specs=[in_vmem()] * 2,
+        scratch_shapes=[
+            VMEM((size, size), jnp.bfloat16),
+            VMEM((size, width), jnp.bfloat16),
+            VMEM((size, width), jnp.float32),
+        ],
+        name="taylor",
+    )(copy_list, *pieces, *candidates)
+
+
+def place_kernel(steps, n_o, *refs):
+    n_line = len(steps)
+    pieces, out_ref, sems = refs[:n_line], refs[n_line], refs[n_line + 1]
+    z, o = lax.axis_index("vec"), lax.axis_index("orb")
+    copies = [
+        pltpu.make_async_copy(
+            pieces[k],
+            out_ref.at[jnp.bitwise_xor(z, dz) * n_o + jnp.bitwise_xor(o, flip)],
+            sems.at[k],
+        )
+        for k, (dz, flip) in enumerate(steps)
+    ]
+    for copy in copies:
+        copy.start()
+    for copy in copies:
+        copy.wait()
+
+
+def put_in_place(steps, pieces, n_o):
+    n_line = len(pieces)
+    return pl.pallas_call(
+        partial(place_kernel, steps, n_o),
+        out_shape=jax.ShapeDtypeStruct((n_line,) + pieces[0].shape, pieces[0].dtype),
+        in_specs=[in_any()] * n_line,
+        out_specs=in_vmem(),
+        scratch_shapes=[pltpu.SemaphoreType.DMA((n_line,))],
+        name="place",
+    )(*pieces)
+
+
+def swapped(value, axes, sizes, masks):
+    perm = []
+    for a in range(sizes[0]):
+        for b in range(sizes[1]):
+            perm.append((a * sizes[1] + b, (a ^ masks[0]) * sizes[1] + (b ^ masks[1])))
+    return lax.ppermute(value, axes, perm)
+
+
+def slot_device(n_z, n_x, n_o, walkers, inv_intersection, trial, vectors, aux_field, log_weight, copy_list):
+    line = partial(swapped, axes=("vec", "orb"), sizes=(n_z, n_o))
+    near = partial(swapped, axes=("walk", "orb"), sizes=(n_x, n_o))
+
+    mate_vectors = near(vectors, masks=(0, 1))
+    far_copy = near(copy_list, masks=(1, 0))
+    own_pack = partial_bias_of(aux_field, log_weight, walkers, inv_intersection, trial, vectors)
+    packs = [own_pack] + [near(own_pack, masks=m) for m in ((0, 1), (1, 0), (1, 1))]
+    wanted = source_walkers(copy_list, far_copy, walkers, n_o)
+    candidates = [wanted[0]] + [
+        near(value, masks=m) for value, m in zip(wanted[1:], ((0, 1), (1, 0), (1, 1)))
+    ]
+    factor, log_column, *pieces = partial_operators(copy_list, packs, vectors, mate_vectors, n_z, n_o)
+    arrived = [pieces[0]] + [line(pieces[k], masks=(k, 0)) for k in range(1, n_z)]
+    factors = [factor] + [line(factor, masks=(k, 0)) for k in range(1, n_z)]
+    weights_out = slot_weights(copy_list, log_column, factors)
+
+    mine, other = taylor(copy_list, arrived, candidates, n_o)
+    steps = [(k, flip) for k in range(n_z) for flip in range(n_o)]
+    landed = []
+    for dz, flip in steps:
+        half = mine if flip == 0 else other
+        landed.append(half if (dz, flip) == (0, 0) else line(half, masks=(dz, flip)))
+    return put_in_place(steps, landed, n_o), weights_out
+
+
+def suits(mesh, walkers, trial, vectors):
+    n_z, n_x, n_o = mesh.shape["vec"], mesh.shape["walk"], mesh.shape["orb"]
+    per_device = walkers.shape[0] // (mesh.shape["grp"] * n_x)
+    local_vectors = vectors.shape[0] // n_z
+    return (
+        n_o == 2
+        and n_x == 2
+        and n_z == 4
+        and per_device == n_z * n_o
+        and local_vectors == per_device
+        and vectors.shape[1] == 4 * LANE
+        and trial.shape[1] == LANE
+    )
+
+
 def solution(mesh):
-    return jax.shard_map(
-        per_device,
-        mesh=mesh,
-        in_specs=(
-            P(("grp", "walk"), "orb", None),
-            P(("grp", "walk"), None, None),
-            P(),
-            P("vec", "orb", None),
-            P(("grp", "walk"), "vec"),
-            P(("grp", "walk")),
-            P(("grp", "walk")),
-        ),
-        out_specs=(P(("grp", "walk"), "orb", None), P(("grp", "walk"))),
-        check_vma=False,
-    )
+    def step(walkers, inv_intersection, trial, vectors, aux_field, log_weight, copy_list):
+        if suits(mesh, walkers, trial, vectors):
+            body = partial(slot_device, mesh.shape["vec"], mesh.shape["walk"], mesh.shape["orb"])
+        else:
+            body = general_device
+        return jax.shard_map(
+            body,
+            mesh=mesh,
+            in_specs=(
+                P(("grp", "walk"), "orb", None),
+                P(("grp", "walk"), None, None),
+                P(),
+                P("vec", "orb", None),
+                P(("grp", "walk"), "vec"),
+                P(("grp", "walk")),
+                P(("grp", "walk")),
+            ),
+            out_specs=(P(("grp", "walk"), "orb", None), P(("grp", "walk"))),
+            check_vma=False,
+        )(walkers, inv_intersection, trial, vectors, aux_field, log_weight, copy_list)
+
+    return step

time: 277 us -> 74.1 us (0.27)
  blocking collectives: 158 us -> 0 us
  waiting for transfers between devices: 65.4 us -> 23.6 us
  matrix products: 31.5 us -> 0 us
  starting transfers between devices: 0.29 us -> 25.3 us
  Pallas kernels: 0 us -> 19.6 us
  between operations: 14.9 us -> 0.8 us
    psum x2 -> x0, blocking collectives: 153 us -> none  [the longest x1 151 us: per_device(): operator = lax.psum(local_operator, 'vec').astype(jnp.bfloat16)]
    all_gather x7 -> x0, waiting for transfers between devices: 64.6 us -> none  [the longest x6 49.4 us: per_device(): lax.all_gather(operand, 'orb', axis=1, tiled=True)]
    dot_general x10 -> x0, matrix products: 31.5 us -> none  [the longest x6 24.9 us: fold_rows(): jnp.einsum('wnm,wme->wne', operator, piece, preferred_element_type=jnp.fl...]
    ppermute x0 -> x21, starting transfers between devices: none -> 25.3 us  [swapped(): return lax.ppermute(value, axes, perm)]
    ppermute x0 -> x21, waiting for transfers between devices: none -> 23.6 us  [swapped(): return lax.ppermute(value, axes, perm)]
    pallas_call x0 -> x6, Pallas kernels: none -> 19.6 us  [the longest x1 5.49 us: partial_bias_of(): pl.pallas_call(bias_kernel, out_shape=jax.ShapeDtypeStruct((3 * n_walk, n...]
    unnamed x1 -> x0, blocking collectives: 4.91 us -> none
    unnamed x18 -> x44, local copies, waits for them, and re-layouts: 0.64 us -> 4.5 us
  transfers between devices with their start and end apart: 7 -> 21, of which waited for: 6 -> 10; matrix products, arithmetic and copies ran while one was open for 4% -> 0% of each run, Pallas kernels for 0% -> 13%
where the time goes in v2:
time: 74.1 us; the launch traced here: 73.7 us
  starting transfers between devices  25.3 us (34%)
  waiting for transfers between devices  23.6 us (32%)
  Pallas kernels  19.6 us (26%)
  local copies, waits for them, and re-layouts  4.5 us (6%)
  between operations  0.8 us (1%)
    ppermute x21, starting transfers between devices, swapped(): return lax.ppermute(value, axes, perm)  25.3 us
    ppermute x21, waiting for transfers between devices, swapped(): return lax.ppermute(value, axes, perm)  23.6 us
    pallas_call x1, Pallas kernels, partial_bias_of(): pl.pallas_call(bias_kernel, out_shape=jax.ShapeDtypeStruct((3 * n_walk, n...  5.49 us
    unnamed x44, local copies, waits for them, and re-layouts  4.5 us
    pallas_call x1, Pallas kernels, taylor(): pl.pallas_call(partial(taylor_kernel, len(pieces), n_o), out_shape=[out,...  4.32 us
    pallas_call x1, Pallas kernels, partial_operators(): pl.pallas_call(partial(operator_kernel, n_z, n_o, group), out_shape=[colu...  4.1 us
    pallas_call x1, Pallas kernels, source_walkers(): pl.pallas_call(partial(source_kernel, n_o), out_shape=[out] * 4, in_specs...  2.36 us
    pallas_call x1, Pallas kernels, put_in_place(): pl.pallas_call(partial(place_kernel, steps, n_o), out_shape=jax.ShapeDtyp...  1.92 us
  transfers between devices with their start and end apart: 21, of which 10 were waited for; matrix products, arithmetic and copies ran while one was open for 0% of the time, Pallas kernels for 13%

profile of v2, /device:TPU:0, one launch (start us, length us, event | category | flops | bytes accessed | tf_op | source)
XLA Modules:
  0.0 73.7 jit_solution(3564082204583363502)
XLA Ops:
  0.6 0.6 collective-permute-start.3
  1.2 5.5 %bias.1.own_ref = f32[24,8]{1,0:T(8,128)} custom-call(f32[8,8]{1,0:T(8,128)} %aux_ref.1, f32[1,8]{1,0:T(1,128)} %bitcast.4, bf16[8,256,128]{2,1,0:T(8,128)(2,1)} %walkers_hbm.3, bf16[8,128,128]{2,1,0:T(8,128)(2,1)} %inv_hbm.1, bf16[512,128]{1,0:T(8,128)(2,1)} %trial_hbm.1, bf16[8,256,512]{2,1,0:T(8,128)(2,1)} %here_hbm.1), custom_call_target="tpu_custom_call" | custom-call | tf_op jit(solution)/shard_map/bias/pallas_call | solution.py:110
  6.7 0.0 copy-start.17
  6.7 0.1 collective-permute-start
  6.8 3.0 %collective-permute-start.1 = (f32[24,8]{1,0:T(8,128)}, f32[24,8]{1,0:T(8,128)S(1)}, u32[]{:S(2)}, u32[]{:S(2)}) collective-permute-start(f32[24,8]{1,0:T(8,128)} %bias.1.own_ref), channel_id=1, source_target_pairs={{0,2},{1,3},{2,0},{3,1},{4,6},{5,7},{6,4},{7,5},{8,10},{9,11},{10,... | collective-permute-start | bytes 2312 | tf_op jit(solution)/shard_map/ppermute | solution.py:413
  9.8 0.0 collective-permute-done.orb_ref
  9.8 1.9 %collective-permute-done.1.walk_ref = f32[24,8]{1,0:T(8,128)S(1)} collective-permute-done((f32[24,8]{1,0:T(8,128)}, f32[24,8]{1,0:T(8,128)S(1)}, u32[]{:S(2)}, u32[]{:S(2)}) %collective-permute-start.1) | collective-permute-done | bytes 800 | tf_op jit(solution)/shard_map/ppermute | solution.py:413
  11.6 1.6 %collective-permute-done.2.far_ref = f32[24,8]{1,0:T(8,128)S(1)} collective-permute-done((f32[24,8]{1,0:T(8,128)}, f32[24,8]{1,0:T(8,128)S(1)}, u32[]{:S(2)}, u32[]{:S(2)}) %collective-permute-start.2) | collective-permute-done | bytes 800 | tf_op jit(solution)/shard_map/ppermute | solution.py:413
  13.2 0.0 collective-permute-done.3.mate_hbm
  13.2 0.6 copy-done.16
  13.8 1.3 %copy-done = bf16[8,256,512]{2,1,0:T(8,128)(2,1)} copy-done((bf16[8,256,512]{2,1,0:T(8,128)(2,1)}, bf16[8,256,512]{2,1,0:T(8,128)(2,1)S(1)}, u32[]{:S(2)}) %copy-start) | copy-done | bytes 2097176
  15.1 4.1 %operators.1 = (f32[16,1]{1,0:T(8,128)}, f32[16,1]{1,0:T(8,128)}, bf16[1056,128]{1,0:T(8,128)(2,1)}, bf16[1056,128]{1,0:T(8,128)(2,1)}, bf16[1056,128]{1,0:T(8,128)(2,1)}, /*index=5*/bf16[1056,128]{1,0:T(8,128)(2,1)}) custom-call(s32[8]{0:T(128)} %copy_ref.5, f32[24,8]{1,0:T(8,128)} %bias.1.own_ref, f32[24,8]{1,0:T(8,128)} %copy-done.14, ...), custom_call_target="tpu_custom_call" | custom-call | tf_op jit(solution)/shard_map/operators/pallas_call | solution.py:241
  19.3 1.6 %collective-permute-start.4 = (bf16[1056,128]{1,0:T(8,128)(2,1)}, bf16[1056,128]{1,0:T(8,128)(2,1)S(1)}, u32[]{:S(2)}, u32[]{:S(2)}) collective-permute-start(bf16[1056,128]{1,0:T(8,128)(2,1)} %get-tuple-element.15), channel_id=1, source_target_pairs={{0,4},{1,5},{4,0},{5,1},{8,12},{9,13},{12,8},{13,9},{2,6},{3,7},{6... | collective-permute-start | bytes 811016 | tf_op jit(solution)/shard_map/ppermute | solution.py:413
  20.9 2.6 %collective-permute-start.5 = (bf16[1056,128]{1,0:T(8,128)(2,1)}, bf16[1056,128]{1,0:T(8,128)(2,1)S(1)}, u32[]{:S(2)}, u32[]{:S(2)}) collective-permute-start(bf16[1056,128]{1,0:T(8,128)(2,1)} %get-tuple-element.16), channel_id=1, source_target_pairs={{0,8},{1,9},{4,12},{5,13},{8,0},{9,1},{12,4},{13,5},{2,10},{3,11},... | collective-permute-start | bytes 811016 | tf_op jit(solution)/shard_map/ppermute | solution.py:413
  23.5 0.2 collective-permute-start.6
  23.7 0.5 collective-permute-start.7
  24.2 3.1 %collective-permute-done.7.far_ref = s32[8]{0:T(128)S(1)} collective-permute-done((s32[8]{0:T(128)S(1)}, s32[8]{0:T(128)S(1)}, u32[]{:S(2)}, u32[]{:S(2)}) %collective-permute-start.7) | collective-permute-done | bytes 64 | tf_op jit(solution)/shard_map/ppermute | solution.py:413
  27.3 0.5 copy-done.21
  27.8 2.4 %sources.1 = (bf16[256,128]{1,0:T(8,128)(2,1)}, bf16[256,128]{1,0:T(8,128)(2,1)}, bf16[256,128]{1,0:T(8,128)(2,1)}, bf16[256,128]{1,0:T(8,128)(2,1)}) custom-call(s32[8]{0:T(128)} %copy_ref.5, s32[8]{0:T(128)} %copy-done.21, bf16[8,256,128]{2,1,0:T(8,128)(2,1)} %walkers_hbm.3), custom_call_target="tpu_custom_call" | custom-call | tf_op jit(solution)/shard_map/sources/pallas_call | solution.py:275
  30.2 0.1 collective-permute-start.10
  30.2 0.6 collective-permute-start.8
  30.8 3.3 %collective-permute-done.10.refs_7_ = bf16[256,128]{1,0:T(8,128)(2,1)S(1)} collective-permute-done((bf16[256,128]{1,0:T(8,128)(2,1)}, bf16[256,128]{1,0:T(8,128)(2,1)S(1)}, u32[]{:S(2)}, u32[]{:S(2)}) %collective-permute-start.10) | collective-permute-done | bytes 65568 | tf_op jit(solution)/shard_map/ppermute | solution.py:413
  34.1 1.1 %collective-permute-start.9 = (bf16[256,128]{1,0:T(8,128)(2,1)}, bf16[256,128]{1,0:T(8,128)(2,1)S(1)}, u32[]{:S(2)}, u32[]{:S(2)}) collective-permute-start(bf16[256,128]{1,0:T(8,128)(2,1)} %get-tuple-element.20), channel_id=1, source_target_pairs={{0,2},{1,3},{2,0},{3,1},{4,6},{5,7},{6,4},{7,5},{8,10},{9,11},{10,... | collective-permute-start | bytes 196616 | tf_op jit(solution)/shard_map/ppermute | solution.py:413
  35.2 0.0 collective-permute-done.8.refs_5_
  35.2 3.4 %collective-permute-done.9.refs_6_ = bf16[256,128]{1,0:T(8,128)(2,1)S(1)} collective-permute-done((bf16[256,128]{1,0:T(8,128)(2,1)}, bf16[256,128]{1,0:T(8,128)(2,1)S(1)}, u32[]{:S(2)}, u32[]{:S(2)}) %collective-permute-start.9) | collective-permute-done | bytes 65568 | tf_op jit(solution)/shard_map/ppermute | solution.py:413
  38.6 0.0 collective-permute-done.4.refs_1_
  38.6 4.3 %collective-permute-done.5.refs_2_ = bf16[1056,128]{1,0:T(8,128)(2,1)S(1)} collective-permute-done((bf16[1056,128]{1,0:T(8,128)(2,1)}, bf16[1056,128]{1,0:T(8,128)(2,1)S(1)}, u32[]{:S(2)}, u32[]{:S(2)}) %collective-permute-start.5) | collective-permute-done | bytes 270368 | tf_op jit(solution)/shard_map/ppermute | solution.py:413
  42.9 0.0 collective-permute-done.6.refs_3_
  43.0 0.7 copy-done.2
  43.7 0.1 copy-done.3
  43.8 4.3 %taylor.1 = (bf16[256,128]{1,0:T(8,128)(2,1)}, bf16[256,128]{1,0:T(8,128)(2,1)}) custom-call(s32[8]{0:T(128)} %copy_ref.5, bf16[1056,128]{1,0:T(8,128)(2,1)} %get-tuple-element.14.refs_0_, bf16[1056,128]{1,0:T(8,128)(2,1)} %copy-done.1, bf16[1056,128]{1,0:T(8,128)(2,1)} %copy-done.2, bf16[1056,128]{1,0:T(8,128)(2,1)} %copy-done.3, ...), custom_call_target="tpu_custom_call" | custom-call | tf_op jit(solution)/shard_map/taylor/pallas_call | solution.py:364
  48.1 5.2 %collective-permute-start.12 = (bf16[256,128]{1,0:T(8,128)(2,1)}, bf16[256,128]{1,0:T(8,128)(2,1)S(1)}, u32[]{:S(2)}, u32[]{:S(2)}) collective-permute-start(bf16[256,128]{1,0:T(8,128)(2,1)} %get-tuple-element.22.refs_0_), channel_id=1, source_target_pairs={{0,4},{1,5},{4,0},{5,1},{8,12},{9,13},{12,8},{13,9},{2,6},{3,7},{6... | collective-permute-start | bytes 196616 | tf_op jit(solution)/shard_map/ppermute | solution.py:413
  53.3 0.1 collective-permute-start.18
  53.4 3.0 %collective-permute-start.19 = (f32[16,1]{1,0:T(8,128)}, f32[16,1]{1,0:T(8,128)S(1)}, u32[]{:S(2)}, u32[]{:S(2)}) collective-permute-start(f32[16,1]{1,0:T(8,128)} %get-tuple-element.25.f0), channel_id=1, source_target_pairs={{0,8},{1,9},{4,12},{5,13},{8,0},{9,1},{12,4},{13,5},{2,10},{3,11},... | collective-permute-start | bytes 200 | tf_op jit(solution)/shard_map/ppermute | solution.py:413
  56.3 1.3 %collective-permute-start.20 = (f32[16,1]{1,0:T(8,128)}, f32[16,1]{1,0:T(8,128)S(1)}, u32[]{:S(2)}, u32[]{:S(2)}) collective-permute-start(f32[16,1]{1,0:T(8,128)} %get-tuple-element.25.f0), channel_id=1, source_target_pairs={{0,12},{1,13},{4,8},{5,9},{8,4},{9,5},{12,0},{13,1},{2,14},{3,15},... | collective-permute-start | bytes 200 | tf_op jit(solution)/shard_map/ppermute | solution.py:413
  57.7 0.0 collective-permute-done.18.f1
  57.7 0.5 collective-permute-done.19.f2
  58.2 3.0 %collective-permute-start.14 = (bf16[256,128]{1,0:T(8,128)(2,1)}, bf16[256,128]{1,0:T(8,128)(2,1)S(1)}, u32[]{:S(2)}, u32[]{:S(2)}) collective-permute-start(bf16[256,128]{1,0:T(8,128)(2,1)} %get-tuple-element.22.refs_0_), channel_id=1, source_target_pairs={{0,8},{1,9},{4,12},{5,13},{8,0},{9,1},{12,4},{13,5},{2,10},{3,11},... | collective-permute-start | bytes 196616 | tf_op jit(solution)/shard_map/ppermute | solution.py:413
  61.2 0.9 %collective-permute-done.20.f3 = f32[16,1]{1,0:T(8,128)S(1)} collective-permute-done((f32[16,1]{1,0:T(8,128)}, f32[16,1]{1,0:T(8,128)S(1)}, u32[]{:S(2)}, u32[]{:S(2)}) %collective-permute-start.20) | collective-permute-done | bytes 96 | tf_op jit(solution)/shard_map/ppermute | solution.py:413
  62.1 1.4 %collective-permute-start.16 = (bf16[256,128]{1,0:T(8,128)(2,1)}, bf16[256,128]{1,0:T(8,128)(2,1)S(1)}, u32[]{:S(2)}, u32[]{:S(2)}) collective-permute-start(bf16[256,128]{1,0:T(8,128)(2,1)} %get-tuple-element.22.refs_0_), channel_id=1, source_target_pairs={{0,12},{1,13},{4,8},{5,9},{8,4},{9,5},{12,0},{13,1},{2,14},{3,15},... | collective-permute-start | bytes 196616 | tf_op jit(solution)/shard_map/ppermute | solution.py:413
  63.5 1.0 %collective-permute-start.17 = (bf16[256,128]{1,0:T(8,128)(2,1)}, bf16[256,128]{1,0:T(8,128)(2,1)S(1)}, u32[]{:S(2)}, u32[]{:S(2)}) collective-permute-start(bf16[256,128]{1,0:T(8,128)(2,1)} %get-tuple-element.23), channel_id=1, source_target_pairs={{0,13},{1,12},{4,9},{5,8},{8,5},{9,4},{12,1},{13,0},{2,15},{3,14},... | collective-permute-start | bytes 196616 | tf_op jit(solution)/shard_map/ppermute | solution.py:413
  64.5 1.4 %weights.1 = f32[1,8]{1,0:T(1,128)} custom-call(s32[1,8]{1,0:T(1,128)} %bitcast.3, f32[16,1]{1,0:T(8,128)} %get-tuple-element.24.log_ref, f32[16,1]{1,0:T(8,128)} %get-tuple-element.25.f0, f32[16,1]{1,0:T(8,128)} %copy-done.18, f32[16,1]{1,0:T(8,128)} %copy-done.19, f32[16,1]{1,0:T(8,128)} %copy-done.20), custom_call_target="tpu_custom_call" | custom-call | tf_op jit(solution)/shard_map/weights/pallas_call | solution.py:301
  65.9 1.4 %collective-permute-done.14.refs_4_ = bf16[256,128]{1,0:T(8,128)(2,1)S(1)} collective-permute-done((bf16[256,128]{1,0:T(8,128)(2,1)}, bf16[256,128]{1,0:T(8,128)(2,1)S(1)}, u32[]{:S(2)}, u32[]{:S(2)}) %collective-permute-start.14) | collective-permute-done | bytes 65568 | tf_op jit(solution)/shard_map/ppermute | solution.py:413
  67.3 3.2 %collective-permute-done.15.refs_5_ = bf16[256,128]{1,0:T(8,128)(2,1)S(1)} collective-permute-done((bf16[256,128]{1,0:T(8,128)(2,1)}, bf16[256,128]{1,0:T(8,128)(2,1)S(1)}, u32[]{:S(2)}, u32[]{:S(2)}) %collective-permute-start.15) | collective-permute-done | bytes 65568 | tf_op jit(solution)/shard_map/ppermute | solution.py:413
  70.6 0.6 copy-done.8
  71.1 0.0 copy-done.11
  71.2 0.6 copy-done.13
  71.8 1.9 %place.1 = bf16[8,256,128]{2,1,0:T(8,128)(2,1)} custom-call(bf16[256,128]{1,0:T(8,128)(2,1)} %get-tuple-element.22.refs_0_, bf16[256,128]{1,0:T(8,128)(2,1)} %copy-done.4, bf16[256,128]{1,0:T(8,128)(2,1)} %copy-done.5, bf16[256,128]{1,0:T(8,128)(2,1)} %copy-done.6, bf16[256,128]{1,0:T(8,128)(2,1)} %copy-done.7, bf16[256,128]{1,0:T(8,128)(2,1)} %copy-done.8, ...), custom_call_target="tpu_custom_call" | custom-call | tf_op jit(solution)/shard_map/place/pallas_call | solution.py:398
  (44 shorter events, 0.1 us)
Async XLA Ops:
  0.6 12.6 %collective-permute-start.3 = (bf16[8,256,512]{2,1,0:T(8,128)(2,1)}, bf16[8,256,512]{2,1,0:T(8,128)(2,1)S(1)}, u32[]{:S(2)}, u32[]{:S(2)}) collective-permute-start(bf16[8,256,512]{2,1,0:T(8,128)(2,1)} %here_hbm.1), channel_id=1, source_target_pairs={{0,1},{1,0},{2,3},{3,2},{4,5},{5,4},{6,7},{7,6},{8,9},{9,8},{10,11... | collective-permute-start | bytes 6291464 | tf_op jit(solution)/shard_map/ppermute | solution.py:413
  6.7 17.0 %copy-start.17 = (s32[8]{0:T(128)S(1)}, s32[8]{0:T(128)}, u32[]{:S(2)}) copy-start(s32[8]{0:T(128)} %copy_ref.5) | copy-start | bytes 100
  6.7 3.1 %collective-permute-start = (f32[24,8]{1,0:T(8,128)}, f32[24,8]{1,0:T(8,128)S(1)}, u32[]{:S(2)}, u32[]{:S(2)}) collective-permute-start(f32[24,8]{1,0:T(8,128)} %bias.1.own_ref), channel_id=1, source_target_pairs={{0,1},{1,0},{2,3},{3,2},{4,5},{5,4},{6,7},{7,6},{8,9},{9,8},{10,11... | collective-permute-start | bytes 2312 | tf_op jit(solution)/shard_map/ppermute | solution.py:413
  6.8 4.9 %collective-permute-start.1 = (f32[24,8]{1,0:T(8,128)}, f32[24,8]{1,0:T(8,128)S(1)}, u32[]{:S(2)}, u32[]{:S(2)}) collective-permute-start(f32[24,8]{1,0:T(8,128)} %bias.1.own_ref), channel_id=1, source_target_pairs={{0,2},{1,3},{2,0},{3,1},{4,6},{5,7},{6,4},{7,5},{8,10},{9,11},{10,... | collective-permute-start | bytes 2312 | tf_op jit(solution)/shard_map/ppermute | solution.py:413
  9.8 3.4 %collective-permute-start.2 = (f32[24,8]{1,0:T(8,128)}, f32[24,8]{1,0:T(8,128)S(1)}, u32[]{:S(2)}, u32[]{:S(2)}) collective-permute-start(f32[24,8]{1,0:T(8,128)} %bias.1.own_ref), channel_id=1, source_target_pairs={{0,3},{1,2},{2,1},{3,0},{4,7},{5,6},{6,5},{7,4},{8,11},{9,10},{10,... | collective-permute-start | bytes 2312 | tf_op jit(solution)/shard_map/ppermute | solution.py:413
  9.8 3.4 %copy-start.14 = (f32[24,8]{1,0:T(8,128)}, f32[24,8]{1,0:T(8,128)S(1)}, u32[]{:S(2)}) copy-start(f32[24,8]{1,0:T(8,128)S(1)} %collective-permute-done.orb_ref) | copy-start | bytes 2308
  11.6 1.6 %copy-start.15 = (f32[24,8]{1,0:T(8,128)}, f32[24,8]{1,0:T(8,128)S(1)}, u32[]{:S(2)}) copy-start(f32[24,8]{1,0:T(8,128)S(1)} %collective-permute-done.1.walk_ref) | copy-start | bytes 2308
  13.2 0.6 copy-start.16
  13.8 1.4 %copy-start = (bf16[8,256,512]{2,1,0:T(8,128)(2,1)}, bf16[8,256,512]{2,1,0:T(8,128)(2,1)S(1)}, u32[]{:S(2)}) copy-start(bf16[8,256,512]{2,1,0:T(8,128)(2,1)S(1)} %collective-permute-done.3.mate_hbm) | copy-start | bytes 6291460
  19.3 19.4 %collective-permute-start.4 = (bf16[1056,128]{1,0:T(8,128)(2,1)}, bf16[1056,128]{1,0:T(8,128)(2,1)S(1)}, u32[]{:S(2)}, u32[]{:S(2)}) collective-permute-start(bf16[1056,128]{1,0:T(8,128)(2,1)} %get-tuple-element.15), channel_id=1, source_target_pairs={{0,4},{1,5},{4,0},{5,1},{8,12},{9,13},{12,8},{13,9},{2,6},{3,7},{6... | collective-permute-start | bytes 811016 | tf_op jit(solution)/shard_map/ppermute | solution.py:413
  20.9 22.0 %collective-permute-start.5 = (bf16[1056,128]{1,0:T(8,128)(2,1)}, bf16[1056,128]{1,0:T(8,128)(2,1)S(1)}, u32[]{:S(2)}, u32[]{:S(2)}) collective-permute-start(bf16[1056,128]{1,0:T(8,128)(2,1)} %get-tuple-element.16), channel_id=1, source_target_pairs={{0,8},{1,9},{4,12},{5,13},{8,0},{9,1},{12,4},{13,5},{2,10},{3,11},... | collective-permute-start | bytes 811016 | tf_op jit(solution)/shard_map/ppermute | solution.py:413
  23.5 19.5 %collective-permute-start.6 = (bf16[1056,128]{1,0:T(8,128)(2,1)}, bf16[1056,128]{1,0:T(8,128)(2,1)S(1)}, u32[]{:S(2)}, u32[]{:S(2)}) collective-permute-start(bf16[1056,128]{1,0:T(8,128)(2,1)} %get-tuple-element.17), channel_id=1, source_target_pairs={{0,12},{1,13},{4,8},{5,9},{8,4},{9,5},{12,0},{13,1},{2,14},{3,15},... | collective-permute-start | bytes 811016 | tf_op jit(solution)/shard_map/ppermute | solution.py:413
  23.7 3.6 %collective-permute-start.7 = (s32[8]{0:T(128)S(1)}, s32[8]{0:T(128)S(1)}, u32[]{:S(2)}, u32[]{:S(2)}) collective-permute-start(s32[8]{0:T(128)S(1)} %copy-done.17), channel_id=1, source_target_pairs={{0,2},{1,3},{2,0},{3,1},{4,6},{5,7},{6,4},{7,5},{8,10},{9,11},{10,... | collective-permute-start | bytes 104 | tf_op jit(solution)/shard_map/ppermute | solution.py:413
  27.3 0.5 copy-start.21
  30.2 4.0 %collective-permute-start.10 = (bf16[256,128]{1,0:T(8,128)(2,1)}, bf16[256,128]{1,0:T(8,128)(2,1)S(1)}, u32[]{:S(2)}, u32[]{:S(2)}) collective-permute-start(bf16[256,128]{1,0:T(8,128)(2,1)} %get-tuple-element.21), channel_id=1, source_target_pairs={{0,3},{1,2},{2,1},{3,0},{4,7},{5,6},{6,5},{7,4},{8,11},{9,10},{10,... | collective-permute-start | bytes 196616 | tf_op jit(solution)/shard_map/ppermute | solution.py:413
  30.2 5.0 %collective-permute-start.8 = (bf16[256,128]{1,0:T(8,128)(2,1)}, bf16[256,128]{1,0:T(8,128)(2,1)S(1)}, u32[]{:S(2)}, u32[]{:S(2)}) collective-permute-start(bf16[256,128]{1,0:T(8,128)(2,1)} %get-tuple-element.19), channel_id=1, source_target_pairs={{0,1},{1,0},{2,3},{3,2},{4,5},{5,4},{6,7},{7,6},{8,9},{9,8},{10,11... | collective-permute-start | bytes 196616 | tf_op jit(solution)/shard_map/ppermute | solution.py:413
  34.1 8.8 %copy-start.9 = (bf16[256,128]{1,0:T(8,128)(2,1)}, bf16[256,128]{1,0:T(8,128)(2,1)S(1)}, u32[]{:S(2)}) copy-start(bf16[256,128]{1,0:T(8,128)(2,1)S(1)} %collective-permute-done.10.refs_7_) | copy-start | bytes 196612
  34.1 4.5 %collective-permute-start.9 = (bf16[256,128]{1,0:T(8,128)(2,1)}, bf16[256,128]{1,0:T(8,128)(2,1)S(1)}, u32[]{:S(2)}, u32[]{:S(2)}) collective-permute-start(bf16[256,128]{1,0:T(8,128)(2,1)} %get-tuple-element.20), channel_id=1, source_target_pairs={{0,2},{1,3},{2,0},{3,1},{4,6},{5,7},{6,4},{7,5},{8,10},{9,11},{10,... | collective-permute-start | bytes 196616 | tf_op jit(solution)/shard_map/ppermute | solution.py:413
  35.2 7.8 %copy-start.10 = (bf16[256,128]{1,0:T(8,128)(2,1)}, bf16[256,128]{1,0:T(8,128)(2,1)S(1)}, u32[]{:S(2)}) copy-start(bf16[256,128]{1,0:T(8,128)(2,1)S(1)} %collective-permute-done.8.refs_5_) | copy-start | bytes 196612
  38.6 4.4 %copy-start.12 = (bf16[256,128]{1,0:T(8,128)(2,1)}, bf16[256,128]{1,0:T(8,128)(2,1)S(1)}, u32[]{:S(2)}) copy-start(bf16[256,128]{1,0:T(8,128)(2,1)S(1)} %collective-permute-done.9.refs_6_) | copy-start | bytes 196612
  38.6 4.4 %copy-start.1 = (bf16[1056,128]{1,0:T(8,128)(2,1)}, bf16[1056,128]{1,0:T(8,128)(2,1)S(1)}, u32[]{:S(2)}) copy-start(bf16[1056,128]{1,0:T(8,128)(2,1)S(1)} %collective-permute-done.4.refs_1_) | copy-start | bytes 811012
  42.9 0.7 copy-start.2
  42.9 0.8 %copy-start.3 = (bf16[1056,128]{1,0:T(8,128)(2,1)}, bf16[1056,128]{1,0:T(8,128)(2,1)S(1)}, u32[]{:S(2)}) copy-start(bf16[1056,128]{1,0:T(8,128)(2,1)S(1)} %collective-permute-done.6.refs_3_) | copy-start | bytes 811012
  48.1 14.0 %collective-permute-start.11 = (bf16[256,128]{1,0:T(8,128)(2,1)}, bf16[256,128]{1,0:T(8,128)(2,1)S(1)}, u32[]{:S(2)}, u32[]{:S(2)}) collective-permute-start(bf16[256,128]{1,0:T(8,128)(2,1)} %get-tuple-element.23), channel_id=1, source_target_pairs={{0,1},{1,0},{4,5},{5,4},{8,9},{9,8},{12,13},{13,12},{2,3},{3,2},{6... | collective-permute-start | bytes 196616 | tf_op jit(solution)/shard_map/ppermute | solution.py:413
  48.1 15.4 %collective-permute-start.12 = (bf16[256,128]{1,0:T(8,128)(2,1)}, bf16[256,128]{1,0:T(8,128)(2,1)S(1)}, u32[]{:S(2)}, u32[]{:S(2)}) collective-permute-start(bf16[256,128]{1,0:T(8,128)(2,1)} %get-tuple-element.22.refs_0_), channel_id=1, source_target_pairs={{0,4},{1,5},{4,0},{5,1},{8,12},{9,13},{12,8},{13,9},{2,6},{3,7},{6... | collective-permute-start | bytes 196616 | tf_op jit(solution)/shard_map/ppermute | solution.py:413
  53.3 4.4 %collective-permute-start.18 = (f32[16,1]{1,0:T(8,128)}, f32[16,1]{1,0:T(8,128)S(1)}, u32[]{:S(2)}, u32[]{:S(2)}) collective-permute-start(f32[16,1]{1,0:T(8,128)} %get-tuple-element.25.f0), channel_id=1, source_target_pairs={{0,4},{1,5},{4,0},{5,1},{8,12},{9,13},{12,8},{13,9},{2,6},{3,7},{6... | collective-permute-start | bytes 200 | tf_op jit(solution)/shard_map/ppermute | solution.py:413
  53.4 4.8 %collective-permute-start.19 = (f32[16,1]{1,0:T(8,128)}, f32[16,1]{1,0:T(8,128)S(1)}, u32[]{:S(2)}, u32[]{:S(2)}) collective-permute-start(f32[16,1]{1,0:T(8,128)} %get-tuple-element.25.f0), channel_id=1, source_target_pairs={{0,8},{1,9},{4,12},{5,13},{8,0},{9,1},{12,4},{13,5},{2,10},{3,11},... | collective-permute-start | bytes 200 | tf_op jit(solution)/shard_map/ppermute | solution.py:413
  56.3 5.7 %collective-permute-start.20 = (f32[16,1]{1,0:T(8,128)}, f32[16,1]{1,0:T(8,128)S(1)}, u32[]{:S(2)}, u32[]{:S(2)}) collective-permute-start(f32[16,1]{1,0:T(8,128)} %get-tuple-element.25.f0), channel_id=1, source_target_pairs={{0,12},{1,13},{4,8},{5,9},{8,4},{9,5},{12,0},{13,1},{2,14},{3,15},... | collective-permute-start | bytes 200 | tf_op jit(solution)/shard_map/ppermute | solution.py:413
  57.7 6.9 %copy-start.18 = (f32[16,1]{1,0:T(8,128)}, f32[16,1]{1,0:T(8,128)S(1)}, u32[]{:S(2)}) copy-start(f32[16,1]{1,0:T(8,128)S(1)} %collective-permute-done.18.f1) | copy-start | bytes 196
  57.7 8.2 %collective-permute-start.13 = (bf16[256,128]{1,0:T(8,128)(2,1)}, bf16[256,128]{1,0:T(8,128)(2,1)S(1)}, u32[]{:S(2)}, u32[]{:S(2)}) collective-permute-start(bf16[256,128]{1,0:T(8,128)(2,1)} %get-tuple-element.23), channel_id=1, source_target_pairs={{0,5},{1,4},{4,1},{5,0},{8,13},{9,12},{12,9},{13,8},{2,7},{3,6},{6... | collective-permute-start | bytes 196616 | tf_op jit(solution)/shard_map/ppermute | solution.py:413
  58.2 6.3 %copy-start.19 = (f32[16,1]{1,0:T(8,128)}, f32[16,1]{1,0:T(8,128)S(1)}, u32[]{:S(2)}) copy-start(f32[16,1]{1,0:T(8,128)S(1)} %collective-permute-done.19.f2) | copy-start | bytes 196
  58.2 9.1 %collective-permute-start.14 = (bf16[256,128]{1,0:T(8,128)(2,1)}, bf16[256,128]{1,0:T(8,128)(2,1)S(1)}, u32[]{:S(2)}, u32[]{:S(2)}) collective-permute-start(bf16[256,128]{1,0:T(8,128)(2,1)} %get-tuple-element.22.refs_0_), channel_id=1, source_target_pairs={{0,8},{1,9},{4,12},{5,13},{8,0},{9,1},{12,4},{13,5},{2,10},{3,11},... | collective-permute-start | bytes 196616 | tf_op jit(solution)/shard_map/ppermute | solution.py:413
  62.1 2.5 %copy-start.20 = (f32[16,1]{1,0:T(8,128)}, f32[16,1]{1,0:T(8,128)S(1)}, u32[]{:S(2)}) copy-start(f32[16,1]{1,0:T(8,128)S(1)} %collective-permute-done.20.f3) | copy-start | bytes 196
  62.1 8.4 %collective-permute-start.15 = (bf16[256,128]{1,0:T(8,128)(2,1)}, bf16[256,128]{1,0:T(8,128)(2,1)S(1)}, u32[]{:S(2)}, u32[]{:S(2)}) collective-permute-start(bf16[256,128]{1,0:T(8,128)(2,1)} %get-tuple-element.23), channel_id=1, source_target_pairs={{0,9},{1,8},{4,13},{5,12},{8,1},{9,0},{12,5},{13,4},{2,11},{3,10},... | collective-permute-start | bytes 196616 | tf_op jit(solution)/shard_map/ppermute | solution.py:413
  62.1 8.4 %copy-start.4 = (bf16[256,128]{1,0:T(8,128)(2,1)}, bf16[256,128]{1,0:T(8,128)(2,1)S(1)}, u32[]{:S(2)}) copy-start(bf16[256,128]{1,0:T(8,128)(2,1)S(1)} %collective-permute-done.11.refs_1_) | copy-start | bytes 196612
  62.1 8.4 %collective-permute-start.16 = (bf16[256,128]{1,0:T(8,128)(2,1)}, bf16[256,128]{1,0:T(8,128)(2,1)S(1)}, u32[]{:S(2)}, u32[]{:S(2)}) collective-permute-start(bf16[256,128]{1,0:T(8,128)(2,1)} %get-tuple-element.22.refs_0_), channel_id=1, source_target_pairs={{0,12},{1,13},{4,8},{5,9},{8,4},{9,5},{12,0},{13,1},{2,14},{3,15},... | collective-permute-start | bytes 196616 | tf_op jit(solution)/shard_map/ppermute | solution.py:413
  63.5 7.0 %copy-start.5 = (bf16[256,128]{1,0:T(8,128)(2,1)}, bf16[256,128]{1,0:T(8,128)(2,1)S(1)}, u32[]{:S(2)}) copy-start(bf16[256,128]{1,0:T(8,128)(2,1)S(1)} %collective-permute-done.12.refs_2_) | copy-start | bytes 196612
  63.5 7.0 %collective-permute-start.17 = (bf16[256,128]{1,0:T(8,128)(2,1)}, bf16[256,128]{1,0:T(8,128)(2,1)S(1)}, u32[]{:S(2)}, u32[]{:S(2)}) collective-permute-start(bf16[256,128]{1,0:T(8,128)(2,1)} %get-tuple-element.23), channel_id=1, source_target_pairs={{0,13},{1,12},{4,9},{5,8},{8,5},{9,4},{12,1},{13,0},{2,15},{3,14},... | collective-permute-start | bytes 196616 | tf_op jit(solution)/shard_map/ppermute | solution.py:413
  65.9 4.6 %copy-start.6 = (bf16[256,128]{1,0:T(8,128)(2,1)}, bf16[256,128]{1,0:T(8,128)(2,1)S(1)}, u32[]{:S(2)}) copy-start(bf16[256,128]{1,0:T(8,128)(2,1)S(1)} %collective-permute-done.13.refs_3_) | copy-start | bytes 196612
  67.3 3.3 %copy-start.7 = (bf16[256,128]{1,0:T(8,128)(2,1)}, bf16[256,128]{1,0:T(8,128)(2,1)S(1)}, u32[]{:S(2)}) copy-start(bf16[256,128]{1,0:T(8,128)(2,1)S(1)} %collective-permute-done.14.refs_4_) | copy-start | bytes 196612
  70.5 0.6 copy-start.8
  70.5 0.7 copy-start.11
  71.2 0.6 copy-start.13

commit v3 on v2

--- a/solution.py
+++ b/solution.py
@@ -27,6 +27,10 @@
 
 def in_any():
     return pl.BlockSpec(memory_space=pl.ANY)
+
+
+def on_chip(*values):
+    return [pltpu.with_memory_space_constraint(value, VMEM) for value in values]
 
 
 def mm(a, b):
@@ -71,7 +75,7 @@
     return (every_walker[copy_list], every_log[copy_list])
 
 
-def bias_kernel(aux_ref, log_ref, walkers_hbm, inv_hbm, trial_hbm, vec_hbm, out_ref,
+def bias_kernel(aux_ref, log_ref, copy_ref, walkers_hbm, inv_hbm, trial_hbm, vec_hbm, out_ref,
                 walkers_ref, inv_ref, trial_ref, vec_ref, green_ref, sems):
     n_walk = walkers_hbm.shape[0]
     n_vec = vec_hbm.shape[0]
@@ -88,6 +92,7 @@
     out_ref[...] = jnp.zeros_like(out_ref)
     out_ref[pl.ds(n_walk, n_walk), :] = aux_ref[...]
     out_ref[pl.ds(2 * n_walk, 1), :] = log_ref[...]
+    out_ref[pl.ds(2 * n_walk + 1, 1), :] = copy_ref[...].astype(jnp.float32)
     copies[0].wait()
     copies[1].wait()
     for w in range(n_walk):
@@ -105,12 +110,12 @@
     out_ref[pl.ds(0, n_walk), :] = total
 
 
-def partial_bias_of(aux, log_weight, walkers, inv, trial, vectors):
+def partial_bias_of(aux, log_weight, copy_list, walkers, inv, trial, vectors):
     n_walk, n_vec = aux.shape
     return pl.pallas_call(
         bias_kernel,
-        out_shape=jax.ShapeDtypeStruct((3 * n_walk, n_vec), jnp.float32),
-        in_specs=[in_vmem()] * 2 + [in_any()] * 4,
+        out_shape=VMEM((3 * n_walk, n_vec), jnp.float32),
+        in_specs=[in_vmem()] * 3 + [in_any()] * 4,
         out_specs=in_vmem(),
         scratch_shapes=[
             VMEM(walkers.shape, walkers.dtype),
@@ -121,13 +126,13 @@
             pltpu.SemaphoreType.DMA((3 + n_vec,)),
         ],
         name="bias",
-    )(aux, log_weight[None, :], walkers, inv, trial, vectors)
+    )(aux, log_weight[None, :], copy_list[None, :], walkers, inv, trial, vectors)
 
 
 def operator_kernel(n_z, n_o, group, copy_ref, own_ref, orb_ref, walk_ref, far_ref, here_hbm, mate_hbm,
-                    factor_ref, log_ref, *rest):
-    piece_refs = rest[:n_z]
-    vec_ref, field_ref, weight_ref, sems = rest[n_z:]
+                    walkers_hbm, log_ref, *rest):
+    piece_refs, source_refs = rest[:n_z], rest[n_z : n_z + 4]
+    vec_ref, field_ref, weight_ref, sems = rest[n_z + 4 :]
     n_walk = own_ref.shape[0] // 3
     n_vec = own_ref.shape[1]
     size = here_hbm.shape[2]
@@ -153,6 +158,21 @@
         def _():
             block_copy(b, mate_hbm).start()
 
+    slot, mate = z * n_o + o, z * n_o + (n_o - 1 - o)
+    far_lane = lax.broadcasted_iota(jnp.int32, (1, n_walk), 1)
+    far_list = walk_ref[pl.ds(2 * n_walk + 1, 1), :]
+
+    def far_copy(at):
+        return jnp.sum(jnp.where(far_lane == at, far_list, 0.0)).astype(jnp.int32)
+
+    wanted = (copy_ref[slot], copy_ref[mate], far_copy(slot), far_copy(mate))
+    source_copies = [
+        pltpu.make_async_copy(walkers_hbm.at[lax.rem(at, n_walk)], out, sems.at[n_block + i])
+        for i, (at, out) in enumerate(zip(wanted, source_refs))
+    ]
+    for copy in source_copies:
+        copy.start()
+
     bias = jnp.concatenate(
         [own_ref[pl.ds(0, n_walk), :] + orb_ref[pl.ds(0, n_walk), :],
          walk_ref[pl.ds(0, n_walk), :] + far_ref[pl.ds(0, n_walk), :]], axis=0
@@ -160,7 +180,7 @@
     aux = jnp.concatenate([own_ref[pl.ds(n_walk, n_walk), :], walk_ref[pl.ds(n_walk, n_walk), :]], axis=0)
     shift = -step_root * bias
     field_ref[...] = (aux - shift) * step_root
-    factor_ref[...] = jnp.sum(aux * shift - 0.5 * shift * shift, axis=1, keepdims=True)
+    factor = jnp.sum(aux * shift - 0.5 * shift * shift, axis=1, keepdims=True)
     for side, ref in enumerate((own_ref, walk_ref)):
         square = (n_walk, n_walk)
         eye = lax.broadcasted_iota(jnp.int32, square, 0) == lax.broadcasted_iota(jnp.int32, square, 1)
@@ -225,91 +245,61 @@
                 piece_refs[k][pl.ds(at + (i // 2) * 16, 16), :] = jnp.broadcast_to(
                     diagonal[k], (16, LANE)
                 ).astype(jnp.bfloat16)
-
-
-def piece_rows(size):
+    at += half * 16
+    lane = lax.broadcasted_iota(jnp.int32, (2 * n_walk, LANE), 1)
+    split = jnp.zeros(lane.shape, jnp.float32)
+    for i in range(3):
+        part = factor.astype(jnp.bfloat16).astype(jnp.float32)
+        split = jnp.where(lane == i, jnp.broadcast_to(part, lane.shape), split)
+        factor = factor - part
+    for k in range(n_z):
+        piece_refs[k][pl.ds(at, 2 * n_walk), :] = split.astype(jnp.bfloat16)
+    for copy in source_copies:
+        copy.wait()
+
+
+def piece_rows(size, n_both):
     n_block = size // LANE
-    return (n_block // 2 + n_block * (n_block - 1) // 2) * LANE + n_block // 2 * 16
-
-
-def partial_operators(copy_list, packs, vectors, mate_vectors, n_z, n_o):
+    return (n_block // 2 + n_block * (n_block - 1) // 2) * LANE + n_block // 2 * 16 + n_both
+
+
+def partial_operators(copy_list, packs, vectors, mate_vectors, walkers, n_z, n_o):
     n_walk, n_vec = packs[0].shape[0] // 3, packs[0].shape[1]
     size = vectors.shape[2]
     group = 2 * LANE // n_vec
-    piece = jax.ShapeDtypeStruct((piece_rows(size), LANE), jnp.bfloat16)
-    column = jax.ShapeDtypeStruct((2 * n_walk, 1), jnp.float32)
+    piece = VMEM((piece_rows(size, 2 * n_walk), LANE), jnp.bfloat16)
+    source = VMEM(walkers.shape[1:], walkers.dtype)
     return pl.pallas_call(
         partial(operator_kernel, n_z, n_o, group),
-        out_shape=[column, column] + [piece] * n_z,
-        in_specs=[in_smem()] + [in_vmem()] * 4 + [in_any()] * 2,
-        out_specs=[in_vmem()] * (2 + n_z),
+        out_shape=[VMEM((2 * n_walk, 1), jnp.float32)] + [piece] * n_z + [source] * 4,
+        in_specs=[in_smem()] + [in_vmem()] * 4 + [in_any()] * 3,
+        out_specs=[in_vmem()] * (1 + n_z + 4),
         scratch_shapes=[
             VMEM((n_vec, size, size), vectors.dtype),
             VMEM((2 * n_walk, n_vec), jnp.float32),
             VMEM((n_z, n_vec), jnp.float32),
-            pltpu.SemaphoreType.DMA((size // LANE,)),
+            pltpu.SemaphoreType.DMA((size // LANE + 4,)),
         ],
         name="operators",
-    )(copy_list, *packs, vectors, mate_vectors)
-
-
-def source_kernel(n_o, copy_ref, far_ref, walkers_hbm, own_out, orb_out, walk_out, diag_out, sems):
-    n_walk = walkers_hbm.shape[0]
-    z, o = lax.axis_index("vec"), lax.axis_index("orb")
-    slot, mate = z * n_o + o, z * n_o + (n_o - 1 - o)
-    wanted = [
-        (copy_ref, slot, own_out), (copy_ref, mate, orb_out), (far_ref, slot, walk_out), (far_ref, mate, diag_out)
-    ]
-    copies = [
-        pltpu.make_async_copy(walkers_hbm.at[lax.rem(ref[at], n_walk)], out, sems.at[i])
-        for i, (ref, at, out) in enumerate(wanted)
-    ]
-    for copy in copies:
-        copy.start()
-    for copy in copies:
-        copy.wait()
-
-
-def source_walkers(copy_list, far_copy, walkers, n_o):
-    out = jax.ShapeDtypeStruct(walkers.shape[1:], walkers.dtype)
-    return pl.pallas_call(
-        partial(source_kernel, n_o),
-        out_shape=[out] * 4,
-        in_specs=[in_smem()] * 2 + [in_any()],
-        out_specs=[in_vmem()] * 4,
-        scratch_shapes=[pltpu.SemaphoreType.DMA((4,))],
-        name="sources",
-    )(copy_list, far_copy, walkers)
-
-
-def weights_kernel(copy_ref, log_ref, f0, f1, f2, f3, out_ref):
-    n_both = log_ref.shape[0]
-    n_walk = n_both // 2
-    x = lax.axis_index("walk")
-    new_log = log_ref[...] + ((f0[...] + f1[...]) + (f2[...] + f3[...]))
-    source = copy_ref[...]
-    row = lax.rem(source, n_walk) + n_walk * (lax.div(source, n_walk) != x).astype(jnp.int32)
-    shape = (n_both, source.shape[1])
+    )(copy_list, *on_chip(*packs), vectors, mate_vectors, walkers)
+
+
+def log_weights(copy_row, log_column, parts, x):
+    n_walk = log_column.shape[0] // 2
+    while len(parts) > 1:
+        parts = [parts[i] + parts[i + 1] for i in range(0, len(parts), 2)]
+    new_log = log_column + parts[0]
+    row = lax.rem(copy_row, n_walk) + n_walk * (lax.div(copy_row, n_walk) != x).astype(jnp.int32)
+    shape = (2 * n_walk, copy_row.shape[1])
     at = lax.broadcasted_iota(jnp.int32, shape, 0)
-    out_ref[...] = jnp.sum(
-        jnp.where(at == jnp.broadcast_to(row, shape), jnp.broadcast_to(new_log, shape), 0.0),
-        axis=0, keepdims=True,
-    )
-
-
-def slot_weights(copy_list, log_column, factors):
-    return pl.pallas_call(
-        weights_kernel,
-        out_shape=jax.ShapeDtypeStruct((1,) + copy_list.shape, jnp.float32),
-        in_specs=[in_vmem()] * 6,
-        out_specs=in_vmem(),
-        name="weights",
-    )(copy_list[None, :], log_column, *factors)[0]
-
-
-def taylor_kernel(n_z, n_o, copy_ref, *refs):
+    chosen = jnp.where(at == jnp.broadcast_to(row, shape), jnp.broadcast_to(new_log, shape), 0.0)
+    return jnp.sum(chosen, axis=0, keepdims=True)
+
+
+def taylor_kernel(n_z, n_o, copy_ref, row_ref, log_ref, *refs):
     pieces = refs[:n_z]
-    own_ref, orb_ref, walk_ref, far_ref, mine_ref, other_ref, op_ref, term_ref, sum_ref = refs[n_z:]
+    (own_ref, orb_ref, walk_ref, far_ref, mine_ref, other_ref, weights_ref,
+     op_ref, term_ref, sum_ref) = refs[n_z:]
     z, x, o = lax.axis_index("vec"), lax.axis_index("walk"), lax.axis_index("orb")
     n_walk = copy_ref.shape[0]
     n_block = op_ref.shape[0] // LANE
@@ -339,6 +329,13 @@
         put(2 * pair, 2 * pair, jnp.where(i_at <= j_at, merged, turned))
         second = jnp.where(i_at > j_at, merged, turned)
         put(2 * pair + 1, 2 * pair + 1, jnp.where(i_at == j_at, diagonal, second))
+
+    at += n_block // 2 * 16
+    factors = [
+        jnp.sum(piece[pl.ds(at, 2 * n_walk), :].astype(jnp.float32), axis=1, keepdims=True)
+        for piece in pieces
+    ]
+    weights_ref[...] = log_weights(row_ref[...], log_ref[...], factors, x)
 
     here = lax.div(copy_ref[z * n_o + o], n_walk) == x
     rows = own_ref.shape[0]
@@ -357,22 +354,22 @@
     other_ref[...] = sum_ref[bottom, :].astype(jnp.bfloat16)
 
 
-def taylor(copy_list, pieces, candidates, n_o):
+def taylor(copy_list, log_column, pieces, candidates, n_o):
     rows, width = candidates[0].shape
     size = n_o * rows
-    out = jax.ShapeDtypeStruct((rows, width), jnp.bfloat16)
+    out = VMEM((rows, width), jnp.bfloat16)
     return pl.pallas_call(
         partial(taylor_kernel, len(pieces), n_o),
-        out_shape=[out, out],
-        in_specs=[in_smem()] + [in_vmem()] * (len(pieces) + 4),
-        out_specs=[in_vmem()] * 2,
+        out_shape=[out, out, jax.ShapeDtypeStruct((1,) + copy_list.shape, jnp.float32)],
+        in_specs=[in_smem()] + [in_vmem()] * (2 + len(pieces) + 4),
+        out_specs=[in_vmem()] * 3,
         scratch_shapes=[
             VMEM((size, size), jnp.bfloat16),
             VMEM((size, width), jnp.bfloat16),
             VMEM((size, width), jnp.float32),
         ],
         name="taylor",
-    )(copy_list, *pieces, *candidates)
+    )(copy_list, copy_list[None, :], *on_chip(log_column, *pieces, *candidates))
 
 
 def place_kernel(steps, n_o, *refs):
@@ -398,11 +395,11 @@
     return pl.pallas_call(
         partial(place_kernel, steps, n_o),
         out_shape=jax.ShapeDtypeStruct((n_line,) + pieces[0].shape, pieces[0].dtype),
-        in_specs=[in_any()] * n_line,
-        out_specs=in_vmem(),
+        in_specs=[in_vmem()] * n_line,
+        out_specs=in_any(),
         scratch_shapes=[pltpu.SemaphoreType.DMA((n_line,))],
         name="place",
-    )(*pieces)
+    )(*on_chip(*pieces))
 
 
 def swapped(value, axes, sizes, masks):
@@ -418,25 +415,20 @@
     near = partial(swapped, axes=("walk", "orb"), sizes=(n_x, n_o))
 
     mate_vectors = near(vectors, masks=(0, 1))
-    far_copy = near(copy_list, masks=(1, 0))
-    own_pack = partial_bias_of(aux_field, log_weight, walkers, inv_intersection, trial, vectors)
-    packs = [own_pack] + [near(own_pack, masks=m) for m in ((0, 1), (1, 0), (1, 1))]
-    wanted = source_walkers(copy_list, far_copy, walkers, n_o)
-    candidates = [wanted[0]] + [
-        near(value, masks=m) for value, m in zip(wanted[1:], ((0, 1), (1, 0), (1, 1)))
-    ]
-    factor, log_column, *pieces = partial_operators(copy_list, packs, vectors, mate_vectors, n_z, n_o)
+    own_pack = partial_bias_of(aux_field, log_weight, copy_list, walkers, inv_intersection, trial, vectors)
+    others = ((0, 1), (1, 0), (1, 1))
+    packs = [own_pack] + [near(own_pack, masks=m) for m in others]
+    log_column, *made = partial_operators(copy_list, packs, vectors, mate_vectors, walkers, n_z, n_o)
+    pieces, sources = made[:n_z], made[n_z:]
     arrived = [pieces[0]] + [line(pieces[k], masks=(k, 0)) for k in range(1, n_z)]
-    factors = [factor] + [line(factor, masks=(k, 0)) for k in range(1, n_z)]
-    weights_out = slot_weights(copy_list, log_column, factors)
-
-    mine, other = taylor(copy_list, arrived, candidates, n_o)
+    candidates = [sources[0]] + [near(value, masks=m) for value, m in zip(sources[1:], others)]
+    mine, other, weights_out = taylor(copy_list, log_column, arrived, candidates, n_o)
     steps = [(k, flip) for k in range(n_z) for flip in range(n_o)]
     landed = []
     for dz, flip in steps:
         half = mine if flip == 0 else other
         landed.append(half if (dz, flip) == (0, 0) else line(half, masks=(dz, flip)))
-    return put_in_place(steps, landed, n_o), weights_out
+    return put_in_place(steps, landed, n_o), weights_out[0]
 
 
 def suits(mesh, walkers, trial, vectors):

time: 74.1 us -> 60.5 us (0.82)
  Pallas kernels: 19.6 us -> 12.5 us
  starting transfers between devices: 25.3 us -> 19.4 us
  local copies, waits for them, and re-layouts: 4.5 us -> 0 us
  waiting for transfers between devices: 23.6 us -> 27.8 us
    ppermute x21 -> x17, starting transfers between devices: 25.3 us -> 19.4 us  [swapped(): return lax.ppermute(value, axes, perm)]
    pallas_call x4 -> x2, Pallas kernels: 13.3 us -> 7.97 us  [the longest x1 4.91 us: partial_bias_of(): pl.pallas_call(bias_kernel, out_shape=VMEM((3 * n_walk, n_vec), jnp.float...]
    unnamed x44 -> x0, local copies, waits for them, and re-layouts: 4.5 us -> none
    ppermute x21 -> x17, waiting for transfers between devices: 23.6 us -> 27.8 us  [swapped(): return lax.ppermute(value, axes, perm)]
    pallas_call x1, Pallas kernels: 1.92 us -> 0.85 us  [put_in_place(): pl.pallas_call(partial(place_kernel, steps, n_o), out_shape=jax.ShapeDtyp...]
  transfers between devices with their start and end apart: 21 -> 17, of which waited for: 10 -> 9; matrix products, arithmetic and copies ran while one was open for 0% -> 0% of each run, Pallas kernels for 13% -> 8%
where the time goes in v3:
time: 60.5 us; the launch traced here: 60.3 us
  waiting for transfers between devices  27.8 us (46%)
  starting transfers between devices  19.4 us (32%)
  Pallas kernels  12.5 us (21%)
  between operations  0.67 us (1%)
    ppermute x17, waiting for transfers between devices, swapped(): return lax.ppermute(value, axes, perm)  27.8 us
    ppermute x17, starting transfers between devices, swapped(): return lax.ppermute(value, axes, perm)  19.4 us
    pallas_call x1, Pallas kernels, partial_bias_of(): pl.pallas_call(bias_kernel, out_shape=VMEM((3 * n_walk, n_vec), jnp.float...  4.91 us
    pallas_call x1, Pallas kernels, taylor(): pl.pallas_call(partial(taylor_kernel, len(pieces), n_o), out_shape=[out,...  3.63 us
    pallas_call x1, Pallas kernels, partial_operators(): pl.pallas_call(partial(operator_kernel, n_z, n_o, group), out_shape=[VMEM...  3.06 us
  transfers between devices with their start and end apart: 17, of which 9 were waited for; matrix products, arithmetic and copies ran while one was open for 0% of the time, Pallas kernels for 8%

profile of v3, /device:TPU:0, one launch (start us, length us, event | category | flops | bytes accessed | tf_op | source)
XLA Modules:
  0.0 60.3 jit_solution(10830269981128174080)
XLA Ops:
  0.6 0.6 collective-permute-start.3
  1.2 4.9 %bias.1.own_ref = f32[24,8]{1,0:T(8,128)S(1)} custom-call(f32[8,8]{1,0:T(8,128)} %aux_ref.1, f32[1,8]{1,0:T(1,128)} %bitcast.5, s32[1,8]{1,0:T(1,128)} %bitcast.3, bf16[8,256,128]{2,1,0:T(8,128)(2,1)} %walkers_hbm.3, bf16[8,128,128]{2,1,0:T(8,128)(2,1)} %inv_hbm.1, bf16[512,128]{1,0:T(8,128)(2,1)} %trial_hbm.1, bf16[8,256,512]{2,1,0:T(8,128)(2,1)} %here_hbm.1), custom_call_target="tpu_custom_call" | custom-call | tf_op jit(solution)/shard_map/bias/pallas_call | solution.py:115
  6.1 2.7 %collective-permute-start.2 = (f32[24,8]{1,0:T(8,128)S(1)}, f32[24,8]{1,0:T(8,128)S(1)}, u32[]{:S(2)}, u32[]{:S(2)}) collective-permute-start(f32[24,8]{1,0:T(8,128)S(1)} %bias.1.own_ref), channel_id=1, source_target_pairs={{0,3},{1,2},{2,1},{3,0},{4,7},{5,6},{6,5},{7,4},{8,11},{9,10},{10,... | collective-permute-start | bytes 2312 | tf_op jit(solution)/shard_map/ppermute | solution.py:410
  8.8 0.0 collective-permute-start.1
  8.8 0.2 collective-permute-start
  9.0 1.2 %collective-permute-done.2.far_ref = f32[24,8]{1,0:T(8,128)S(1)} collective-permute-done((f32[24,8]{1,0:T(8,128)S(1)}, f32[24,8]{1,0:T(8,128)S(1)}, u32[]{:S(2)}, u32[]{:S(2)}) %collective-permute-start.2) | collective-permute-done | bytes 800 | tf_op jit(solution)/shard_map/ppermute | solution.py:410
  10.2 2.3 %collective-permute-done.1.walk_ref = f32[24,8]{1,0:T(8,128)S(1)} collective-permute-done((f32[24,8]{1,0:T(8,128)S(1)}, f32[24,8]{1,0:T(8,128)S(1)}, u32[]{:S(2)}, u32[]{:S(2)}) %collective-permute-start.1) | collective-permute-done | bytes 800 | tf_op jit(solution)/shard_map/ppermute | solution.py:410
  12.5 0.0 collective-permute-done.orb_ref
  12.5 0.0 collective-permute-done.3.mate_hbm
  12.5 3.1 %operators.1 = (f32[16,1]{1,0:T(8,128)S(1)}, bf16[1072,128]{1,0:T(8,128)(2,1)S(1)}, bf16[1072,128]{1,0:T(8,128)(2,1)S(1)}, bf16[1072,128]{1,0:T(8,128)(2,1)S(1)}...) custom-call(s32[8]{0:T(128)} %copy_ref.3, ...), custom_call_target="tpu_custom_call" | custom-call | tf_op jit(solution)/shard_map/operators/pallas_call | solution.py:272
  15.5 1.6 %collective-permute-start.4 = (bf16[1072,128]{1,0:T(8,128)(2,1)S(1)}, bf16[1072,128]{1,0:T(8,128)(2,1)S(1)}, u32[]{:S(2)}, u32[]{:S(2)}) collective-permute-start(bf16[1072,128]{1,0:T(8,128)(2,1)S(1)} %get-tuple-element.16), channel_id=1, source_target_pairs={{0,4},{1,5},{4,0},{5,1},{8,12},{9,13},{12,8},{13,9},{2,6},{3,7},{6... | collective-permute-start | bytes 823304 | tf_op jit(solution)/shard_map/ppermute | solution.py:410
  17.2 2.6 %collective-permute-start.5 = (bf16[1072,128]{1,0:T(8,128)(2,1)S(1)}, bf16[1072,128]{1,0:T(8,128)(2,1)S(1)}, u32[]{:S(2)}, u32[]{:S(2)}) collective-permute-start(bf16[1072,128]{1,0:T(8,128)(2,1)S(1)} %get-tuple-element.17), channel_id=1, source_target_pairs={{0,8},{1,9},{4,12},{5,13},{8,0},{9,1},{12,4},{13,5},{2,10},{3,11},... | collective-permute-start | bytes 823304 | tf_op jit(solution)/shard_map/ppermute | solution.py:410
  19.8 0.2 collective-permute-start.6
  20.0 0.0 collective-permute-start.7
  20.0 0.3 collective-permute-start.8
  20.3 0.9 %collective-permute-done.7.refs_5_ = bf16[256,128]{1,0:T(8,128)(2,1)S(1)} collective-permute-done((bf16[256,128]{1,0:T(8,128)(2,1)S(1)}, bf16[256,128]{1,0:T(8,128)(2,1)S(1)}, u32[]{:S(2)}, u32[]{:S(2)}) %collective-permute-start.7) | collective-permute-done | bytes 65568 | tf_op jit(solution)/shard_map/ppermute | solution.py:410
  21.2 0.6 %collective-permute-start.9 = (bf16[256,128]{1,0:T(8,128)(2,1)S(1)}, bf16[256,128]{1,0:T(8,128)(2,1)S(1)}, u32[]{:S(2)}, u32[]{:S(2)}) collective-permute-start(bf16[256,128]{1,0:T(8,128)(2,1)S(1)} %get-tuple-element.22), channel_id=1, source_target_pairs={{0,3},{1,2},{2,1},{3,0},{4,7},{5,6},{6,5},{7,4},{8,11},{9,10},{10,... | collective-permute-start | bytes 196616 | tf_op jit(solution)/shard_map/ppermute | solution.py:410
  21.8 2.9 %collective-permute-done.8.refs_6_ = bf16[256,128]{1,0:T(8,128)(2,1)S(1)} collective-permute-done((bf16[256,128]{1,0:T(8,128)(2,1)S(1)}, bf16[256,128]{1,0:T(8,128)(2,1)S(1)}, u32[]{:S(2)}, u32[]{:S(2)}) %collective-permute-start.8) | collective-permute-done | bytes 65568 | tf_op jit(solution)/shard_map/ppermute | solution.py:410
  24.8 0.9 %collective-permute-done.9.refs_7_ = bf16[256,128]{1,0:T(8,128)(2,1)S(1)} collective-permute-done((bf16[256,128]{1,0:T(8,128)(2,1)S(1)}, bf16[256,128]{1,0:T(8,128)(2,1)S(1)}, u32[]{:S(2)}, u32[]{:S(2)}) %collective-permute-start.9) | collective-permute-done | bytes 65568 | tf_op jit(solution)/shard_map/ppermute | solution.py:410
  25.6 2.0 %collective-permute-done.4.refs_1_ = bf16[1072,128]{1,0:T(8,128)(2,1)S(1)} collective-permute-done((bf16[1072,128]{1,0:T(8,128)(2,1)S(1)}, bf16[1072,128]{1,0:T(8,128)(2,1)S(1)}, u32[]{:S(2)}, u32[]{:S(2)}) %collective-permute-start.4) | collective-permute-done | bytes 274464 | tf_op jit(solution)/shard_map/ppermute | solution.py:410
  27.6 11.7 %collective-permute-done.5.refs_2_ = bf16[1072,128]{1,0:T(8,128)(2,1)S(1)} collective-permute-done((bf16[1072,128]{1,0:T(8,128)(2,1)S(1)}, bf16[1072,128]{1,0:T(8,128)(2,1)S(1)}, u32[]{:S(2)}, u32[]{:S(2)}) %collective-permute-start.5) | collective-permute-done | bytes 274464 | tf_op jit(solution)/shard_map/ppermute | solution.py:410
  39.3 0.0 collective-permute-done.6.refs_3_
  39.3 3.6 %taylor.1 = (bf16[256,128]{1,0:T(8,128)(2,1)S(1)}, bf16[256,128]{1,0:T(8,128)(2,1)S(1)}, f32[1,8]{1,0:T(1,128)}) custom-call(s32[8]{0:T(128)} %copy_ref.3, s32[1,8]{1,0:T(1,128)} %bitcast.4, f32[16,1]{1,0:T(8,128)S(1)} %get-tuple-element.14.log_ref, bf16[1072,128]{1,0:T(8,128)(2,1)S(1)} %get-tuple-element.15.refs_0_, ...), custom_call_target="tpu_custom_call" | custom-call | tf_op jit(solution)/shard_map/taylor/pallas_call | solution.py:361
  42.9 2.5 %collective-permute-start.15 = (bf16[256,128]{1,0:T(8,128)(2,1)S(1)}, bf16[256,128]{1,0:T(8,128)(2,1)S(1)}, u32[]{:S(2)}, u32[]{:S(2)}) collective-permute-start(bf16[256,128]{1,0:T(8,128)(2,1)S(1)} %get-tuple-element.23.refs_0_), channel_id=1, source_target_pairs={{0,12},{1,13},{4,8},{5,9},{8,4},{9,5},{12,0},{13,1},{2,14},{3,15},... | collective-permute-start | bytes 196616 | tf_op jit(solution)/shard_map/ppermute | solution.py:410
  45.4 3.4 %collective-permute-start.13 = (bf16[256,128]{1,0:T(8,128)(2,1)S(1)}, bf16[256,128]{1,0:T(8,128)(2,1)S(1)}, u32[]{:S(2)}, u32[]{:S(2)}) collective-permute-start(bf16[256,128]{1,0:T(8,128)(2,1)S(1)} %get-tuple-element.23.refs_0_), channel_id=1, source_target_pairs={{0,8},{1,9},{4,12},{5,13},{8,0},{9,1},{12,4},{13,5},{2,10},{3,11},... | collective-permute-start | bytes 196616 | tf_op jit(solution)/shard_map/ppermute | solution.py:410
  48.7 0.6 collective-permute-start.11
  49.3 0.0 collective-permute-start.16
  49.3 2.6 %collective-permute-start.14 = (bf16[256,128]{1,0:T(8,128)(2,1)S(1)}, bf16[256,128]{1,0:T(8,128)(2,1)S(1)}, u32[]{:S(2)}, u32[]{:S(2)}) collective-permute-start(bf16[256,128]{1,0:T(8,128)(2,1)S(1)} %get-tuple-element.24), channel_id=1, source_target_pairs={{0,9},{1,8},{4,13},{5,12},{8,1},{9,0},{12,5},{13,4},{2,11},{3,10},... | collective-permute-start | bytes 196616 | tf_op jit(solution)/shard_map/ppermute | solution.py:410
  52.0 0.0 collective-permute-done.15.refs_6_
  52.0 0.6 collective-permute-start.12
  52.5 0.0 collective-permute-done.13.refs_4_
  52.5 1.0 %collective-permute-start.10 = (bf16[256,128]{1,0:T(8,128)(2,1)S(1)}, bf16[256,128]{1,0:T(8,128)(2,1)S(1)}, u32[]{:S(2)}, u32[]{:S(2)}) collective-permute-start(bf16[256,128]{1,0:T(8,128)(2,1)S(1)} %get-tuple-element.24), channel_id=1, source_target_pairs={{0,1},{1,0},{4,5},{5,4},{8,9},{9,8},{12,13},{13,12},{2,3},{3,2},{6... | collective-permute-start | bytes 196616 | tf_op jit(solution)/shard_map/ppermute | solution.py:410
  53.5 0.0 collective-permute-done.11.refs_2_
  53.5 2.1 %collective-permute-done.16.refs_7_ = bf16[256,128]{1,0:T(8,128)(2,1)S(1)} collective-permute-done((bf16[256,128]{1,0:T(8,128)(2,1)S(1)}, bf16[256,128]{1,0:T(8,128)(2,1)S(1)}, u32[]{:S(2)}, u32[]{:S(2)}) %collective-permute-start.16) | collective-permute-done | bytes 65568 | tf_op jit(solution)/shard_map/ppermute | solution.py:410
  55.6 3.8 %collective-permute-done.14.refs_5_ = bf16[256,128]{1,0:T(8,128)(2,1)S(1)} collective-permute-done((bf16[256,128]{1,0:T(8,128)(2,1)S(1)}, bf16[256,128]{1,0:T(8,128)(2,1)S(1)}, u32[]{:S(2)}, u32[]{:S(2)}) %collective-permute-start.14) | collective-permute-done | bytes 65568 | tf_op jit(solution)/shard_map/ppermute | solution.py:410
  59.4 0.0 collective-permute-done.12.refs_3_
  59.4 0.0 collective-permute-done.10.refs_1_
  59.4 0.8 %place.1 = bf16[8,256,128]{2,1,0:T(8,128)(2,1)} custom-call(bf16[256,128]{1,0:T(8,128)(2,1)S(1)} %get-tuple-element.23.refs_0_, bf16[256,128]{1,0:T(8,128)(2,1)S(1)} %collective-permute-done.10.refs_1_, bf16[256,128]{1,0:T(8,128)(2,1)S(1)} %collective-permute-done.11.refs_2_, bf16[256,128]{1,0:T(8,128)(2,1)S(1)} %collective-permute-done.12.refs_3_, ...), custom_call_target="tpu_custom_call" | custom-call | tf_op jit(solution)/shard_map/place/pallas_call | solution.py:395
Async XLA Ops:
  0.6 11.8 %collective-permute-start.3 = (bf16[8,256,512]{2,1,0:T(8,128)(2,1)}, bf16[8,256,512]{2,1,0:T(8,128)(2,1)}, u32[]{:S(2)}, u32[]{:S(2)}) collective-permute-start(bf16[8,256,512]{2,1,0:T(8,128)(2,1)} %here_hbm.1), channel_id=1, source_target_pairs={{0,1},{1,0},{2,3},{3,2},{4,5},{5,4},{6,7},{7,6},{8,9},{9,8},{10,11... | collective-permute-start | bytes 6291464 | tf_op jit(solution)/shard_map/ppermute | solution.py:410
  6.1 4.1 %collective-permute-start.2 = (f32[24,8]{1,0:T(8,128)S(1)}, f32[24,8]{1,0:T(8,128)S(1)}, u32[]{:S(2)}, u32[]{:S(2)}) collective-permute-start(f32[24,8]{1,0:T(8,128)S(1)} %bias.1.own_ref), channel_id=1, source_target_pairs={{0,3},{1,2},{2,1},{3,0},{4,7},{5,6},{6,5},{7,4},{8,11},{9,10},{10,... | collective-permute-start | bytes 2312 | tf_op jit(solution)/shard_map/ppermute | solution.py:410
  8.8 3.7 %collective-permute-start.1 = (f32[24,8]{1,0:T(8,128)S(1)}, f32[24,8]{1,0:T(8,128)S(1)}, u32[]{:S(2)}, u32[]{:S(2)}) collective-permute-start(f32[24,8]{1,0:T(8,128)S(1)} %bias.1.own_ref), channel_id=1, source_target_pairs={{0,2},{1,3},{2,0},{3,1},{4,6},{5,7},{6,4},{7,5},{8,10},{9,11},{10,... | collective-permute-start | bytes 2312 | tf_op jit(solution)/shard_map/ppermute | solution.py:410
  8.8 3.7 %collective-permute-start = (f32[24,8]{1,0:T(8,128)S(1)}, f32[24,8]{1,0:T(8,128)S(1)}, u32[]{:S(2)}, u32[]{:S(2)}) collective-permute-start(f32[24,8]{1,0:T(8,128)S(1)} %bias.1.own_ref), channel_id=1, source_target_pairs={{0,1},{1,0},{2,3},{3,2},{4,5},{5,4},{6,7},{7,6},{8,9},{9,8},{10,11... | collective-permute-start | bytes 2312 | tf_op jit(solution)/shard_map/ppermute | solution.py:410
  15.5 12.1 %collective-permute-start.4 = (bf16[1072,128]{1,0:T(8,128)(2,1)S(1)}, bf16[1072,128]{1,0:T(8,128)(2,1)S(1)}, u32[]{:S(2)}, u32[]{:S(2)}) collective-permute-start(bf16[1072,128]{1,0:T(8,128)(2,1)S(1)} %get-tuple-element.16), channel_id=1, source_target_pairs={{0,4},{1,5},{4,0},{5,1},{8,12},{9,13},{12,8},{13,9},{2,6},{3,7},{6... | collective-permute-start | bytes 823304 | tf_op jit(solution)/shard_map/ppermute | solution.py:410
  17.2 22.1 %collective-permute-start.5 = (bf16[1072,128]{1,0:T(8,128)(2,1)S(1)}, bf16[1072,128]{1,0:T(8,128)(2,1)S(1)}, u32[]{:S(2)}, u32[]{:S(2)}) collective-permute-start(bf16[1072,128]{1,0:T(8,128)(2,1)S(1)} %get-tuple-element.17), channel_id=1, source_target_pairs={{0,8},{1,9},{4,12},{5,13},{8,0},{9,1},{12,4},{13,5},{2,10},{3,11},... | collective-permute-start | bytes 823304 | tf_op jit(solution)/shard_map/ppermute | solution.py:410
  19.8 19.5 %collective-permute-start.6 = (bf16[1072,128]{1,0:T(8,128)(2,1)S(1)}, bf16[1072,128]{1,0:T(8,128)(2,1)S(1)}, u32[]{:S(2)}, u32[]{:S(2)}) collective-permute-start(bf16[1072,128]{1,0:T(8,128)(2,1)S(1)} %get-tuple-element.18), channel_id=1, source_target_pairs={{0,12},{1,13},{4,8},{5,9},{8,4},{9,5},{12,0},{13,1},{2,14},{3,15},... | collective-permute-start | bytes 823304 | tf_op jit(solution)/shard_map/ppermute | solution.py:410
  20.0 1.3 %collective-permute-start.7 = (bf16[256,128]{1,0:T(8,128)(2,1)S(1)}, bf16[256,128]{1,0:T(8,128)(2,1)S(1)}, u32[]{:S(2)}, u32[]{:S(2)}) collective-permute-start(bf16[256,128]{1,0:T(8,128)(2,1)S(1)} %get-tuple-element.20), channel_id=1, source_target_pairs={{0,1},{1,0},{2,3},{3,2},{4,5},{5,4},{6,7},{7,6},{8,9},{9,8},{10,11... | collective-permute-start | bytes 196616 | tf_op jit(solution)/shard_map/ppermute | solution.py:410
  20.0 4.8 %collective-permute-start.8 = (bf16[256,128]{1,0:T(8,128)(2,1)S(1)}, bf16[256,128]{1,0:T(8,128)(2,1)S(1)}, u32[]{:S(2)}, u32[]{:S(2)}) collective-permute-start(bf16[256,128]{1,0:T(8,128)(2,1)S(1)} %get-tuple-element.21), channel_id=1, source_target_pairs={{0,2},{1,3},{2,0},{3,1},{4,6},{5,7},{6,4},{7,5},{8,10},{9,11},{10,... | collective-permute-start | bytes 196616 | tf_op jit(solution)/shard_map/ppermute | solution.py:410
  21.2 4.4 %collective-permute-start.9 = (bf16[256,128]{1,0:T(8,128)(2,1)S(1)}, bf16[256,128]{1,0:T(8,128)(2,1)S(1)}, u32[]{:S(2)}, u32[]{:S(2)}) collective-permute-start(bf16[256,128]{1,0:T(8,128)(2,1)S(1)} %get-tuple-element.22), channel_id=1, source_target_pairs={{0,3},{1,2},{2,1},{3,0},{4,7},{5,6},{6,5},{7,4},{8,11},{9,10},{10,... | collective-permute-start | bytes 196616 | tf_op jit(solution)/shard_map/ppermute | solution.py:410
  42.9 9.0 %collective-permute-start.15 = (bf16[256,128]{1,0:T(8,128)(2,1)S(1)}, bf16[256,128]{1,0:T(8,128)(2,1)S(1)}, u32[]{:S(2)}, u32[]{:S(2)}) collective-permute-start(bf16[256,128]{1,0:T(8,128)(2,1)S(1)} %get-tuple-element.23.refs_0_), channel_id=1, source_target_pairs={{0,12},{1,13},{4,8},{5,9},{8,4},{9,5},{12,0},{13,1},{2,14},{3,15},... | collective-permute-start | bytes 196616 | tf_op jit(solution)/shard_map/ppermute | solution.py:410
  45.4 7.1 %collective-permute-start.13 = (bf16[256,128]{1,0:T(8,128)(2,1)S(1)}, bf16[256,128]{1,0:T(8,128)(2,1)S(1)}, u32[]{:S(2)}, u32[]{:S(2)}) collective-permute-start(bf16[256,128]{1,0:T(8,128)(2,1)S(1)} %get-tuple-element.23.refs_0_), channel_id=1, source_target_pairs={{0,8},{1,9},{4,12},{5,13},{8,0},{9,1},{12,4},{13,5},{2,10},{3,11},... | collective-permute-start | bytes 196616 | tf_op jit(solution)/shard_map/ppermute | solution.py:410
  48.7 4.8 %collective-permute-start.11 = (bf16[256,128]{1,0:T(8,128)(2,1)S(1)}, bf16[256,128]{1,0:T(8,128)(2,1)S(1)}, u32[]{:S(2)}, u32[]{:S(2)}) collective-permute-start(bf16[256,128]{1,0:T(8,128)(2,1)S(1)} %get-tuple-element.23.refs_0_), channel_id=1, source_target_pairs={{0,4},{1,5},{4,0},{5,1},{8,12},{9,13},{12,8},{13,9},{2,6},{3,7},{6... | collective-permute-start | bytes 196616 | tf_op jit(solution)/shard_map/ppermute | solution.py:410
  49.3 6.3 %collective-permute-start.16 = (bf16[256,128]{1,0:T(8,128)(2,1)S(1)}, bf16[256,128]{1,0:T(8,128)(2,1)S(1)}, u32[]{:S(2)}, u32[]{:S(2)}) collective-permute-start(bf16[256,128]{1,0:T(8,128)(2,1)S(1)} %get-tuple-element.24), channel_id=1, source_target_pairs={{0,13},{1,12},{4,9},{5,8},{8,5},{9,4},{12,1},{13,0},{2,15},{3,14},... | collective-permute-start | bytes 196616 | tf_op jit(solution)/shard_map/ppermute | solution.py:410
  49.3 10.1 %collective-permute-start.14 = (bf16[256,128]{1,0:T(8,128)(2,1)S(1)}, bf16[256,128]{1,0:T(8,128)(2,1)S(1)}, u32[]{:S(2)}, u32[]{:S(2)}) collective-permute-start(bf16[256,128]{1,0:T(8,128)(2,1)S(1)} %get-tuple-element.24), channel_id=1, source_target_pairs={{0,9},{1,8},{4,13},{5,12},{8,1},{9,0},{12,5},{13,4},{2,11},{3,10},... | collective-permute-start | bytes 196616 | tf_op jit(solution)/shard_map/ppermute | solution.py:410
  52.0 7.5 %collective-permute-start.12 = (bf16[256,128]{1,0:T(8,128)(2,1)S(1)}, bf16[256,128]{1,0:T(8,128)(2,1)S(1)}, u32[]{:S(2)}, u32[]{:S(2)}) collective-permute-start(bf16[256,128]{1,0:T(8,128)(2,1)S(1)} %get-tuple-element.24), channel_id=1, source_target_pairs={{0,5},{1,4},{4,1},{5,0},{8,13},{9,12},{12,9},{13,8},{2,7},{3,6},{6... | collective-permute-start | bytes 196616 | tf_op jit(solution)/shard_map/ppermute | solution.py:410
  52.5 6.9 %collective-permute-start.10 = (bf16[256,128]{1,0:T(8,128)(2,1)S(1)}, bf16[256,128]{1,0:T(8,128)(2,1)S(1)}, u32[]{:S(2)}, u32[]{:S(2)}) collective-permute-start(bf16[256,128]{1,0:T(8,128)(2,1)S(1)} %get-tuple-element.24), channel_id=1, source_target_pairs={{0,1},{1,0},{4,5},{5,4},{8,9},{9,8},{12,13},{13,12},{2,3},{3,2},{6... | collective-permute-start | bytes 196616 | tf_op jit(solution)/shard_map/ppermute | solution.py:410

commit v4 on v0

--- a/solution.py
+++ b/solution.py
@@ -4,19 +4,45 @@
 import jax
 import jax.numpy as jnp
 from jax import lax
+from jax.experimental import pallas as pl
+from jax.experimental.pallas import tpu as pltpu
 from jax.sharding import PartitionSpec as P
 
+
 ORDER = 6
-
+LANE = 128
+VMEM_LIMIT = 24 * 1024 * 1024
 
 step_root = math.sqrt(0.08)
+
+VMEM = pltpu.VMEM
+
+
+def in_vmem():
+    return pl.BlockSpec(memory_space=VMEM)
+
+
+def in_hbm():
+    return pl.BlockSpec(memory_space=pltpu.HBM)
+
+
+def on_chip(*values):
+    return [pltpu.with_memory_space_constraint(value, VMEM) for value in values]
+
+
+def in_place(*values):
+    return [pltpu.with_memory_space_constraint(value, pltpu.HBM) for value in values]
+
+
+def mm(a, b):
+    return jnp.dot(a, b, preferred_element_type=jnp.float32)
 
 
 def fold_rows(operator, carry, piece, start):
     return jnp.einsum("wnm,wme->wne", operator, piece, preferred_element_type=jnp.float32)
 
 
-def per_device(walkers, inv_intersection, trial, vectors, aux_field, log_weight, copy_list):
+def general_device(walkers, inv_intersection, trial, vectors, aux_field, log_weight, copy_list):
     green = jnp.einsum(
         "wne,wef->wnf", walkers, inv_intersection, preferred_element_type=jnp.float32
     ).astype(jnp.bfloat16)
@@ -50,19 +76,486 @@
     return (every_walker[copy_list], every_log[copy_list])
 
 
+def bias_kernel(aux_hbm, log_hbm, copy_hbm, walkers_hbm, inv_hbm, trial_hbm, vec_hbm, out_ref, vec_ref,
+                aux_ref, log_ref, copy_ref, walkers_ref, inv_ref, trial_ref, green_ref, sems):
+    n_walk = walkers_hbm.shape[0]
+    n_vec = vec_hbm.shape[0]
+    copies = [
+        pltpu.make_async_copy(source, target, sems.at[i])
+        for i, (source, target) in enumerate((
+            (walkers_hbm, walkers_ref), (inv_hbm, inv_ref), (trial_hbm, trial_ref),
+            (aux_hbm, aux_ref), (log_hbm, log_ref), (copy_hbm, copy_ref),
+        ))
+    ]
+    vec_copies = [
+        pltpu.make_async_copy(vec_hbm.at[g], vec_ref.at[g], sems.at[len(copies) + g]) for g in range(n_vec)
+    ]
+    for copy in copies[:3] + vec_copies + copies[3:]:
+        copy.start()
+    copies[0].wait()
+    copies[1].wait()
+    for w in range(n_walk):
+        green_ref[w] = mm(walkers_ref[w], inv_ref[w]).astype(jnp.bfloat16).astype(jnp.float32)
+    copies[2].wait()
+    trial = trial_ref[...]
+    lane = lax.broadcasted_iota(jnp.int32, (n_walk, n_vec), 1)
+    total = jnp.zeros((n_walk, n_vec), jnp.float32)
+    for g in range(n_vec):
+        vec_copies[g].wait()
+        mixed = mm(vec_ref[g], trial).astype(jnp.bfloat16).astype(jnp.float32)
+        rows = [jnp.sum(green_ref[w] * mixed, axis=0, keepdims=True) for w in range(n_walk)]
+        column = jnp.sum(jnp.concatenate(rows, axis=0), axis=1, keepdims=True)
+        total = total + jnp.where(lane == g, column, 0.0)
+    for copy in copies[3:]:
+        copy.wait()
+    out_ref[pl.ds(0, n_walk), :] = total
+    out_ref[pl.ds(n_walk, n_walk), :] = aux_ref[...]
+    out_ref[pl.ds(2 * n_walk, n_walk), :] = jnp.zeros((n_walk, n_vec), jnp.float32)
+    out_ref[pl.ds(2 * n_walk, 1), :] = log_ref[...]
+    out_ref[pl.ds(2 * n_walk + 1, 1), :] = copy_ref[...].astype(jnp.float32)
+
+
+def partial_bias_of(aux, log_weight, copy_list, walkers, inv, trial, vectors):
+    n_walk, n_vec = aux.shape
+    log_row, copy_row = log_weight[None, :], copy_list[None, :]
+    return pl.pallas_call(
+        bias_kernel,
+        out_shape=[VMEM((3 * n_walk, n_vec), jnp.float32), VMEM(vectors.shape, vectors.dtype)],
+        in_specs=[in_hbm()] * 7,
+        out_specs=[in_vmem()] * 2,
+        scratch_shapes=[
+            VMEM(aux.shape, aux.dtype),
+            VMEM(log_row.shape, log_row.dtype),
+            VMEM(copy_row.shape, copy_row.dtype),
+            VMEM(walkers.shape, walkers.dtype),
+            VMEM(inv.shape, inv.dtype),
+            VMEM(trial.shape, trial.dtype),
+            VMEM(walkers.shape, jnp.float32),
+            pltpu.SemaphoreType.DMA((6 + n_vec,)),
+        ],
+        compiler_params=pltpu.CompilerParams(vmem_limit_bytes=VMEM_LIMIT),
+        name="bias",
+    )(*in_place(aux, log_row, copy_row, walkers, inv, trial, vectors))
+
+
+def copies_of(pack_ref):
+    n_walk = pack_ref.shape[0] // 3
+    return pack_ref[pl.ds(2 * n_walk + 1, 1), :]
+
+
+def entry(row, at):
+    lane = lax.broadcasted_iota(jnp.int32, row.shape, 1)
+    return jnp.sum(jnp.where(lane == at, row, 0.0)).astype(jnp.int32)
+
+
+def layout(n_block):
+    at = n_block // 2 * LANE
+    offsets = {}
+    for i in range(n_block):
+        for j in range(i + 1, n_block):
+            offsets[(i, j)] = at
+            at += LANE
+    return offsets, at
+
+
+def piece_rows(size, n_both):
+    n_block = size // LANE
+    return layout(n_block)[1] + n_block // 2 * 16 + n_both
+
+
+def fill_pieces(weights, here_ref, mate_ref, piece_refs, split, o):
+    n_vec, n_rows, size = here_ref.shape
+    n_block = size // LANE
+    in_half = n_rows // LANE
+    offsets, at = layout(n_block)
+    count = len(piece_refs)
+    tall = LANE // 2
+    splats = [
+        [jnp.broadcast_to(weights[k : k + 1, g : g + 1], (tall, LANE)) for g in range(n_vec)]
+        for k in range(count)
+    ]
+
+    def sums(i, j, step):
+        source = here_ref if i < in_half else mate_ref
+        rows = pl.ds(i % in_half * LANE + step * tall, tall)
+        column = lax.rem(j + o * in_half, n_block) * LANE
+        columns = pl.ds(pl.multiple_of(column, LANE), LANE)
+        result = [None] * count
+        for g in range(n_vec):
+            value = source[g, rows, columns].astype(jnp.float32)
+            for k in range(count):
+                part = splats[k][g] * value
+                result[k] = part if g == 0 else result[k] + part
+        return result
+
+    line = lax.broadcasted_iota(jnp.int32, (tall, LANE), 0)
+    lane = lax.broadcasted_iota(jnp.int32, (tall, LANE), 1)
+    for step in range(LANE // tall):
+        row_at = line + step * tall
+        for (i, j), offset in offsets.items():
+            for k, value in enumerate(sums(i, j, step)):
+                piece_refs[k][pl.ds(offset + step * tall, tall), :] = value.astype(jnp.bfloat16)
+        for pair in range(n_block // 2):
+            upper = sums(2 * pair, 2 * pair, step)
+            lower = sums(2 * pair + 1, 2 * pair + 1, step)
+            for k in range(count):
+                merged = jnp.where(row_at <= lane, upper[k], lower[k])
+                piece_refs[k][pl.ds(pair * LANE + step * tall, tall), :] = merged.astype(jnp.bfloat16)
+                found = jnp.sum(jnp.where(row_at == lane, lower[k], 0.0), axis=0, keepdims=True)
+                spot = pl.ds(at + pair * 16, 16)
+                row = jnp.broadcast_to(found, (16, LANE)).astype(jnp.bfloat16)
+                if step == 0:
+                    piece_refs[k][spot, :] = row
+                else:
+                    held = piece_refs[k][spot, :]
+                    seen = lax.broadcasted_iota(jnp.int32, (16, LANE), 1) < step * tall
+                    piece_refs[k][spot, :] = jnp.where(seen, held, row)
+    at += n_block // 2 * 16
+    for k in range(count):
+        piece_refs[k][pl.ds(at, split.shape[0]), :] = split
+
+
+def split_column(column):
+    lane = lax.broadcasted_iota(jnp.int32, (column.shape[0], LANE), 1)
+    split = jnp.zeros(lane.shape, jnp.float32)
+    for i in range(3):
+        part = column.astype(jnp.bfloat16).astype(jnp.float32)
+        split = jnp.where(lane == i, jnp.broadcast_to(part, lane.shape), split)
+        column = column - part
+    return split.astype(jnp.bfloat16)
+
+
+def joined(split):
+    wide = split.astype(jnp.float32)
+    return (wide[:, 0:1] + wide[:, 1:2]) + wide[:, 2:3]
+
+
+def routes(z):
+    inner = jnp.logical_or(z == 1, z == 2)
+    first = jnp.where(lax.rem(z, 2) == 0, 3, 0)
+    crossing = jnp.where(z == 0, 2, jnp.where(z == 3, 1, jnp.where(z == 1, 3, 0)))
+    nearby = jnp.where(lax.rem(z, 2) == 0, 1, 2)
+    return inner, first, crossing, nearby
+
+
+def first_kernel(n_o, own_ref, orb_ref, walk_ref, far_ref, here_ref, mate_ref,
+                 piece_ref, weight_ref, split_ref, log_ref):
+    n_walk = own_ref.shape[0] // 3
+    z, x, o = lax.axis_index("vec"), lax.axis_index("walk"), lax.axis_index("orb")
+    bias = jnp.concatenate(
+        [own_ref[pl.ds(0, n_walk), :] + orb_ref[pl.ds(0, n_walk), :],
+         walk_ref[pl.ds(0, n_walk), :] + far_ref[pl.ds(0, n_walk), :]], axis=0
+    )
+    aux = jnp.concatenate([own_ref[pl.ds(n_walk, n_walk), :], walk_ref[pl.ds(n_walk, n_walk), :]], axis=0)
+    shift = -step_root * bias
+    weighted = ((aux - shift) * step_root).astype(jnp.bfloat16)
+    split = split_column(jnp.sum(aux * shift - 0.5 * shift * shift, axis=1, keepdims=True))
+    split_ref[...] = split
+    _, first, crossing, nearby = routes(z)
+    k_at = lax.broadcasted_iota(jnp.int32, (8, n_walk), 0)
+    lane = lax.broadcasted_iota(jnp.int32, (8, n_walk), 1)
+    to_z = jnp.where(k_at == 0, first, jnp.where(k_at == 1, crossing, jnp.where(k_at == 2, nearby, z)))
+    sources = jnp.sum(
+        jnp.where(lane == to_z * n_o + o, jnp.broadcast_to(copies_of(own_ref), lane.shape), 0.0),
+        axis=1, keepdims=True,
+    ).astype(jnp.int32)
+    row = lax.rem(sources, n_walk) + n_walk * (lax.div(sources, n_walk) != x).astype(jnp.int32)
+    pick = lax.broadcasted_iota(jnp.int32, (8, 2 * n_walk), 1) == row
+    weights = mm(pick.astype(jnp.float32).astype(jnp.bfloat16), weighted)
+    weight_ref[...] = weights
+    fill_pieces(weights, here_ref, mate_ref, [piece_ref], split, o)
+    square = (n_walk, n_walk)
+    eye = lax.broadcasted_iota(jnp.int32, square, 0) == lax.broadcasted_iota(jnp.int32, square, 1)
+    for side, ref in enumerate((own_ref, walk_ref)):
+        log_ref[pl.ds(side * n_walk, n_walk), :] = jnp.sum(
+            jnp.where(eye, ref[pl.ds(2 * n_walk, 1), :], 0.0), axis=1, keepdims=True
+        )
+
+
+def first_piece(packs, here, mate, n_o):
+    n_walk, n_vec = packs[0].shape[0] // 3, packs[0].shape[1]
+    return pl.pallas_call(
+        partial(first_kernel, n_o),
+        out_shape=[
+            VMEM((piece_rows(here.shape[2], 2 * n_walk), LANE), jnp.bfloat16),
+            VMEM((8, n_vec), jnp.float32),
+            VMEM((2 * n_walk, LANE), jnp.bfloat16),
+            VMEM((2 * n_walk, 1), jnp.float32),
+        ],
+        in_specs=[in_vmem()] * 6,
+        out_specs=[in_vmem()] * 4,
+        compiler_params=pltpu.CompilerParams(vmem_limit_bytes=VMEM_LIMIT),
+        name="first_piece",
+    )(*on_chip(*packs, here, mate))
+
+
+def other_kernel(n_o, own_ref, walk_ref, weight_ref, split_ref, here_ref, mate_ref, walkers_hbm, *refs):
+    pieces, sources, sems = refs[:3], refs[3:7], refs[7]
+    n_walk = walkers_hbm.shape[0]
+    z, o = lax.axis_index("vec"), lax.axis_index("orb")
+    slot, mate = z * n_o + o, z * n_o + (n_o - 1 - o)
+    own_list, far_list = copies_of(own_ref), copies_of(walk_ref)
+    wanted = ((own_list, slot), (own_list, mate), (far_list, slot), (far_list, mate))
+    copies = [
+        pltpu.make_async_copy(walkers_hbm.at[lax.rem(entry(row, at), n_walk)], out, sems.at[i])
+        for i, ((row, at), out) in enumerate(zip(wanted, sources))
+    ]
+    for copy in copies:
+        copy.start()
+    fill_pieces(weight_ref[...][1:4], here_ref, mate_ref, pieces, split_ref[...], o)
+    for copy in copies:
+        copy.wait()
+
+
+def other_pieces(own_pack, walk_pack, weights, split, here, mate, walkers, n_o):
+    piece = VMEM((piece_rows(here.shape[2], split.shape[0]), LANE), jnp.bfloat16)
+    source = VMEM(walkers.shape[1:], walkers.dtype)
+    return pl.pallas_call(
+        partial(other_kernel, n_o),
+        out_shape=[piece] * 3 + [source] * 4,
+        in_specs=[in_vmem()] * 6 + [in_hbm()],
+        out_specs=[in_vmem()] * 7,
+        scratch_shapes=[pltpu.SemaphoreType.DMA((4,))],
+        compiler_params=pltpu.CompilerParams(vmem_limit_bytes=VMEM_LIMIT),
+        name="other_pieces",
+    )(*on_chip(own_pack, walk_pack, weights, split, here, mate), *in_place(walkers))
+
+
+def combine_kernel(n_both, mine_ref, came_ref, out_ref):
+    inner = routes(lax.axis_index("vec"))[0]
+    body = mine_ref.shape[0] - n_both
+
+    @pl.when(inner)
+    def _():
+        for low in range(0, body, LANE):
+            rows = pl.ds(low, min(LANE, body - low))
+            value = mine_ref[rows, :].astype(jnp.float32) + came_ref[rows, :].astype(jnp.float32)
+            out_ref[rows, :] = value.astype(jnp.bfloat16)
+        tail = pl.ds(body, n_both)
+        out_ref[tail, :] = split_column(joined(mine_ref[tail, :]) + joined(came_ref[tail, :]))
+
+    @pl.when(jnp.logical_not(inner))
+    def _():
+        out_ref[...] = mine_ref[...]
+
+
+def combined(mine, came, n_both):
+    return pl.pallas_call(
+        partial(combine_kernel, n_both),
+        out_shape=VMEM(mine.shape, mine.dtype),
+        in_specs=[in_vmem()] * 2,
+        out_specs=in_vmem(),
+        compiler_params=pltpu.CompilerParams(vmem_limit_bytes=VMEM_LIMIT),
+        name="combine",
+    )(*on_chip(mine, came))
+
+
+def log_weights(copy_row, log_column, total, x):
+    n_walk = log_column.shape[0] // 2
+    new_log = log_column + total
+    source = copy_row.astype(jnp.int32)
+    row = lax.rem(source, n_walk) + n_walk * (lax.div(source, n_walk) != x).astype(jnp.int32)
+    shape = (2 * n_walk, copy_row.shape[1])
+    at = lax.broadcasted_iota(jnp.int32, shape, 0)
+    chosen = jnp.where(at == jnp.broadcast_to(row, shape), jnp.broadcast_to(new_log, shape), 0.0)
+    return jnp.sum(chosen, axis=0, keepdims=True)
+
+
+def taylor_kernel(n_o, pack_ref, log_ref, kept_ref, first_ref, cross_ref, inside_ref, inward_ref,
+                  own_ref, orb_ref, walk_ref, far_ref, mine_ref, other_ref, weights_ref,
+                  op_ref, term_ref, sum_ref):
+    z, x, o = lax.axis_index("vec"), lax.axis_index("walk"), lax.axis_index("orb")
+    inner = routes(z)[0]
+    n_both = log_ref.shape[0]
+    n_walk = n_both // 2
+    n_block = op_ref.shape[0] // LANE
+    offsets, at = layout(n_block)
+    i_at = lax.broadcasted_iota(jnp.int32, (LANE, LANE), 0)
+    j_at = lax.broadcasted_iota(jnp.int32, (LANE, LANE), 1)
+
+    def total(start, count):
+        rows = pl.ds(start, count)
+        first, cross, inside, inward, kept = (
+            ref[rows, :].astype(jnp.float32)
+            for ref in (first_ref, cross_ref, inside_ref, inward_ref, kept_ref)
+        )
+        return (kept + cross) + jnp.where(inner, inside + inward, first)
+
+    def put(i, j, value):
+        op_ref[pl.ds(i * LANE, LANE), pl.ds(j * LANE, LANE)] = value.astype(jnp.bfloat16)
+
+    for (i, j), offset in offsets.items():
+        value = total(offset, LANE)
+        put(i, j, value)
+        put(j, i, value.T)
+    for pair in range(n_block // 2):
+        merged = total(pair * LANE, LANE)
+        diagonal = total(at + pair * 16, 16)[:1]
+        turned = merged.T
+        put(2 * pair, 2 * pair, jnp.where(i_at <= j_at, merged, turned))
+        second = jnp.where(i_at > j_at, merged, turned)
+        put(2 * pair + 1, 2 * pair + 1, jnp.where(i_at == j_at, diagonal, second))
+    at += n_block // 2 * 16
+
+    copy_row = copies_of(pack_ref)
+    here = lax.div(entry(copy_row, z * n_o + o), n_walk) == x
+    rows = own_ref.shape[0]
+    top, bottom = pl.ds(0, rows), pl.ds(rows, rows)
+    term_ref[top, :] = jnp.where(here, own_ref[...], walk_ref[...])
+    term_ref[bottom, :] = jnp.where(here, orb_ref[...], far_ref[...])
+    sum_ref[...] = term_ref[...].astype(jnp.float32)
+    for degree in range(1, ORDER + 1):
+        product = mm(op_ref[...], term_ref[...])
+        term = (product / degree).astype(jnp.bfloat16)
+        sum_ref[...] += term.astype(jnp.float32)
+        if degree < ORDER:
+            term_ref[...] = term
+    mine_ref[...] = sum_ref[top, :].astype(jnp.bfloat16)
+    other_ref[...] = sum_ref[bottom, :].astype(jnp.bfloat16)
+
+    tail = pl.ds(at, n_both)
+    first, cross, inside, inward, kept = (
+        joined(ref[tail, :]) for ref in (first_ref, cross_ref, inside_ref, inward_ref, kept_ref)
+    )
+    factor = (kept + jnp.where(inner, inward, first)) + jnp.where(inner, inside + cross, cross)
+    weights_ref[...] = log_weights(copy_row, log_ref[...], factor, x)
+
+
+def taylor(pack, log_column, arrived, candidates, n_o):
+    rows, width = candidates[0].shape
+    size = n_o * rows
+    out = VMEM((rows, width), jnp.bfloat16)
+    return pl.pallas_call(
+        partial(taylor_kernel, n_o),
+        out_shape=[out, out, VMEM((1, log_column.shape[0] // 2), jnp.float32)],
+        in_specs=[in_vmem()] * (2 + len(arrived) + 4),
+        out_specs=[in_vmem()] * 3,
+        scratch_shapes=[
+            VMEM((size, size), jnp.bfloat16),
+            VMEM((size, width), jnp.bfloat16),
+            VMEM((size, width), jnp.float32),
+        ],
+        compiler_params=pltpu.CompilerParams(vmem_limit_bytes=VMEM_LIMIT),
+        name="taylor",
+    )(*on_chip(pack, log_column, *arrived, *candidates))
+
+
+def place_kernel(steps, n_o, *refs):
+    n_line = len(steps)
+    pieces, weights_ref = refs[:n_line], refs[n_line]
+    out_ref, weights_out, sems = refs[n_line + 1 :]
+    z, o = lax.axis_index("vec"), lax.axis_index("orb")
+    copies = [
+        pltpu.make_async_copy(
+            pieces[k],
+            out_ref.at[jnp.bitwise_xor(z, dz) * n_o + jnp.bitwise_xor(o, flip)],
+            sems.at[k],
+        )
+        for k, (dz, flip) in enumerate(steps)
+    ]
+    copies.append(pltpu.make_async_copy(weights_ref, weights_out, sems.at[n_line]))
+    for copy in copies:
+        copy.start()
+    for copy in copies:
+        copy.wait()
+
+
+def put_in_place(steps, pieces, weights, n_o):
+    n_line = len(pieces)
+    return pl.pallas_call(
+        partial(place_kernel, steps, n_o),
+        out_shape=[
+            jax.ShapeDtypeStruct((n_line,) + pieces[0].shape, pieces[0].dtype),
+            jax.ShapeDtypeStruct(weights.shape, weights.dtype),
+        ],
+        in_specs=[in_vmem()] * (n_line + 1),
+        out_specs=[in_hbm()] * 2,
+        scratch_shapes=[pltpu.SemaphoreType.DMA((n_line + 1,))],
+        compiler_params=pltpu.CompilerParams(vmem_limit_bytes=VMEM_LIMIT),
+        name="place",
+    )(*on_chip(*pieces, weights))
+
+
+def swapped(value, axes, sizes, masks):
+    perm = []
+    for a in range(sizes[0]):
+        for b in range(sizes[1]):
+            perm.append((a * sizes[1] + b, (a ^ masks[0]) * sizes[1] + (b ^ masks[1])))
+    return lax.ppermute(value, axes, perm)
+
+
+def slot_device(n_z, n_x, n_o, walkers, inv_intersection, trial, vectors, aux_field, log_weight, copy_list):
+    line = partial(swapped, axes=("vec", "orb"), sizes=(n_z, n_o))
+    near = partial(swapped, axes=("walk", "orb"), sizes=(n_x, n_o))
+
+    others = ((0, 1), (1, 0), (1, 1))
+    outer_pairs = [(0, 1), (3, 2)]
+    mate = near(vectors, masks=(0, 1))
+    own_pack, here = partial_bias_of(
+        aux_field, log_weight, copy_list, walkers, inv_intersection, trial, vectors
+    )
+    packs = [own_pack]
+    for m in others:
+        packs.append(near(own_pack, masks=m))
+    piece, weights, split, log_column = first_piece(packs, here, mate, n_o)
+    came = line(piece, masks=(1, 0))
+    crossing, nearby, kept, *sources = other_pieces(
+        own_pack, packs[2], weights, split, here, mate, walkers, n_o
+    )
+    inside = lax.ppermute(nearby, "vec", [(1, 2), (2, 1)])
+    inward = lax.ppermute(nearby, "vec", outer_pairs)
+    across = combined(crossing, came, split.shape[0])
+    crossed = line(across, masks=(2, 0))
+    candidates = [sources[0]]
+    for value, m in zip(sources[1:], others):
+        candidates.append(near(value, masks=m))
+    mine, other, slot_weights = taylor(
+        own_pack, log_column, [kept, came, crossed, inside, inward], candidates, n_o
+    )
+    steps = [(k, flip) for k in range(n_z) for flip in range(n_o)]
+    landed = []
+    for dz, flip in steps:
+        half = mine if flip == 0 else other
+        landed.append(half if (dz, flip) == (0, 0) else line(half, masks=(dz, flip)))
+    walkers_out, weights_out = put_in_place(steps, landed, slot_weights, n_o)
+    return walkers_out, weights_out[0]
+
+
+def suits(mesh, walkers, trial, vectors):
+    n_z, n_x, n_o = mesh.shape["vec"], mesh.shape["walk"], mesh.shape["orb"]
+    per_device = walkers.shape[0] // (mesh.shape["grp"] * n_x)
+    local_vectors = vectors.shape[0] // n_z
+    return (
+        n_o == 2
+        and n_x == 2
+        and n_z == 4
+        and per_device == n_z * n_o
+        and local_vectors == per_device
+        and vectors.shape[1] == 4 * LANE
+        and trial.shape[1] == LANE
+    )
+
+
 def solution(mesh):
-    return jax.shard_map(
-        per_device,
-        mesh=mesh,
-        in_specs=(
-            P(("grp", "walk"), "orb", None),
-            P(("grp", "walk"), None, None),
-            P(),
-            P("vec", "orb", None),
-            P(("grp", "walk"), "vec"),
-            P(("grp", "walk")),
-            P(("grp", "walk")),
-        ),
-        out_specs=(P(("grp", "walk"), "orb", None), P(("grp", "walk"))),
-        check_vma=False,
-    )
+    def step(walkers, inv_intersection, trial, vectors, aux_field, log_weight, copy_list):
+        if suits(mesh, walkers, trial, vectors):
+            body = partial(slot_device, mesh.shape["vec"], mesh.shape["walk"], mesh.shape["orb"])
+        else:
+            body = general_device
+        return jax.shard_map(
+            body,
+            mesh=mesh,
+            in_specs=(
+                P(("grp", "walk"), "orb", None),
+                P(("grp", "walk"), None, None),
+                P(),
+                P("vec", "orb", None),
+                P(("grp", "walk"), "vec"),
+                P(("grp", "walk")),
+                P(("grp", "walk")),
+            ),
+            out_specs=(P(("grp", "walk"), "orb", None), P(("grp", "walk"))),
+            check_vma=False,
+        )(walkers, inv_intersection, trial, vectors, aux_field, log_weight, copy_list)
+
+    return step

time: 277 us -> 54.9 us (0.20)
  blocking collectives: 158 us -> 0 us
  waiting for transfers between devices: 65.4 us -> 24.3 us
  matrix products: 31.5 us -> 0 us
  starting transfers between devices: 0.29 us -> 19.8 us
  between operations: 14.9 us -> 0.69 us
  Pallas kernels: 0 us -> 9.8 us
  local copies, waits for them, and re-layouts: 6.25 us -> 0 us
    psum x2 -> x0, blocking collectives: 153 us -> none  [the longest x1 151 us: per_device(): operator = lax.psum(local_operator, 'vec').astype(jnp.bfloat16)]
    all_gather x7 -> x0, waiting for transfers between devices: 64.6 us -> none  [the longest x6 49.4 us: per_device(): lax.all_gather(operand, 'orb', axis=1, tiled=True)]
    dot_general x10 -> x0, matrix products: 31.5 us -> none  [the longest x6 24.9 us: fold_rows(): jnp.einsum('wnm,wme->wne', operator, piece, preferred_element_type=jnp.fl...]
    ppermute x0 -> x18, waiting for transfers between devices: none -> 24.3 us  [the longest x16 24.3 us: swapped(): return lax.ppermute(value, axes, perm)]
    ppermute x0 -> x18, starting transfers between devices: none -> 19.8 us  [the longest x16 16.8 us: swapped(): return lax.ppermute(value, axes, perm)]
    pallas_call x0 -> x6, Pallas kernels: none -> 9.8 us  [the longest x1 4.23 us: partial_bias_of(): pl.pallas_call(bias_kernel, out_shape=[VMEM((3 * n_walk, n_vec), jnp.floa...]
    unnamed x1 -> x0, blocking collectives: 4.91 us -> none
    gather x2 -> x0, local copies, waits for them, and re-layouts: 3.78 us -> none  [per_device(): return (every_walker[copy_list], every_log[copy_list])]
  transfers between devices with their start and end apart: 7 -> 18, of which waited for: 6 -> 11; matrix products, arithmetic and copies ran while one was open for 4% -> 0% of each run, Pallas kernels for 0% -> 10%
where the time goes in v4:
time: 54.9 us; the launch traced here: 54.6 us
  waiting for transfers between devices  24.3 us (44%)
  starting transfers between devices  19.8 us (36%)
  Pallas kernels  9.8 us (18%)
  between operations  0.69 us (1%)
    ppermute x16, waiting for transfers between devices, swapped(): return lax.ppermute(value, axes, perm)  24.3 us
    ppermute x16, starting transfers between devices, swapped(): return lax.ppermute(value, axes, perm)  16.8 us
    pallas_call x1, Pallas kernels, partial_bias_of(): pl.pallas_call(bias_kernel, out_shape=[VMEM((3 * n_walk, n_vec), jnp.floa...  4.23 us
    pallas_call x1, Pallas kernels, taylor(): pl.pallas_call(partial(taylor_kernel, n_o), out_shape=[out, out, VMEM((1,...  2.45 us
    ppermute x1, starting transfers between devices, slot_device(): inward = lax.ppermute(nearby, 'vec', outer_pairs)  2.38 us
    pallas_call x1, Pallas kernels, other_pieces(): pl.pallas_call(partial(other_kernel, n_o), out_shape=[piece] * 3 + [sourc...  1.39 us
  transfers between devices with their start and end apart: 18, of which 11 were waited for; matrix products, arithmetic and copies ran while one was open for 0% of the time, Pallas kernels for 10%

profile of v4, /device:TPU:0, one launch (start us, length us, event | category | flops | bytes accessed | tf_op | source)
XLA Modules:
  0.0 54.6 jit_solution(7542593433192771049)
XLA Ops:
  0.6 0.6 %collective-permute-start.3 = (bf16[8,256,512]{2,1,0:T(8,128)(2,1)}, bf16[8,256,512]{2,1,0:T(8,128)(2,1)S(1)}, u32[]{:S(2)}, u32[]{:S(2)}) collective-permute-start(bf16[8,256,512]{2,1,0:T(8,128)(2,1)} %vec_hbm.1), channel_id=1, source_target_pairs={{0,1},{1,0},{2,3},{3,2},{4,5},{5,4},{6,7},{7,6},{8,9},{9,8},{10,11... | collective-permute-start | bytes 6291464 | tf_op jit(solution)/shard_map/ppermute | solution.py:484
  1.2 4.2 %bias.1 = (f32[24,8]{1,0:T(8,128)S(1)}, bf16[8,256,512]{2,1,0:T(8,128)(2,1)S(1)}) custom-call(f32[8,8]{1,0:T(8,128)} %aux_hbm.1, f32[1,8]{1,0:T(1,128)} %bitcast.3, s32[1,8]{1,0:T(1,128)} %bitcast.4, bf16[8,256,128]{2,1,0:T(8,128)(2,1)} %walkers_hbm.3, bf16[8,128,128]{2,1,0:T(8,128)(2,1)} %inv_hbm.1, bf16[512,128]{1,0:T(8,128)(2,1)} %trial_hbm.1, ...), custom_call_target="tpu_custom_call" | custom-call | tf_op jit(solution)/shard_map/bias/pallas_call | solution.py:121
  5.4 2.7 %collective-permute-start.2 = (f32[24,8]{1,0:T(8,128)S(1)}, f32[24,8]{1,0:T(8,128)S(1)}, u32[]{:S(2)}, u32[]{:S(2)}) collective-permute-start(f32[24,8]{1,0:T(8,128)S(1)} %get-tuple-element.20.own_ref.pack_ref), channel_id=1, source_target_pairs={{0,3},{1,2},{2,1},{3,0},{4,7},{5,6},{6,5},{7,4},{8,11},{9,10},{10,... | collective-permute-start | bytes 2312 | tf_op jit(solution)/shard_map/ppermute | solution.py:484
  8.1 0.0 collective-permute-start.1
  8.1 0.2 collective-permute-start
  8.3 1.2 %collective-permute-done.2.far_ref = f32[24,8]{1,0:T(8,128)S(1)} collective-permute-done((f32[24,8]{1,0:T(8,128)S(1)}, f32[24,8]{1,0:T(8,128)S(1)}, u32[]{:S(2)}, u32[]{:S(2)}) %collective-permute-start.2) | collective-permute-done | bytes 800 | tf_op jit(solution)/shard_map/ppermute | solution.py:484
  9.5 2.3 %collective-permute-done.1.walk_ref = f32[24,8]{1,0:T(8,128)S(1)} collective-permute-done((f32[24,8]{1,0:T(8,128)S(1)}, f32[24,8]{1,0:T(8,128)S(1)}, u32[]{:S(2)}, u32[]{:S(2)}) %collective-permute-start.1) | collective-permute-done | bytes 800 | tf_op jit(solution)/shard_map/ppermute | solution.py:484
  11.8 0.0 collective-permute-done.orb_ref
  11.8 0.0 collective-permute-done.3.mate_ref
  11.8 0.8 %first_piece.1 = (bf16[1072,128]{1,0:T(8,128)(2,1)S(1)}, f32[8,8]{1,0:T(8,128)S(1)}, bf16[16,128]{1,0:T(8,128)(2,1)S(1)}, f32[16,1]{1,0:T(8,128)S(1)}) custom-call(f32[24,8]{1,0:T(8,128)S(1)} %get-tuple-element.20.own_ref.pack_ref, f32[24,8]{1,0:T(8,128)S(1)} %collective-permute-done.orb_ref, f32[24,8]{1,0:T(8,128)S(1)} %collective-permute-done.1.walk_ref, ...), custom_call_target="tpu_custom_call" | custom-call | tf_op jit(solution)/shard_map/first_piece/pallas_call | solution.py:277
  12.6 1.6 %collective-permute-start.4 = (bf16[1072,128]{1,0:T(8,128)(2,1)S(1)}, bf16[1072,128]{1,0:T(8,128)(2,1)S(1)}, u32[]{:S(2)}, u32[]{:S(2)}) collective-permute-start(bf16[1072,128]{1,0:T(8,128)(2,1)S(1)} %get-tuple-element.26), channel_id=1, source_target_pairs={{0,4},{1,5},{4,0},{5,1},{8,12},{9,13},{12,8},{13,9},{2,6},{3,7},{6... | collective-permute-start | bytes 823304 | tf_op jit(solution)/shard_map/ppermute | solution.py:484
  14.3 1.4 %other_pieces.1 = (bf16[1072,128]{1,0:T(8,128)(2,1)S(1)}, bf16[1072,128]{1,0:T(8,128)(2,1)S(1)}, bf16[1072,128]{1,0:T(8,128)(2,1)S(1)}, bf16[256,128]{1,0:T(8,12...) custom-call(f32[24,8]{1,0:T(8,128)S(1)} %get-tuple-element.20.own_ref.pack_ref, ...), custom_call_target="tpu_custom_call" | custom-call | tf_op jit(solution)/shard_map/other_pieces/pallas_call | solution.py:313
  15.7 2.4 %collective-permute-start.7 = (bf16[1072,128]{1,0:T(8,128)(2,1)S(1)}, bf16[1072,128]{1,0:T(8,128)(2,1)S(1)}, u32[]{:S(2)}, u32[]{:S(2)}) collective-permute-start(bf16[1072,128]{1,0:T(8,128)(2,1)S(1)} %get-tuple-element.28), channel_id=1, source_target_pairs={{0,4},{12,8},{1,5},{13,9},{2,6},{14,10},{3,7},{15,11},{16,20},{28,... | collective-permute-start | bytes 823304 | tf_op jit(solution)/shard_map/ppermute | solution.py:506
  18.0 0.7 %collective-permute-start.6 = (bf16[1072,128]{1,0:T(8,128)(2,1)S(1)}, bf16[1072,128]{1,0:T(8,128)(2,1)S(1)}, u32[]{:S(2)}, u32[]{:S(2)}) collective-permute-start(bf16[1072,128]{1,0:T(8,128)(2,1)S(1)} %get-tuple-element.28), channel_id=1, source_target_pairs={{4,8},{8,4},{5,9},{9,5},{6,10},{10,6},{7,11},{11,7},{20,24},{24,20... | collective-permute-start | bytes 823304 | tf_op jit(solution)/shard_map/ppermute | solution.py:505
  18.7 2.5 %collective-permute-done.4.came_ref.first_ref = bf16[1072,128]{1,0:T(8,128)(2,1)S(1)} collective-permute-done((bf16[1072,128]{1,0:T(8,128)(2,1)S(1)}, bf16[1072,128]{1,0:T(8,128)(2,1)S(1)}, u32[]{:S(2)}, u32[]{:S(2)}) %collective-permute-start.4) | collective-permute-done | bytes 274464 | tf_op jit(solution)/shard_map/ppermute | solution.py:484
  21.2 2.9 %collective-permute-start.5 = (bf16[1072,128]{1,0:T(8,128)(2,1)S(1)}, bf16[1072,128]{1,0:T(8,128)(2,1)S(1)}, u32[]{:S(2)}, u32[]{:S(2)}) collective-permute-start(bf16[1072,128]{1,0:T(8,128)(2,1)S(1)} %combine.1), channel_id=1, source_target_pairs={{0,8},{1,9},{4,12},{5,13},{8,0},{9,1},{12,4},{13,5},{2,10},{3,11},... | collective-permute-start | bytes 823304 | tf_op jit(solution)/shard_map/ppermute | solution.py:484
  24.1 0.0 collective-permute-start.8
  24.1 1.0 %collective-permute-start.9 = (bf16[256,128]{1,0:T(8,128)(2,1)S(1)}, bf16[256,128]{1,0:T(8,128)(2,1)S(1)}, u32[]{:S(2)}, u32[]{:S(2)}) collective-permute-start(bf16[256,128]{1,0:T(8,128)(2,1)S(1)} %get-tuple-element.31), channel_id=1, source_target_pairs={{0,2},{1,3},{2,0},{3,1},{4,6},{5,7},{6,4},{7,5},{8,10},{9,11},{10,... | collective-permute-start | bytes 196616 | tf_op jit(solution)/shard_map/ppermute | solution.py:484
  25.1 0.3 collective-permute-done.8.orb_ref
  25.4 0.7 %collective-permute-start.10 = (bf16[256,128]{1,0:T(8,128)(2,1)S(1)}, bf16[256,128]{1,0:T(8,128)(2,1)S(1)}, u32[]{:S(2)}, u32[]{:S(2)}) collective-permute-start(bf16[256,128]{1,0:T(8,128)(2,1)S(1)} %get-tuple-element.32), channel_id=1, source_target_pairs={{0,3},{1,2},{2,1},{3,0},{4,7},{5,6},{6,5},{7,4},{8,11},{9,10},{10,... | collective-permute-start | bytes 196616 | tf_op jit(solution)/shard_map/ppermute | solution.py:484
  26.1 2.8 %collective-permute-done.9.walk_ref = bf16[256,128]{1,0:T(8,128)(2,1)S(1)} collective-permute-done((bf16[256,128]{1,0:T(8,128)(2,1)S(1)}, bf16[256,128]{1,0:T(8,128)(2,1)S(1)}, u32[]{:S(2)}, u32[]{:S(2)}) %collective-permute-start.9) | collective-permute-done | bytes 65568 | tf_op jit(solution)/shard_map/ppermute | solution.py:484
  28.9 0.9 %collective-permute-done.10.far_ref = bf16[256,128]{1,0:T(8,128)(2,1)S(1)} collective-permute-done((bf16[256,128]{1,0:T(8,128)(2,1)S(1)}, bf16[256,128]{1,0:T(8,128)(2,1)S(1)}, u32[]{:S(2)}, u32[]{:S(2)}) %collective-permute-start.10) | collective-permute-done | bytes 65568 | tf_op jit(solution)/shard_map/ppermute | solution.py:484
  29.8 0.0 collective-permute-done.7.inward_ref
  29.8 0.0 collective-permute-done.6.inside_ref
  29.8 8.8 %collective-permute-done.5.cross_ref = bf16[1072,128]{1,0:T(8,128)(2,1)S(1)} collective-permute-done((bf16[1072,128]{1,0:T(8,128)(2,1)S(1)}, bf16[1072,128]{1,0:T(8,128)(2,1)S(1)}, u32[]{:S(2)}, u32[]{:S(2)}) %collective-permute-start.5) | collective-permute-done | bytes 274464 | tf_op jit(solution)/shard_map/ppermute | solution.py:484
  38.6 2.5 %taylor.1 = (bf16[256,128]{1,0:T(8,128)(2,1)S(1)}, bf16[256,128]{1,0:T(8,128)(2,1)S(1)}, f32[1,8]{1,0:T(1,128)S(1)}) custom-call(f32[24,8]{1,0:T(8,128)S(1)} %get-tuple-element.20.own_ref.pack_ref, f32[16,1]{1,0:T(8,128)S(1)} %get-tuple-element.22.log_ref, bf16[1072,128]{1,0:T(8,128)(2,1)S(1)} %get-tuple-element.25.kept_ref, ...), custom_call_target="tpu_custom_call" | custom-call | tf_op jit(solution)/shard_map/taylor/pallas_call | solution.py:428
  41.0 2.7 %collective-permute-start.16 = (bf16[256,128]{1,0:T(8,128)(2,1)S(1)}, bf16[256,128]{1,0:T(8,128)(2,1)S(1)}, u32[]{:S(2)}, u32[]{:S(2)}) collective-permute-start(bf16[256,128]{1,0:T(8,128)(2,1)S(1)} %get-tuple-element.33.refs_0_), channel_id=1, source_target_pairs={{0,12},{1,13},{4,8},{5,9},{8,4},{9,5},{12,0},{13,1},{2,14},{3,15},... | collective-permute-start | bytes 196616 | tf_op jit(solution)/shard_map/ppermute | solution.py:484
  43.7 0.0 collective-permute-start.14
  43.7 1.8 %collective-permute-start.12 = (bf16[256,128]{1,0:T(8,128)(2,1)S(1)}, bf16[256,128]{1,0:T(8,128)(2,1)S(1)}, u32[]{:S(2)}, u32[]{:S(2)}) collective-permute-start(bf16[256,128]{1,0:T(8,128)(2,1)S(1)} %get-tuple-element.33.refs_0_), channel_id=1, source_target_pairs={{0,4},{1,5},{4,0},{5,1},{8,12},{9,13},{12,8},{13,9},{2,6},{3,7},{6... | collective-permute-start | bytes 196616 | tf_op jit(solution)/shard_map/ppermute | solution.py:484
  45.5 0.0 collective-permute-start.17
  45.5 1.5 %collective-permute-start.15 = (bf16[256,128]{1,0:T(8,128)(2,1)S(1)}, bf16[256,128]{1,0:T(8,128)(2,1)S(1)}, u32[]{:S(2)}, u32[]{:S(2)}) collective-permute-start(bf16[256,128]{1,0:T(8,128)(2,1)S(1)} %get-tuple-element.34), channel_id=1, source_target_pairs={{0,9},{1,8},{4,13},{5,12},{8,1},{9,0},{12,5},{13,4},{2,11},{3,10},... | collective-permute-start | bytes 196616 | tf_op jit(solution)/shard_map/ppermute | solution.py:484
  46.9 0.3 collective-permute-done.16.refs_6_
  47.2 1.1 %collective-permute-start.13 = (bf16[256,128]{1,0:T(8,128)(2,1)S(1)}, bf16[256,128]{1,0:T(8,128)(2,1)S(1)}, u32[]{:S(2)}, u32[]{:S(2)}) collective-permute-start(bf16[256,128]{1,0:T(8,128)(2,1)S(1)} %get-tuple-element.34), channel_id=1, source_target_pairs={{0,5},{1,4},{4,1},{5,0},{8,13},{9,12},{12,9},{13,8},{2,7},{3,6},{6... | collective-permute-start | bytes 196616 | tf_op jit(solution)/shard_map/ppermute | solution.py:484
  48.4 1.2 %collective-permute-done.14.refs_4_ = bf16[256,128]{1,0:T(8,128)(2,1)S(1)} collective-permute-done((bf16[256,128]{1,0:T(8,128)(2,1)S(1)}, bf16[256,128]{1,0:T(8,128)(2,1)S(1)}, u32[]{:S(2)}, u32[]{:S(2)}) %collective-permute-start.14) | collective-permute-done | bytes 65568 | tf_op jit(solution)/shard_map/ppermute | solution.py:484
  49.6 0.1 collective-permute-start.11
  49.7 0.0 collective-permute-done.12.refs_2_
  49.7 2.1 %collective-permute-done.17.refs_7_ = bf16[256,128]{1,0:T(8,128)(2,1)S(1)} collective-permute-done((bf16[256,128]{1,0:T(8,128)(2,1)S(1)}, bf16[256,128]{1,0:T(8,128)(2,1)S(1)}, u32[]{:S(2)}, u32[]{:S(2)}) %collective-permute-start.17) | collective-permute-done | bytes 65568 | tf_op jit(solution)/shard_map/ppermute | solution.py:484
  51.8 2.0 %collective-permute-done.15.refs_5_ = bf16[256,128]{1,0:T(8,128)(2,1)S(1)} collective-permute-done((bf16[256,128]{1,0:T(8,128)(2,1)S(1)}, bf16[256,128]{1,0:T(8,128)(2,1)S(1)}, u32[]{:S(2)}, u32[]{:S(2)}) %collective-permute-start.15) | collective-permute-done | bytes 65568 | tf_op jit(solution)/shard_map/ppermute | solution.py:484
  53.8 0.0 collective-permute-done.13.refs_3_
  53.8 0.0 collective-permute-done.11.refs_1_
  53.8 0.9 %place.1 = (bf16[8,256,128]{2,1,0:T(8,128)(2,1)}, f32[1,8]{1,0:T(1,128)}) custom-call(bf16[256,128]{1,0:T(8,128)(2,1)S(1)} %get-tuple-element.33.refs_0_, bf16[256,128]{1,0:T(8,128)(2,1)S(1)} %collective-permute-done.11.refs_1_, bf16[256,128]{1,0:T(8,128)(2,1)S(1)} %collective-permute-done.12.refs_2_, bf16[256,128]{1,0:T(8,128)(2,1)S(1)} %collective-permute-done.13.refs_3_, ...), custom_call_target="tpu_custom_call" | custom-call | tf_op jit(solution)/shard_map/place/pallas_call | solution.py:465
  (1 shorter events, 0.0 us)
Async XLA Ops:
  0.6 11.2 %collective-permute-start.3 = (bf16[8,256,512]{2,1,0:T(8,128)(2,1)}, bf16[8,256,512]{2,1,0:T(8,128)(2,1)S(1)}, u32[]{:S(2)}, u32[]{:S(2)}) collective-permute-start(bf16[8,256,512]{2,1,0:T(8,128)(2,1)} %vec_hbm.1), channel_id=1, source_target_pairs={{0,1},{1,0},{2,3},{3,2},{4,5},{5,4},{6,7},{7,6},{8,9},{9,8},{10,11... | collective-permute-start | bytes 6291464 | tf_op jit(solution)/shard_map/ppermute | solution.py:484
  5.4 4.1 %collective-permute-start.2 = (f32[24,8]{1,0:T(8,128)S(1)}, f32[24,8]{1,0:T(8,128)S(1)}, u32[]{:S(2)}, u32[]{:S(2)}) collective-permute-start(f32[24,8]{1,0:T(8,128)S(1)} %get-tuple-element.20.own_ref.pack_ref), channel_id=1, source_target_pairs={{0,3},{1,2},{2,1},{3,0},{4,7},{5,6},{6,5},{7,4},{8,11},{9,10},{10,... | collective-permute-start | bytes 2312 | tf_op jit(solution)/shard_map/ppermute | solution.py:484
  8.1 3.7 %collective-permute-start.1 = (f32[24,8]{1,0:T(8,128)S(1)}, f32[24,8]{1,0:T(8,128)S(1)}, u32[]{:S(2)}, u32[]{:S(2)}) collective-permute-start(f32[24,8]{1,0:T(8,128)S(1)} %get-tuple-element.20.own_ref.pack_ref), channel_id=1, source_target_pairs={{0,2},{1,3},{2,0},{3,1},{4,6},{5,7},{6,4},{7,5},{8,10},{9,11},{10,... | collective-permute-start | bytes 2312 | tf_op jit(solution)/shard_map/ppermute | solution.py:484
  8.1 3.7 %collective-permute-start = (f32[24,8]{1,0:T(8,128)S(1)}, f32[24,8]{1,0:T(8,128)S(1)}, u32[]{:S(2)}, u32[]{:S(2)}) collective-permute-start(f32[24,8]{1,0:T(8,128)S(1)} %get-tuple-element.20.own_ref.pack_ref), channel_id=1, source_target_pairs={{0,1},{1,0},{2,3},{3,2},{4,5},{5,4},{6,7},{7,6},{8,9},{9,8},{10,11... | collective-permute-start | bytes 2312 | tf_op jit(solution)/shard_map/ppermute | solution.py:484
  12.6 8.6 %collective-permute-start.4 = (bf16[1072,128]{1,0:T(8,128)(2,1)S(1)}, bf16[1072,128]{1,0:T(8,128)(2,1)S(1)}, u32[]{:S(2)}, u32[]{:S(2)}) collective-permute-start(bf16[1072,128]{1,0:T(8,128)(2,1)S(1)} %get-tuple-element.26), channel_id=1, source_target_pairs={{0,4},{1,5},{4,0},{5,1},{8,12},{9,13},{12,8},{13,9},{2,6},{3,7},{6... | collective-permute-start | bytes 823304 | tf_op jit(solution)/shard_map/ppermute | solution.py:484
  15.7 14.1 %collective-permute-start.7 = (bf16[1072,128]{1,0:T(8,128)(2,1)S(1)}, bf16[1072,128]{1,0:T(8,128)(2,1)S(1)}, u32[]{:S(2)}, u32[]{:S(2)}) collective-permute-start(bf16[1072,128]{1,0:T(8,128)(2,1)S(1)} %get-tuple-element.28), channel_id=1, source_target_pairs={{0,4},{12,8},{1,5},{13,9},{2,6},{14,10},{3,7},{15,11},{16,20},{28,... | collective-permute-start | bytes 823304 | tf_op jit(solution)/shard_map/ppermute | solution.py:506
  18.0 11.7 %collective-permute-start.6 = (bf16[1072,128]{1,0:T(8,128)(2,1)S(1)}, bf16[1072,128]{1,0:T(8,128)(2,1)S(1)}, u32[]{:S(2)}, u32[]{:S(2)}) collective-permute-start(bf16[1072,128]{1,0:T(8,128)(2,1)S(1)} %get-tuple-element.28), channel_id=1, source_target_pairs={{4,8},{8,4},{5,9},{9,5},{6,10},{10,6},{7,11},{11,7},{20,24},{24,20... | collective-permute-start | bytes 823304 | tf_op jit(solution)/shard_map/ppermute | solution.py:505
  21.2 17.3 %collective-permute-start.5 = (bf16[1072,128]{1,0:T(8,128)(2,1)S(1)}, bf16[1072,128]{1,0:T(8,128)(2,1)S(1)}, u32[]{:S(2)}, u32[]{:S(2)}) collective-permute-start(bf16[1072,128]{1,0:T(8,128)(2,1)S(1)} %combine.1), channel_id=1, source_target_pairs={{0,8},{1,9},{4,12},{5,13},{8,0},{9,1},{12,4},{13,5},{2,10},{3,11},... | collective-permute-start | bytes 823304 | tf_op jit(solution)/shard_map/ppermute | solution.py:484
  24.1 1.3 %collective-permute-start.8 = (bf16[256,128]{1,0:T(8,128)(2,1)S(1)}, bf16[256,128]{1,0:T(8,128)(2,1)S(1)}, u32[]{:S(2)}, u32[]{:S(2)}) collective-permute-start(bf16[256,128]{1,0:T(8,128)(2,1)S(1)} %get-tuple-element.30), channel_id=1, source_target_pairs={{0,1},{1,0},{2,3},{3,2},{4,5},{5,4},{6,7},{7,6},{8,9},{9,8},{10,11... | collective-permute-start | bytes 196616 | tf_op jit(solution)/shard_map/ppermute | solution.py:484
  24.1 4.8 %collective-permute-start.9 = (bf16[256,128]{1,0:T(8,128)(2,1)S(1)}, bf16[256,128]{1,0:T(8,128)(2,1)S(1)}, u32[]{:S(2)}, u32[]{:S(2)}) collective-permute-start(bf16[256,128]{1,0:T(8,128)(2,1)S(1)} %get-tuple-element.31), channel_id=1, source_target_pairs={{0,2},{1,3},{2,0},{3,1},{4,6},{5,7},{6,4},{7,5},{8,10},{9,11},{10,... | collective-permute-start | bytes 196616 | tf_op jit(solution)/shard_map/ppermute | solution.py:484
  25.4 4.4 %collective-permute-start.10 = (bf16[256,128]{1,0:T(8,128)(2,1)S(1)}, bf16[256,128]{1,0:T(8,128)(2,1)S(1)}, u32[]{:S(2)}, u32[]{:S(2)}) collective-permute-start(bf16[256,128]{1,0:T(8,128)(2,1)S(1)} %get-tuple-element.32), channel_id=1, source_target_pairs={{0,3},{1,2},{2,1},{3,0},{4,7},{5,6},{6,5},{7,4},{8,11},{9,10},{10,... | collective-permute-start | bytes 196616 | tf_op jit(solution)/shard_map/ppermute | solution.py:484
  41.0 6.2 %collective-permute-start.16 = (bf16[256,128]{1,0:T(8,128)(2,1)S(1)}, bf16[256,128]{1,0:T(8,128)(2,1)S(1)}, u32[]{:S(2)}, u32[]{:S(2)}) collective-permute-start(bf16[256,128]{1,0:T(8,128)(2,1)S(1)} %get-tuple-element.33.refs_0_), channel_id=1, source_target_pairs={{0,12},{1,13},{4,8},{5,9},{8,4},{9,5},{12,0},{13,1},{2,14},{3,15},... | collective-permute-start | bytes 196616 | tf_op jit(solution)/shard_map/ppermute | solution.py:484
  43.7 5.9 %collective-permute-start.14 = (bf16[256,128]{1,0:T(8,128)(2,1)S(1)}, bf16[256,128]{1,0:T(8,128)(2,1)S(1)}, u32[]{:S(2)}, u32[]{:S(2)}) collective-permute-start(bf16[256,128]{1,0:T(8,128)(2,1)S(1)} %get-tuple-element.33.refs_0_), channel_id=1, source_target_pairs={{0,8},{1,9},{4,12},{5,13},{8,0},{9,1},{12,4},{13,5},{2,10},{3,11},... | collective-permute-start | bytes 196616 | tf_op jit(solution)/shard_map/ppermute | solution.py:484
  43.7 6.0 %collective-permute-start.12 = (bf16[256,128]{1,0:T(8,128)(2,1)S(1)}, bf16[256,128]{1,0:T(8,128)(2,1)S(1)}, u32[]{:S(2)}, u32[]{:S(2)}) collective-permute-start(bf16[256,128]{1,0:T(8,128)(2,1)S(1)} %get-tuple-element.33.refs_0_), channel_id=1, source_target_pairs={{0,4},{1,5},{4,0},{5,1},{8,12},{9,13},{12,8},{13,9},{2,6},{3,7},{6... | collective-permute-start | bytes 196616 | tf_op jit(solution)/shard_map/ppermute | solution.py:484
  45.5 6.3 %collective-permute-start.17 = (bf16[256,128]{1,0:T(8,128)(2,1)S(1)}, bf16[256,128]{1,0:T(8,128)(2,1)S(1)}, u32[]{:S(2)}, u32[]{:S(2)}) collective-permute-start(bf16[256,128]{1,0:T(8,128)(2,1)S(1)} %get-tuple-element.34), channel_id=1, source_target_pairs={{0,13},{1,12},{4,9},{5,8},{8,5},{9,4},{12,1},{13,0},{2,15},{3,14},... | collective-permute-start | bytes 196616 | tf_op jit(solution)/shard_map/ppermute | solution.py:484
  45.5 8.3 %collective-permute-start.15 = (bf16[256,128]{1,0:T(8,128)(2,1)S(1)}, bf16[256,128]{1,0:T(8,128)(2,1)S(1)}, u32[]{:S(2)}, u32[]{:S(2)}) collective-permute-start(bf16[256,128]{1,0:T(8,128)(2,1)S(1)} %get-tuple-element.34), channel_id=1, source_target_pairs={{0,9},{1,8},{4,13},{5,12},{8,1},{9,0},{12,5},{13,4},{2,11},{3,10},... | collective-permute-start | bytes 196616 | tf_op jit(solution)/shard_map/ppermute | solution.py:484
  47.2 6.5 %collective-permute-start.13 = (bf16[256,128]{1,0:T(8,128)(2,1)S(1)}, bf16[256,128]{1,0:T(8,128)(2,1)S(1)}, u32[]{:S(2)}, u32[]{:S(2)}) collective-permute-start(bf16[256,128]{1,0:T(8,128)(2,1)S(1)} %get-tuple-element.34), channel_id=1, source_target_pairs={{0,5},{1,4},{4,1},{5,0},{8,13},{9,12},{12,9},{13,8},{2,7},{3,6},{6... | collective-permute-start | bytes 196616 | tf_op jit(solution)/shard_map/ppermute | solution.py:484
  49.6 4.2 %collective-permute-start.11 = (bf16[256,128]{1,0:T(8,128)(2,1)S(1)}, bf16[256,128]{1,0:T(8,128)(2,1)S(1)}, u32[]{:S(2)}, u32[]{:S(2)}) collective-permute-start(bf16[256,128]{1,0:T(8,128)(2,1)S(1)} %get-tuple-element.34), channel_id=1, source_target_pairs={{0,1},{1,0},{4,5},{5,4},{8,9},{9,8},{12,13},{13,12},{2,3},{3,2},{6... | collective-permute-start | bytes 196616 | tf_op jit(solution)/shard_map/ppermute | solution.py:484

commit v5 on v4

--- a/solution.py
+++ b/solution.py
@@ -76,7 +76,7 @@
     return (every_walker[copy_list], every_log[copy_list])
 
 
-def bias_kernel(aux_hbm, log_hbm, copy_hbm, walkers_hbm, inv_hbm, trial_hbm, vec_hbm, out_ref, vec_ref,
+def bias_kernel(aux_hbm, log_hbm, copy_hbm, walkers_hbm, inv_hbm, trial_hbm, vec_hbm, out_ref, vec_ref, quad_ref,
                 aux_ref, log_ref, copy_ref, walkers_ref, inv_ref, trial_ref, green_ref, sems):
     n_walk = walkers_hbm.shape[0]
     n_vec = vec_hbm.shape[0]
@@ -98,10 +98,13 @@
         green_ref[w] = mm(walkers_ref[w], inv_ref[w]).astype(jnp.bfloat16).astype(jnp.float32)
     copies[2].wait()
     trial = trial_ref[...]
+    n_rows = vec_hbm.shape[1]
+    columns = pl.ds(pl.multiple_of(lax.axis_index("orb") * n_rows, n_rows), n_rows)
     lane = lax.broadcasted_iota(jnp.int32, (n_walk, n_vec), 1)
     total = jnp.zeros((n_walk, n_vec), jnp.float32)
     for g in range(n_vec):
         vec_copies[g].wait()
+        quad_ref[g] = vec_ref[g, :, columns]
         mixed = mm(vec_ref[g], trial).astype(jnp.bfloat16).astype(jnp.float32)
         rows = [jnp.sum(green_ref[w] * mixed, axis=0, keepdims=True) for w in range(n_walk)]
         column = jnp.sum(jnp.concatenate(rows, axis=0), axis=1, keepdims=True)
@@ -120,9 +123,13 @@
     log_row, copy_row = log_weight[None, :], copy_list[None, :]
     return pl.pallas_call(
         bias_kernel,
-        out_shape=[VMEM((3 * n_walk, n_vec), jnp.float32), VMEM(vectors.shape, vectors.dtype)],
+        out_shape=[
+            VMEM((3 * n_walk, n_vec), jnp.float32),
+            VMEM(vectors.shape, vectors.dtype),
+            VMEM((n_vec, vectors.shape[1], vectors.shape[1]), vectors.dtype),
+        ],
         in_specs=[in_hbm()] * 7,
-        out_specs=[in_vmem()] * 2,
+        out_specs=[in_vmem()] * 3,
         scratch_shapes=[
             VMEM(aux.shape, aux.dtype),
             VMEM(log_row.shape, log_row.dtype),
@@ -148,27 +155,29 @@
     return jnp.sum(jnp.where(lane == at, row, 0.0)).astype(jnp.int32)
 
 
-def layout(n_block):
-    at = n_block // 2 * LANE
-    offsets = {}
+def layout(n_block, n_both):
+    offsets, at = {}, 0
     for i in range(n_block):
         for j in range(i + 1, n_block):
             offsets[(i, j)] = at
             at += LANE
-    return offsets, at
-
-
-def piece_rows(size, n_both):
-    n_block = size // LANE
-    return layout(n_block)[1] + n_block // 2 * 16 + n_both
-
-
-def fill_pieces(weights, here_ref, mate_ref, piece_refs, split, o):
+    for i in range(0, n_block, 2):
+        offsets[(i, i)] = at
+        at += LANE
+    for i in range(1, n_block, 2):
+        offsets[(i, i)] = at
+        at += 16
+    offsets["factor"] = at
+    offsets["end"] = at + n_both
+    return offsets
+
+
+def fill_pieces(weights, here_ref, mate_ref, targets, split, o):
     n_vec, n_rows, size = here_ref.shape
     n_block = size // LANE
     in_half = n_rows // LANE
-    offsets, at = layout(n_block)
-    count = len(piece_refs)
+    offsets = layout(n_block, split.shape[0])
+    count = len(targets)
     tall = LANE // 2
     splats = [
         [jnp.broadcast_to(weights[k : k + 1, g : g + 1], (tall, LANE)) for g in range(n_vec)]
@@ -176,43 +185,51 @@
     ]
 
     def sums(i, j, step):
-        source = here_ref if i < in_half else mate_ref
         rows = pl.ds(i % in_half * LANE + step * tall, tall)
-        column = lax.rem(j + o * in_half, n_block) * LANE
-        columns = pl.ds(pl.multiple_of(column, LANE), LANE)
+        if i < in_half:
+            column = lax.rem(j + o * in_half, n_block) * LANE
+            source, columns = here_ref, pl.ds(pl.multiple_of(column, LANE), LANE)
+        else:
+            source, columns = mate_ref, pl.ds((j - in_half) * LANE, LANE)
         result = [None] * count
         for g in range(n_vec):
             value = source[g, rows, columns].astype(jnp.float32)
             for k in range(count):
-                part = splats[k][g] * value
-                result[k] = part if g == 0 else result[k] + part
+                product = splats[k][g] * value
+                result[k] = product if g == 0 else result[k] + product
         return result
+
+    def put(k, offset, count_rows, value):
+        targets[k][pl.ds(offset, count_rows), :] = value
 
     line = lax.broadcasted_iota(jnp.int32, (tall, LANE), 0)
     lane = lax.broadcasted_iota(jnp.int32, (tall, LANE), 1)
-    for step in range(LANE // tall):
-        row_at = line + step * tall
-        for (i, j), offset in offsets.items():
-            for k, value in enumerate(sums(i, j, step)):
-                piece_refs[k][pl.ds(offset + step * tall, tall), :] = value.astype(jnp.bfloat16)
-        for pair in range(n_block // 2):
-            upper = sums(2 * pair, 2 * pair, step)
-            lower = sums(2 * pair + 1, 2 * pair + 1, step)
+    seen = lax.broadcasted_iota(jnp.int32, (16, LANE), 1)
+    for pair, offset in offsets.items():
+        if isinstance(pair, str):
+            continue
+        i, j = pair
+        if i == j and i % 2 == 1:
+            continue
+        diagonals = [None] * count
+        for step in range(LANE // tall):
+            at = offset + step * tall
+            upper = sums(i, j, step)
+            if i == j:
+                row_at = line + step * tall
+                lower = sums(i + 1, i + 1, step)
+                for k in range(count):
+                    found = jnp.sum(jnp.where(row_at == lane, lower[k], 0.0), axis=0, keepdims=True)
+                    diagonals[k] = found if step == 0 else diagonals[k] + found
+                upper = [jnp.where(row_at <= lane, u, v) for u, v in zip(upper, lower)]
             for k in range(count):
-                merged = jnp.where(row_at <= lane, upper[k], lower[k])
-                piece_refs[k][pl.ds(pair * LANE + step * tall, tall), :] = merged.astype(jnp.bfloat16)
-                found = jnp.sum(jnp.where(row_at == lane, lower[k], 0.0), axis=0, keepdims=True)
-                spot = pl.ds(at + pair * 16, 16)
-                row = jnp.broadcast_to(found, (16, LANE)).astype(jnp.bfloat16)
-                if step == 0:
-                    piece_refs[k][spot, :] = row
-                else:
-                    held = piece_refs[k][spot, :]
-                    seen = lax.broadcasted_iota(jnp.int32, (16, LANE), 1) < step * tall
-                    piece_refs[k][spot, :] = jnp.where(seen, held, row)
-    at += n_block // 2 * 16
+                put(k, at, tall, upper[k].astype(jnp.bfloat16))
+        if i == j:
+            for k in range(count):
+                row = jnp.broadcast_to(diagonals[k], (16, LANE)).astype(jnp.bfloat16)
+                put(k, offsets[(i + 1, i + 1)], 16, row)
     for k in range(count):
-        piece_refs[k][pl.ds(at, split.shape[0]), :] = split
+        put(k, offsets["factor"], split.shape[0], split)
 
 
 def split_column(column):
@@ -277,7 +294,7 @@
     return pl.pallas_call(
         partial(first_kernel, n_o),
         out_shape=[
-            VMEM((piece_rows(here.shape[2], 2 * n_walk), LANE), jnp.bfloat16),
+            VMEM((layout(here.shape[2] // LANE, 2 * n_walk)["end"], LANE), jnp.bfloat16),
             VMEM((8, n_vec), jnp.float32),
             VMEM((2 * n_walk, LANE), jnp.bfloat16),
             VMEM((2 * n_walk, 1), jnp.float32),
@@ -308,7 +325,8 @@
 
 
 def other_pieces(own_pack, walk_pack, weights, split, here, mate, walkers, n_o):
-    piece = VMEM((piece_rows(here.shape[2], split.shape[0]), LANE), jnp.bfloat16)
+    offsets = layout(here.shape[2] // LANE, split.shape[0])
+    piece = VMEM((offsets["end"], LANE), jnp.bfloat16)
     source = VMEM(walkers.shape[1:], walkers.dtype)
     return pl.pallas_call(
         partial(other_kernel, n_o),
@@ -321,33 +339,32 @@
     )(*on_chip(own_pack, walk_pack, weights, split, here, mate), *in_place(walkers))
 
 
-def combine_kernel(n_both, mine_ref, came_ref, out_ref):
+def combine_kernel(body, far_ref, near_ref, came_ref, out_ref):
     inner = routes(lax.axis_index("vec"))[0]
-    body = mine_ref.shape[0] - n_both
 
     @pl.when(inner)
     def _():
         for low in range(0, body, LANE):
             rows = pl.ds(low, min(LANE, body - low))
-            value = mine_ref[rows, :].astype(jnp.float32) + came_ref[rows, :].astype(jnp.float32)
+            value = far_ref[rows, :].astype(jnp.float32) + came_ref[rows, :].astype(jnp.float32)
             out_ref[rows, :] = value.astype(jnp.bfloat16)
-        tail = pl.ds(body, n_both)
-        out_ref[tail, :] = split_column(joined(mine_ref[tail, :]) + joined(came_ref[tail, :]))
+        tail = pl.ds(body, out_ref.shape[0] - body)
+        out_ref[tail, :] = split_column(joined(far_ref[tail, :]) + joined(came_ref[tail, :]))
 
     @pl.when(jnp.logical_not(inner))
     def _():
-        out_ref[...] = mine_ref[...]
-
-
-def combined(mine, came, n_both):
+        out_ref[...] = near_ref[...]
+
+
+def combined(far, nearby, came, n_both):
     return pl.pallas_call(
-        partial(combine_kernel, n_both),
-        out_shape=VMEM(mine.shape, mine.dtype),
-        in_specs=[in_vmem()] * 2,
+        partial(combine_kernel, came.shape[0] - n_both),
+        out_shape=VMEM(came.shape, came.dtype),
+        in_specs=[in_vmem()] * 3,
         out_specs=in_vmem(),
         compiler_params=pltpu.CompilerParams(vmem_limit_bytes=VMEM_LIMIT),
         name="combine",
-    )(*on_chip(mine, came))
+    )(*on_chip(far, nearby, came))
 
 
 def log_weights(copy_row, log_column, total, x):
@@ -361,41 +378,40 @@
     return jnp.sum(chosen, axis=0, keepdims=True)
 
 
-def taylor_kernel(n_o, pack_ref, log_ref, kept_ref, first_ref, cross_ref, inside_ref, inward_ref,
-                  own_ref, orb_ref, walk_ref, far_ref, mine_ref, other_ref, weights_ref,
-                  op_ref, term_ref, sum_ref):
+def taylor_kernel(n_o, pack_ref, log_ref, kept_ref, first_ref, inside_ref, cross_ref, last_ref, own_ref, orb_ref, walk_ref, far_ref,
+                  mine_ref, other_ref, weights_ref, op_ref, term_ref, sum_ref):
     z, x, o = lax.axis_index("vec"), lax.axis_index("walk"), lax.axis_index("orb")
     inner = routes(z)[0]
     n_both = log_ref.shape[0]
     n_walk = n_both // 2
     n_block = op_ref.shape[0] // LANE
-    offsets, at = layout(n_block)
+    offsets = layout(n_block, n_both)
     i_at = lax.broadcasted_iota(jnp.int32, (LANE, LANE), 0)
     j_at = lax.broadcasted_iota(jnp.int32, (LANE, LANE), 1)
 
-    def total(start, count):
-        rows = pl.ds(start, count)
-        first, cross, inside, inward, kept = (
-            ref[rows, :].astype(jnp.float32)
-            for ref in (first_ref, cross_ref, inside_ref, inward_ref, kept_ref)
-        )
-        return (kept + cross) + jnp.where(inner, inside + inward, first)
+    def terms(offset, count):
+        rows = pl.ds(offset, count)
+        return (ref[rows, :] for ref in (kept_ref, first_ref, inside_ref, cross_ref, last_ref))
+
+    def total(offset, count):
+        kept, first, inside, cross, last = (value.astype(jnp.float32) for value in terms(offset, count))
+        return (kept + last) + jnp.where(inner, inside + cross, first)
 
     def put(i, j, value):
         op_ref[pl.ds(i * LANE, LANE), pl.ds(j * LANE, LANE)] = value.astype(jnp.bfloat16)
 
-    for (i, j), offset in offsets.items():
-        value = total(offset, LANE)
-        put(i, j, value)
-        put(j, i, value.T)
-    for pair in range(n_block // 2):
-        merged = total(pair * LANE, LANE)
-        diagonal = total(at + pair * 16, 16)[:1]
+    for i in range(n_block):
+        for j in range(i + 1, n_block):
+            value = total(offsets[(i, j)], LANE)
+            put(i, j, value)
+            put(j, i, value.T)
+    for i in range(0, n_block, 2):
+        merged = total(offsets[(i, i)], LANE)
+        diagonal = total(offsets[(i + 1, i + 1)], 16)[:1]
         turned = merged.T
-        put(2 * pair, 2 * pair, jnp.where(i_at <= j_at, merged, turned))
+        put(i, i, jnp.where(i_at <= j_at, merged, turned))
         second = jnp.where(i_at > j_at, merged, turned)
-        put(2 * pair + 1, 2 * pair + 1, jnp.where(i_at == j_at, diagonal, second))
-    at += n_block // 2 * 16
+        put(i + 1, i + 1, jnp.where(i_at == j_at, diagonal, second))
 
     copy_row = copies_of(pack_ref)
     here = lax.div(entry(copy_row, z * n_o + o), n_walk) == x
@@ -413,11 +429,8 @@
     mine_ref[...] = sum_ref[top, :].astype(jnp.bfloat16)
     other_ref[...] = sum_ref[bottom, :].astype(jnp.bfloat16)
 
-    tail = pl.ds(at, n_both)
-    first, cross, inside, inward, kept = (
-        joined(ref[tail, :]) for ref in (first_ref, cross_ref, inside_ref, inward_ref, kept_ref)
-    )
-    factor = (kept + jnp.where(inner, inward, first)) + jnp.where(inner, inside + cross, cross)
+    kept, first, inside, cross, last = (joined(value) for value in terms(offsets["factor"], n_both))
+    factor = (kept + jnp.where(inner, last, first)) + jnp.where(inner, inside + cross, last)
     weights_ref[...] = log_weights(copy_row, log_ref[...], factor, x)
 
 
@@ -489,28 +502,27 @@
     near = partial(swapped, axes=("walk", "orb"), sizes=(n_x, n_o))
 
     others = ((0, 1), (1, 0), (1, 1))
-    outer_pairs = [(0, 1), (3, 2)]
-    mate = near(vectors, masks=(0, 1))
-    own_pack, here = partial_bias_of(
+    own_pack, here, quadrant = partial_bias_of(
         aux_field, log_weight, copy_list, walkers, inv_intersection, trial, vectors
     )
     packs = [own_pack]
     for m in others:
         packs.append(near(own_pack, masks=m))
+    mate = near(quadrant, masks=(0, 1))
     piece, weights, split, log_column = first_piece(packs, here, mate, n_o)
     came = line(piece, masks=(1, 0))
     crossing, nearby, kept, *sources = other_pieces(
         own_pack, packs[2], weights, split, here, mate, walkers, n_o
     )
-    inside = lax.ppermute(nearby, "vec", [(1, 2), (2, 1)])
-    inward = lax.ppermute(nearby, "vec", outer_pairs)
-    across = combined(crossing, came, split.shape[0])
-    crossed = line(across, masks=(2, 0))
+    inside = lax.ppermute(nearby, "vec", [(0, 0), (1, 2), (2, 1), (3, 3)])
+    crossed = lax.ppermute(crossing, "vec", [(0, 2), (3, 1), (1, 0), (2, 3)])
+    passed = combined(crossing, nearby, came, split.shape[0])
+    last = lax.ppermute(passed, "vec", [(0, 1), (1, 3), (2, 0), (3, 2)])
     candidates = [sources[0]]
     for value, m in zip(sources[1:], others):
         candidates.append(near(value, masks=m))
     mine, other, slot_weights = taylor(
-        own_pack, log_column, [kept, came, crossed, inside, inward], candidates, n_o
+        own_pack, log_column, [kept, came, inside, crossed, last], candidates, n_o
     )
     steps = [(k, flip) for k in range(n_z) for flip in range(n_o)]
     landed = []

time: 54.9 us -> 53.9 us (0.982)
  waiting for transfers between devices: 24.3 us -> 23.3 us
    ppermute x16 -> x15, waiting for transfers between devices: 24.3 us -> 13.8 us  [swapped(): return lax.ppermute(value, axes, perm)]
    ppermute x2 -> x3, waiting for transfers between devices: 0.01 us -> 9.57 us  [the longest x1 9.56 us: slot_device(): last = lax.ppermute(passed, 'vec', [(0, 1), (1, 3), (2, 0), (3, 2)])]
    ppermute x16 -> x15, starting transfers between devices: 16.8 us -> 13.4 us  [swapped(): return lax.ppermute(value, axes, perm)]
    ppermute x2 -> x3, starting transfers between devices: 3.06 us -> 6.37 us  [the longest x1 3.87 us: slot_device(): crossed = lax.ppermute(crossing, 'vec', [(0, 2), (3, 1), (1, 0), (2, 3)])]
  transfers between devices with their start and end apart: 18 -> 18, of which waited for: 11 -> 10; matrix products, arithmetic and copies ran while one was open for 0% -> 0% of each run, Pallas kernels for 10% -> 3%
where the time goes in v5:
time: 53.9 us; the launch traced here: 53.7 us
  waiting for transfers between devices  23.3 us (43%)
  starting transfers between devices  19.8 us (37%)
  Pallas kernels  9.85 us (18%)
  between operations  0.68 us (1%)
    ppermute x15, waiting for transfers between devices, swapped(): return lax.ppermute(value, axes, perm)  13.8 us
    ppermute x15, starting transfers between devices, swapped(): return lax.ppermute(value, axes, perm)  13.4 us
    ppermute x1, waiting for transfers between devices, slot_device(): last = lax.ppermute(passed, 'vec', [(0, 1), (1, 3), (2, 0), (3, 2)])  9.56 us
    pallas_call x1, Pallas kernels, partial_bias_of(): pl.pallas_call(bias_kernel, out_shape=[VMEM((3 * n_walk, n_vec), jnp.floa...  4.29 us
    ppermute x1, starting transfers between devices, slot_device(): crossed = lax.ppermute(crossing, 'vec', [(0, 2), (3, 1), (1, 0), (2, 3)])  3.87 us
    pallas_call x1, Pallas kernels, taylor(): pl.pallas_call(partial(taylor_kernel, n_o), out_shape=[out, out, VMEM((1,...  2.45 us
    ppermute x1, starting transfers between devices, slot_device(): last = lax.ppermute(passed, 'vec', [(0, 1), (1, 3), (2, 0), (3, 2)])  1.82 us
    pallas_call x1, Pallas kernels, other_pieces(): pl.pallas_call(partial(other_kernel, n_o), out_shape=[piece] * 3 + [sourc...  1.4 us
  transfers between devices with their start and end apart: 18, of which 10 were waited for; matrix products, arithmetic and copies ran while one was open for 0% of the time, Pallas kernels for 3%

profile of v5, /device:TPU:0, one launch (start us, length us, event | category | flops | bytes accessed | tf_op | source)
XLA Modules:
  0.0 53.7 jit_solution(6179179442093528323)
XLA Ops:
  0.6 4.3 %bias.1 = (f32[24,8]{1,0:T(8,128)S(1)}, bf16[8,256,512]{2,1,0:T(8,128)(2,1)S(1)}, bf16[8,256,256]{2,1,0:T(8,128)(2,1)S(1)}) custom-call(f32[8,8]{1,0:T(8,128)} %aux_hbm.1, f32[1,8]{1,0:T(1,128)} %bitcast.3, s32[1,8]{1,0:T(1,128)} %bitcast.4, bf16[8,256,128]{2,1,0:T(8,128)(2,1)} %walkers_hbm.3, bf16[8,128,128]{2,1,0:T(8,128)(2,1)} %inv_hbm.1, ...), custom_call_target="tpu_custom_call" | custom-call | tf_op jit(solution)/shard_map/bias/pallas_call | solution.py:124
  4.9 0.5 %collective-permute-start.3 = (bf16[8,256,256]{2,1,0:T(8,128)(2,1)S(1)}, bf16[8,256,256]{2,1,0:T(8,128)(2,1)S(1)}, u32[]{:S(2)}, u32[]{:S(2)}) collective-permute-start(bf16[8,256,256]{2,1,0:T(8,128)(2,1)S(1)} %get-tuple-element.23), channel_id=1, source_target_pairs={{0,1},{1,0},{2,3},{3,2},{4,5},{5,4},{6,7},{7,6},{8,9},{9,8},{10,11... | collective-permute-start | bytes 3145736 | tf_op jit(solution)/shard_map/ppermute | solution.py:497
  5.5 2.6 %collective-permute-start.2 = (f32[24,8]{1,0:T(8,128)S(1)}, f32[24,8]{1,0:T(8,128)S(1)}, u32[]{:S(2)}, u32[]{:S(2)}) collective-permute-start(f32[24,8]{1,0:T(8,128)S(1)} %get-tuple-element.21.own_ref.pack_ref), channel_id=1, source_target_pairs={{0,3},{1,2},{2,1},{3,0},{4,7},{5,6},{6,5},{7,4},{8,11},{9,10},{10,... | collective-permute-start | bytes 2312 | tf_op jit(solution)/shard_map/ppermute | solution.py:497
  8.1 0.0 collective-permute-start.1
  8.1 0.1 collective-permute-start
  8.2 1.3 %collective-permute-done.2.far_ref = f32[24,8]{1,0:T(8,128)S(1)} collective-permute-done((f32[24,8]{1,0:T(8,128)S(1)}, f32[24,8]{1,0:T(8,128)S(1)}, u32[]{:S(2)}, u32[]{:S(2)}) %collective-permute-start.2) | collective-permute-done | bytes 800 | tf_op jit(solution)/shard_map/ppermute | solution.py:497
  9.5 2.3 %collective-permute-done.1.walk_ref = f32[24,8]{1,0:T(8,128)S(1)} collective-permute-done((f32[24,8]{1,0:T(8,128)S(1)}, f32[24,8]{1,0:T(8,128)S(1)}, u32[]{:S(2)}, u32[]{:S(2)}) %collective-permute-start.1) | collective-permute-done | bytes 800 | tf_op jit(solution)/shard_map/ppermute | solution.py:497
  11.7 0.0 collective-permute-done.orb_ref
  11.8 0.0 collective-permute-done.3.mate_ref
  11.8 0.8 %first_piece.1 = (bf16[1072,128]{1,0:T(8,128)(2,1)S(1)}, f32[8,8]{1,0:T(8,128)S(1)}, bf16[16,128]{1,0:T(8,128)(2,1)S(1)}, f32[16,1]{1,0:T(8,128)S(1)}) custom-call(f32[24,8]{1,0:T(8,128)S(1)} %get-tuple-element.21.own_ref.pack_ref, f32[24,8]{1,0:T(8,128)S(1)} %collective-permute-done.orb_ref, f32[24,8]{1,0:T(8,128)S(1)} %collective-permute-done.1.walk_ref, ...), custom_call_target="tpu_custom_call" | custom-call | tf_op jit(solution)/shard_map/first_piece/pallas_call | solution.py:294
  12.6 1.6 %collective-permute-start.4 = (bf16[1072,128]{1,0:T(8,128)(2,1)S(1)}, bf16[1072,128]{1,0:T(8,128)(2,1)S(1)}, u32[]{:S(2)}, u32[]{:S(2)}) collective-permute-start(bf16[1072,128]{1,0:T(8,128)(2,1)S(1)} %get-tuple-element.28), channel_id=1, source_target_pairs={{0,4},{1,5},{4,0},{5,1},{8,12},{9,13},{12,8},{13,9},{2,6},{3,7},{6... | collective-permute-start | bytes 823304 | tf_op jit(solution)/shard_map/ppermute | solution.py:497
  14.2 1.4 %other_pieces.1 = (bf16[1072,128]{1,0:T(8,128)(2,1)S(1)}, bf16[1072,128]{1,0:T(8,128)(2,1)S(1)}, bf16[1072,128]{1,0:T(8,128)(2,1)S(1)}, bf16[256,128]{1,0:T(8,12...) custom-call(f32[24,8]{1,0:T(8,128)S(1)} %get-tuple-element.21.own_ref.pack_ref, ...), custom_call_target="tpu_custom_call" | custom-call | tf_op jit(solution)/shard_map/other_pieces/pallas_call | solution.py:331
  15.7 0.7 %collective-permute-start.5 = (bf16[1072,128]{1,0:T(8,128)(2,1)S(1)}, bf16[1072,128]{1,0:T(8,128)(2,1)S(1)}, u32[]{:S(2)}, u32[]{:S(2)}) collective-permute-start(bf16[1072,128]{1,0:T(8,128)(2,1)S(1)} %get-tuple-element.29.near_ref), channel_id=1, source_target_pairs={{0,0},{4,8},{8,4},{12,12},{1,1},{5,9},{9,5},{13,13},{2,2},{6,10},{... | collective-permute-start | bytes 823304 | tf_op jit(solution)/shard_map/ppermute | solution.py:517
  16.3 3.9 %collective-permute-start.6 = (bf16[1072,128]{1,0:T(8,128)(2,1)S(1)}, bf16[1072,128]{1,0:T(8,128)(2,1)S(1)}, u32[]{:S(2)}, u32[]{:S(2)}) collective-permute-start(bf16[1072,128]{1,0:T(8,128)(2,1)S(1)} %get-tuple-element.30.far_ref), channel_id=1, source_target_pairs={{0,8},{12,4},{4,0},{8,12},{1,9},{13,5},{5,1},{9,13},{2,10},{14,6},... | collective-permute-start | bytes 823304 | tf_op jit(solution)/shard_map/ppermute | solution.py:518
  20.2 0.0 collective-permute-done.4.came_ref.first_ref
  20.2 1.8 %collective-permute-start.7 = (bf16[1072,128]{1,0:T(8,128)(2,1)S(1)}, bf16[1072,128]{1,0:T(8,128)(2,1)S(1)}, u32[]{:S(2)}, u32[]{:S(2)}) collective-permute-start(bf16[1072,128]{1,0:T(8,128)(2,1)S(1)} %combine.1), channel_id=1, source_target_pairs={{0,4},{4,12},{8,0},{12,8},{1,5},{5,13},{9,1},{13,9},{2,6},{6,14},{... | collective-permute-start | bytes 823304 | tf_op jit(solution)/shard_map/ppermute | solution.py:520
  22.1 0.0 collective-permute-start.8
  22.1 0.9 %collective-permute-start.9 = (bf16[256,128]{1,0:T(8,128)(2,1)S(1)}, bf16[256,128]{1,0:T(8,128)(2,1)S(1)}, u32[]{:S(2)}, u32[]{:S(2)}) collective-permute-start(bf16[256,128]{1,0:T(8,128)(2,1)S(1)} %get-tuple-element.33), channel_id=1, source_target_pairs={{0,2},{1,3},{2,0},{3,1},{4,6},{5,7},{6,4},{7,5},{8,10},{9,11},{10,... | collective-permute-start | bytes 196616 | tf_op jit(solution)/shard_map/ppermute | solution.py:497
  23.0 0.3 collective-permute-done.8.orb_ref
  23.3 0.7 %collective-permute-start.10 = (bf16[256,128]{1,0:T(8,128)(2,1)S(1)}, bf16[256,128]{1,0:T(8,128)(2,1)S(1)}, u32[]{:S(2)}, u32[]{:S(2)}) collective-permute-start(bf16[256,128]{1,0:T(8,128)(2,1)S(1)} %get-tuple-element.34), channel_id=1, source_target_pairs={{0,3},{1,2},{2,1},{3,0},{4,7},{5,6},{6,5},{7,4},{8,11},{9,10},{10,... | collective-permute-start | bytes 196616 | tf_op jit(solution)/shard_map/ppermute | solution.py:497
  24.0 2.9 %collective-permute-done.9.walk_ref = bf16[256,128]{1,0:T(8,128)(2,1)S(1)} collective-permute-done((bf16[256,128]{1,0:T(8,128)(2,1)S(1)}, bf16[256,128]{1,0:T(8,128)(2,1)S(1)}, u32[]{:S(2)}, u32[]{:S(2)}) %collective-permute-start.9) | collective-permute-done | bytes 65568 | tf_op jit(solution)/shard_map/ppermute | solution.py:497
  26.8 0.9 %collective-permute-done.10.far_ref = bf16[256,128]{1,0:T(8,128)(2,1)S(1)} collective-permute-done((bf16[256,128]{1,0:T(8,128)(2,1)S(1)}, bf16[256,128]{1,0:T(8,128)(2,1)S(1)}, u32[]{:S(2)}, u32[]{:S(2)}) %collective-permute-start.10) | collective-permute-done | bytes 65568 | tf_op jit(solution)/shard_map/ppermute | solution.py:497
  27.7 0.0 collective-permute-done.5.inside_ref
  27.7 0.0 collective-permute-done.6.cross_ref
  27.7 9.6 %collective-permute-done.7.last_ref = bf16[1072,128]{1,0:T(8,128)(2,1)S(1)} collective-permute-done((bf16[1072,128]{1,0:T(8,128)(2,1)S(1)}, bf16[1072,128]{1,0:T(8,128)(2,1)S(1)}, u32[]{:S(2)}, u32[]{:S(2)}) %collective-permute-start.7) | collective-permute-done | bytes 274464 | tf_op jit(solution)/shard_map/ppermute | solution.py:520
  37.3 2.4 %taylor.1 = (bf16[256,128]{1,0:T(8,128)(2,1)S(1)}, bf16[256,128]{1,0:T(8,128)(2,1)S(1)}, f32[1,8]{1,0:T(1,128)S(1)}) custom-call(f32[24,8]{1,0:T(8,128)S(1)} %get-tuple-element.21.own_ref.pack_ref, f32[16,1]{1,0:T(8,128)S(1)} %get-tuple-element.24.log_ref, bf16[1072,128]{1,0:T(8,128)(2,1)S(1)} %get-tuple-element.27.kept_ref, ...), custom_call_target="tpu_custom_call" | custom-call | tf_op jit(solution)/shard_map/taylor/pallas_call | solution.py:441
  39.7 2.7 %collective-permute-start.16 = (bf16[256,128]{1,0:T(8,128)(2,1)S(1)}, bf16[256,128]{1,0:T(8,128)(2,1)S(1)}, u32[]{:S(2)}, u32[]{:S(2)}) collective-permute-start(bf16[256,128]{1,0:T(8,128)(2,1)S(1)} %get-tuple-element.35.refs_0_), channel_id=1, source_target_pairs={{0,12},{1,13},{4,8},{5,9},{8,4},{9,5},{12,0},{13,1},{2,14},{3,15},... | collective-permute-start | bytes 196616 | tf_op jit(solution)/shard_map/ppermute | solution.py:497
  42.4 0.0 collective-permute-start.14
  42.4 1.8 %collective-permute-start.12 = (bf16[256,128]{1,0:T(8,128)(2,1)S(1)}, bf16[256,128]{1,0:T(8,128)(2,1)S(1)}, u32[]{:S(2)}, u32[]{:S(2)}) collective-permute-start(bf16[256,128]{1,0:T(8,128)(2,1)S(1)} %get-tuple-element.35.refs_0_), channel_id=1, source_target_pairs={{0,4},{1,5},{4,0},{5,1},{8,12},{9,13},{12,8},{13,9},{2,6},{3,7},{6... | collective-permute-start | bytes 196616 | tf_op jit(solution)/shard_map/ppermute | solution.py:497
  44.2 0.2 collective-permute-start.17
  44.4 1.2 %collective-permute-start.15 = (bf16[256,128]{1,0:T(8,128)(2,1)S(1)}, bf16[256,128]{1,0:T(8,128)(2,1)S(1)}, u32[]{:S(2)}, u32[]{:S(2)}) collective-permute-start(bf16[256,128]{1,0:T(8,128)(2,1)S(1)} %get-tuple-element.36), channel_id=1, source_target_pairs={{0,9},{1,8},{4,13},{5,12},{8,1},{9,0},{12,5},{13,4},{2,11},{3,10},... | collective-permute-start | bytes 196616 | tf_op jit(solution)/shard_map/ppermute | solution.py:497
  45.6 0.4 collective-permute-done.16.refs_6_
  46.1 1.0 %collective-permute-start.13 = (bf16[256,128]{1,0:T(8,128)(2,1)S(1)}, bf16[256,128]{1,0:T(8,128)(2,1)S(1)}, u32[]{:S(2)}, u32[]{:S(2)}) collective-permute-start(bf16[256,128]{1,0:T(8,128)(2,1)S(1)} %get-tuple-element.36), channel_id=1, source_target_pairs={{0,5},{1,4},{4,1},{5,0},{8,13},{9,12},{12,9},{13,8},{2,7},{3,6},{6... | collective-permute-start | bytes 196616 | tf_op jit(solution)/shard_map/ppermute | solution.py:497
  47.1 1.5 %collective-permute-done.14.refs_4_ = bf16[256,128]{1,0:T(8,128)(2,1)S(1)} collective-permute-done((bf16[256,128]{1,0:T(8,128)(2,1)S(1)}, bf16[256,128]{1,0:T(8,128)(2,1)S(1)}, u32[]{:S(2)}, u32[]{:S(2)}) %collective-permute-start.14) | collective-permute-done | bytes 65568 | tf_op jit(solution)/shard_map/ppermute | solution.py:497
  48.6 0.0 collective-permute-start.11
  48.6 0.0 collective-permute-done.12.refs_2_
  48.6 1.9 %collective-permute-done.17.refs_7_ = bf16[256,128]{1,0:T(8,128)(2,1)S(1)} collective-permute-done((bf16[256,128]{1,0:T(8,128)(2,1)S(1)}, bf16[256,128]{1,0:T(8,128)(2,1)S(1)}, u32[]{:S(2)}, u32[]{:S(2)}) %collective-permute-start.17) | collective-permute-done | bytes 65568 | tf_op jit(solution)/shard_map/ppermute | solution.py:497
  50.5 2.3 %collective-permute-done.15.refs_5_ = bf16[256,128]{1,0:T(8,128)(2,1)S(1)} collective-permute-done((bf16[256,128]{1,0:T(8,128)(2,1)S(1)}, bf16[256,128]{1,0:T(8,128)(2,1)S(1)}, u32[]{:S(2)}, u32[]{:S(2)}) %collective-permute-start.15) | collective-permute-done | bytes 65568 | tf_op jit(solution)/shard_map/ppermute | solution.py:497
  52.8 0.0 collective-permute-done.13.refs_3_
  52.8 0.0 collective-permute-done.11.refs_1_
  52.8 0.9 %place.1 = (bf16[8,256,128]{2,1,0:T(8,128)(2,1)}, f32[1,8]{1,0:T(1,128)}) custom-call(bf16[256,128]{1,0:T(8,128)(2,1)S(1)} %get-tuple-element.35.refs_0_, bf16[256,128]{1,0:T(8,128)(2,1)S(1)} %collective-permute-done.11.refs_1_, bf16[256,128]{1,0:T(8,128)(2,1)S(1)} %collective-permute-done.12.refs_2_, bf16[256,128]{1,0:T(8,128)(2,1)S(1)} %collective-permute-done.13.refs_3_, ...), custom_call_target="tpu_custom_call" | custom-call | tf_op jit(solution)/shard_map/place/pallas_call | solution.py:478
  (1 shorter events, 0.0 us)
Async XLA Ops:
  4.9 6.8 %collective-permute-start.3 = (bf16[8,256,256]{2,1,0:T(8,128)(2,1)S(1)}, bf16[8,256,256]{2,1,0:T(8,128)(2,1)S(1)}, u32[]{:S(2)}, u32[]{:S(2)}) collective-permute-start(bf16[8,256,256]{2,1,0:T(8,128)(2,1)S(1)} %get-tuple-element.23), channel_id=1, source_target_pairs={{0,1},{1,0},{2,3},{3,2},{4,5},{5,4},{6,7},{7,6},{8,9},{9,8},{10,11... | collective-permute-start | bytes 3145736 | tf_op jit(solution)/shard_map/ppermute | solution.py:497
  5.5 4.0 %collective-permute-start.2 = (f32[24,8]{1,0:T(8,128)S(1)}, f32[24,8]{1,0:T(8,128)S(1)}, u32[]{:S(2)}, u32[]{:S(2)}) collective-permute-start(f32[24,8]{1,0:T(8,128)S(1)} %get-tuple-element.21.own_ref.pack_ref), channel_id=1, source_target_pairs={{0,3},{1,2},{2,1},{3,0},{4,7},{5,6},{6,5},{7,4},{8,11},{9,10},{10,... | collective-permute-start | bytes 2312 | tf_op jit(solution)/shard_map/ppermute | solution.py:497
  8.1 3.7 %collective-permute-start.1 = (f32[24,8]{1,0:T(8,128)S(1)}, f32[24,8]{1,0:T(8,128)S(1)}, u32[]{:S(2)}, u32[]{:S(2)}) collective-permute-start(f32[24,8]{1,0:T(8,128)S(1)} %get-tuple-element.21.own_ref.pack_ref), channel_id=1, source_target_pairs={{0,2},{1,3},{2,0},{3,1},{4,6},{5,7},{6,4},{7,5},{8,10},{9,11},{10,... | collective-permute-start | bytes 2312 | tf_op jit(solution)/shard_map/ppermute | solution.py:497
  8.1 3.7 %collective-permute-start = (f32[24,8]{1,0:T(8,128)S(1)}, f32[24,8]{1,0:T(8,128)S(1)}, u32[]{:S(2)}, u32[]{:S(2)}) collective-permute-start(f32[24,8]{1,0:T(8,128)S(1)} %get-tuple-element.21.own_ref.pack_ref), channel_id=1, source_target_pairs={{0,1},{1,0},{2,3},{3,2},{4,5},{5,4},{6,7},{7,6},{8,9},{9,8},{10,11... | collective-permute-start | bytes 2312 | tf_op jit(solution)/shard_map/ppermute | solution.py:497
  12.6 7.6 %collective-permute-start.4 = (bf16[1072,128]{1,0:T(8,128)(2,1)S(1)}, bf16[1072,128]{1,0:T(8,128)(2,1)S(1)}, u32[]{:S(2)}, u32[]{:S(2)}) collective-permute-start(bf16[1072,128]{1,0:T(8,128)(2,1)S(1)} %get-tuple-element.28), channel_id=1, source_target_pairs={{0,4},{1,5},{4,0},{5,1},{8,12},{9,13},{12,8},{13,9},{2,6},{3,7},{6... | collective-permute-start | bytes 823304 | tf_op jit(solution)/shard_map/ppermute | solution.py:497
  15.7 12.1 %collective-permute-start.5 = (bf16[1072,128]{1,0:T(8,128)(2,1)S(1)}, bf16[1072,128]{1,0:T(8,128)(2,1)S(1)}, u32[]{:S(2)}, u32[]{:S(2)}) collective-permute-start(bf16[1072,128]{1,0:T(8,128)(2,1)S(1)} %get-tuple-element.29.near_ref), channel_id=1, source_target_pairs={{0,0},{4,8},{8,4},{12,12},{1,1},{5,9},{9,5},{13,13},{2,2},{6,10},{... | collective-permute-start | bytes 823304 | tf_op jit(solution)/shard_map/ppermute | solution.py:517
  16.3 11.4 %collective-permute-start.6 = (bf16[1072,128]{1,0:T(8,128)(2,1)S(1)}, bf16[1072,128]{1,0:T(8,128)(2,1)S(1)}, u32[]{:S(2)}, u32[]{:S(2)}) collective-permute-start(bf16[1072,128]{1,0:T(8,128)(2,1)S(1)} %get-tuple-element.30.far_ref), channel_id=1, source_target_pairs={{0,8},{12,4},{4,0},{8,12},{1,9},{13,5},{5,1},{9,13},{2,10},{14,6},... | collective-permute-start | bytes 823304 | tf_op jit(solution)/shard_map/ppermute | solution.py:518
  20.2 17.0 %collective-permute-start.7 = (bf16[1072,128]{1,0:T(8,128)(2,1)S(1)}, bf16[1072,128]{1,0:T(8,128)(2,1)S(1)}, u32[]{:S(2)}, u32[]{:S(2)}) collective-permute-start(bf16[1072,128]{1,0:T(8,128)(2,1)S(1)} %combine.1), channel_id=1, source_target_pairs={{0,4},{4,12},{8,0},{12,8},{1,5},{5,13},{9,1},{13,9},{2,6},{6,14},{... | collective-permute-start | bytes 823304 | tf_op jit(solution)/shard_map/ppermute | solution.py:520
  22.1 1.3 %collective-permute-start.8 = (bf16[256,128]{1,0:T(8,128)(2,1)S(1)}, bf16[256,128]{1,0:T(8,128)(2,1)S(1)}, u32[]{:S(2)}, u32[]{:S(2)}) collective-permute-start(bf16[256,128]{1,0:T(8,128)(2,1)S(1)} %get-tuple-element.32), channel_id=1, source_target_pairs={{0,1},{1,0},{2,3},{3,2},{4,5},{5,4},{6,7},{7,6},{8,9},{9,8},{10,11... | collective-permute-start | bytes 196616 | tf_op jit(solution)/shard_map/ppermute | solution.py:497
  22.1 4.8 %collective-permute-start.9 = (bf16[256,128]{1,0:T(8,128)(2,1)S(1)}, bf16[256,128]{1,0:T(8,128)(2,1)S(1)}, u32[]{:S(2)}, u32[]{:S(2)}) collective-permute-start(bf16[256,128]{1,0:T(8,128)(2,1)S(1)} %get-tuple-element.33), channel_id=1, source_target_pairs={{0,2},{1,3},{2,0},{3,1},{4,6},{5,7},{6,4},{7,5},{8,10},{9,11},{10,... | collective-permute-start | bytes 196616 | tf_op jit(solution)/shard_map/ppermute | solution.py:497
  23.3 4.4 %collective-permute-start.10 = (bf16[256,128]{1,0:T(8,128)(2,1)S(1)}, bf16[256,128]{1,0:T(8,128)(2,1)S(1)}, u32[]{:S(2)}, u32[]{:S(2)}) collective-permute-start(bf16[256,128]{1,0:T(8,128)(2,1)S(1)} %get-tuple-element.34), channel_id=1, source_target_pairs={{0,3},{1,2},{2,1},{3,0},{4,7},{5,6},{6,5},{7,4},{8,11},{9,10},{10,... | collective-permute-start | bytes 196616 | tf_op jit(solution)/shard_map/ppermute | solution.py:497
  39.7 6.3 %collective-permute-start.16 = (bf16[256,128]{1,0:T(8,128)(2,1)S(1)}, bf16[256,128]{1,0:T(8,128)(2,1)S(1)}, u32[]{:S(2)}, u32[]{:S(2)}) collective-permute-start(bf16[256,128]{1,0:T(8,128)(2,1)S(1)} %get-tuple-element.35.refs_0_), channel_id=1, source_target_pairs={{0,12},{1,13},{4,8},{5,9},{8,4},{9,5},{12,0},{13,1},{2,14},{3,15},... | collective-permute-start | bytes 196616 | tf_op jit(solution)/shard_map/ppermute | solution.py:497
  42.4 6.2 %collective-permute-start.14 = (bf16[256,128]{1,0:T(8,128)(2,1)S(1)}, bf16[256,128]{1,0:T(8,128)(2,1)S(1)}, u32[]{:S(2)}, u32[]{:S(2)}) collective-permute-start(bf16[256,128]{1,0:T(8,128)(2,1)S(1)} %get-tuple-element.35.refs_0_), channel_id=1, source_target_pairs={{0,8},{1,9},{4,12},{5,13},{8,0},{9,1},{12,4},{13,5},{2,10},{3,11},... | collective-permute-start | bytes 196616 | tf_op jit(solution)/shard_map/ppermute | solution.py:497
  42.4 6.2 %collective-permute-start.12 = (bf16[256,128]{1,0:T(8,128)(2,1)S(1)}, bf16[256,128]{1,0:T(8,128)(2,1)S(1)}, u32[]{:S(2)}, u32[]{:S(2)}) collective-permute-start(bf16[256,128]{1,0:T(8,128)(2,1)S(1)} %get-tuple-element.35.refs_0_), channel_id=1, source_target_pairs={{0,4},{1,5},{4,0},{5,1},{8,12},{9,13},{12,8},{13,9},{2,6},{3,7},{6... | collective-permute-start | bytes 196616 | tf_op jit(solution)/shard_map/ppermute | solution.py:497
  44.2 6.3 %collective-permute-start.17 = (bf16[256,128]{1,0:T(8,128)(2,1)S(1)}, bf16[256,128]{1,0:T(8,128)(2,1)S(1)}, u32[]{:S(2)}, u32[]{:S(2)}) collective-permute-start(bf16[256,128]{1,0:T(8,128)(2,1)S(1)} %get-tuple-element.36), channel_id=1, source_target_pairs={{0,13},{1,12},{4,9},{5,8},{8,5},{9,4},{12,1},{13,0},{2,15},{3,14},... | collective-permute-start | bytes 196616 | tf_op jit(solution)/shard_map/ppermute | solution.py:497
  44.4 8.4 %collective-permute-start.15 = (bf16[256,128]{1,0:T(8,128)(2,1)S(1)}, bf16[256,128]{1,0:T(8,128)(2,1)S(1)}, u32[]{:S(2)}, u32[]{:S(2)}) collective-permute-start(bf16[256,128]{1,0:T(8,128)(2,1)S(1)} %get-tuple-element.36), channel_id=1, source_target_pairs={{0,9},{1,8},{4,13},{5,12},{8,1},{9,0},{12,5},{13,4},{2,11},{3,10},... | collective-permute-start | bytes 196616 | tf_op jit(solution)/shard_map/ppermute | solution.py:497
  46.1 6.7 %collective-permute-start.13 = (bf16[256,128]{1,0:T(8,128)(2,1)S(1)}, bf16[256,128]{1,0:T(8,128)(2,1)S(1)}, u32[]{:S(2)}, u32[]{:S(2)}) collective-permute-start(bf16[256,128]{1,0:T(8,128)(2,1)S(1)} %get-tuple-element.36), channel_id=1, source_target_pairs={{0,5},{1,4},{4,1},{5,0},{8,13},{9,12},{12,9},{13,8},{2,7},{3,6},{6... | collective-permute-start | bytes 196616 | tf_op jit(solution)/shard_map/ppermute | solution.py:497
  48.6 4.2 %collective-permute-start.11 = (bf16[256,128]{1,0:T(8,128)(2,1)S(1)}, bf16[256,128]{1,0:T(8,128)(2,1)S(1)}, u32[]{:S(2)}, u32[]{:S(2)}) collective-permute-start(bf16[256,128]{1,0:T(8,128)(2,1)S(1)} %get-tuple-element.36), channel_id=1, source_target_pairs={{0,1},{1,0},{4,5},{5,4},{8,9},{9,8},{12,13},{13,12},{2,3},{3,2},{6... | collective-permute-start | bytes 196616 | tf_op jit(solution)/shard_map/ppermute | solution.py:497

commit v6 on v5

--- a/solution.py
+++ b/solution.py
@@ -102,10 +102,14 @@
     columns = pl.ds(pl.multiple_of(lax.axis_index("orb") * n_rows, n_rows), n_rows)
     lane = lax.broadcasted_iota(jnp.int32, (n_walk, n_vec), 1)
     total = jnp.zeros((n_walk, n_vec), jnp.float32)
+    vec_copies[0].wait()
+    ahead = mm(vec_ref[0], trial)
     for g in range(n_vec):
-        vec_copies[g].wait()
+        mixed = ahead.astype(jnp.bfloat16).astype(jnp.float32)
+        if g + 1 < n_vec:
+            vec_copies[g + 1].wait()
+            ahead = mm(vec_ref[g + 1], trial)
         quad_ref[g] = vec_ref[g, :, columns]
-        mixed = mm(vec_ref[g], trial).astype(jnp.bfloat16).astype(jnp.float32)
         rows = [jnp.sum(green_ref[w] * mixed, axis=0, keepdims=True) for w in range(n_walk)]
         column = jnp.sum(jnp.concatenate(rows, axis=0), axis=1, keepdims=True)
         total = total + jnp.where(lane == g, column, 0.0)
@@ -255,13 +259,12 @@
     return inner, first, crossing, nearby
 
 
-def first_kernel(n_o, own_ref, orb_ref, walk_ref, far_ref, here_ref, mate_ref,
-                 piece_ref, weight_ref, split_ref, log_ref):
+def first_kernel(n_o, own_ref, walk_ref, here_ref, mate_ref,
+                 first_ref, near_ref, weight_ref, split_ref, log_ref):
     n_walk = own_ref.shape[0] // 3
     z, x, o = lax.axis_index("vec"), lax.axis_index("walk"), lax.axis_index("orb")
     bias = jnp.concatenate(
-        [own_ref[pl.ds(0, n_walk), :] + orb_ref[pl.ds(0, n_walk), :],
-         walk_ref[pl.ds(0, n_walk), :] + far_ref[pl.ds(0, n_walk), :]], axis=0
+        [own_ref[pl.ds(0, n_walk), :], walk_ref[pl.ds(0, n_walk), :]], axis=0
     )
     aux = jnp.concatenate([own_ref[pl.ds(n_walk, n_walk), :], walk_ref[pl.ds(n_walk, n_walk), :]], axis=0)
     shift = -step_root * bias
@@ -271,7 +274,7 @@
     _, first, crossing, nearby = routes(z)
     k_at = lax.broadcasted_iota(jnp.int32, (8, n_walk), 0)
     lane = lax.broadcasted_iota(jnp.int32, (8, n_walk), 1)
-    to_z = jnp.where(k_at == 0, first, jnp.where(k_at == 1, crossing, jnp.where(k_at == 2, nearby, z)))
+    to_z = jnp.where(k_at == 0, first, jnp.where(k_at == 1, nearby, jnp.where(k_at == 2, crossing, z)))
     sources = jnp.sum(
         jnp.where(lane == to_z * n_o + o, jnp.broadcast_to(copies_of(own_ref), lane.shape), 0.0),
         axis=1, keepdims=True,
@@ -280,7 +283,7 @@
     pick = lax.broadcasted_iota(jnp.int32, (8, 2 * n_walk), 1) == row
     weights = mm(pick.astype(jnp.float32).astype(jnp.bfloat16), weighted)
     weight_ref[...] = weights
-    fill_pieces(weights, here_ref, mate_ref, [piece_ref], split, o)
+    fill_pieces(weights, here_ref, mate_ref, [first_ref, near_ref], split, o)
     square = (n_walk, n_walk)
     eye = lax.broadcasted_iota(jnp.int32, square, 0) == lax.broadcasted_iota(jnp.int32, square, 1)
     for side, ref in enumerate((own_ref, walk_ref)):
@@ -289,25 +292,41 @@
         )
 
 
-def first_piece(packs, here, mate, n_o):
+def sum_kernel(own_ref, orb_ref, out_ref):
+    n_walk = own_ref.shape[0] // 3
+    out_ref[...] = own_ref[...]
+    out_ref[pl.ds(0, n_walk), :] = own_ref[pl.ds(0, n_walk), :] + orb_ref[pl.ds(0, n_walk), :]
+
+
+def summed_pack(own, orb):
+    return pl.pallas_call(
+        sum_kernel,
+        out_shape=VMEM(own.shape, own.dtype),
+        in_specs=[in_vmem()] * 2,
+        out_specs=in_vmem(),
+        compiler_params=pltpu.CompilerParams(vmem_limit_bytes=VMEM_LIMIT),
+        name="summed_pack",
+    )(*on_chip(own, orb))
+
+
+def first_pieces(packs, here, mate, n_o):
     n_walk, n_vec = packs[0].shape[0] // 3, packs[0].shape[1]
     return pl.pallas_call(
         partial(first_kernel, n_o),
-        out_shape=[
-            VMEM((layout(here.shape[2] // LANE, 2 * n_walk)["end"], LANE), jnp.bfloat16),
+        out_shape=[VMEM((layout(here.shape[2] // LANE, 2 * n_walk)["end"], LANE), jnp.bfloat16)] * 2 + [
             VMEM((8, n_vec), jnp.float32),
             VMEM((2 * n_walk, LANE), jnp.bfloat16),
             VMEM((2 * n_walk, 1), jnp.float32),
         ],
-        in_specs=[in_vmem()] * 6,
-        out_specs=[in_vmem()] * 4,
+        in_specs=[in_vmem()] * 4,
+        out_specs=[in_vmem()] * 5,
         compiler_params=pltpu.CompilerParams(vmem_limit_bytes=VMEM_LIMIT),
         name="first_piece",
     )(*on_chip(*packs, here, mate))
 
 
 def other_kernel(n_o, own_ref, walk_ref, weight_ref, split_ref, here_ref, mate_ref, walkers_hbm, *refs):
-    pieces, sources, sems = refs[:3], refs[3:7], refs[7]
+    pieces, sources, sems = refs[:2], refs[2:6], refs[6]
     n_walk = walkers_hbm.shape[0]
     z, o = lax.axis_index("vec"), lax.axis_index("orb")
     slot, mate = z * n_o + o, z * n_o + (n_o - 1 - o)
@@ -319,7 +338,7 @@
     ]
     for copy in copies:
         copy.start()
-    fill_pieces(weight_ref[...][1:4], here_ref, mate_ref, pieces, split_ref[...], o)
+    fill_pieces(weight_ref[...][2:4], here_ref, mate_ref, pieces, split_ref[...], o)
     for copy in copies:
         copy.wait()
 
@@ -330,9 +349,9 @@
     source = VMEM(walkers.shape[1:], walkers.dtype)
     return pl.pallas_call(
         partial(other_kernel, n_o),
-        out_shape=[piece] * 3 + [source] * 4,
+        out_shape=[piece] * 2 + [source] * 4,
         in_specs=[in_vmem()] * 6 + [in_hbm()],
-        out_specs=[in_vmem()] * 7,
+        out_specs=[in_vmem()] * 6,
         scratch_shapes=[pltpu.SemaphoreType.DMA((4,))],
         compiler_params=pltpu.CompilerParams(vmem_limit_bytes=VMEM_LIMIT),
         name="other_pieces",
@@ -505,16 +524,17 @@
     own_pack, here, quadrant = partial_bias_of(
         aux_field, log_weight, copy_list, walkers, inv_intersection, trial, vectors
     )
-    packs = [own_pack]
-    for m in others:
-        packs.append(near(own_pack, masks=m))
+    orb_pack = near(own_pack, masks=(0, 1))
+    own_pack = summed_pack(own_pack, orb_pack)
+    walk_pack = near(own_pack, masks=(1, 0))
+    packs = [own_pack, walk_pack]
     mate = near(quadrant, masks=(0, 1))
-    piece, weights, split, log_column = first_piece(packs, here, mate, n_o)
+    piece, nearby, weights, split, log_column = first_pieces(packs, here, mate, n_o)
     came = line(piece, masks=(1, 0))
-    crossing, nearby, kept, *sources = other_pieces(
-        own_pack, packs[2], weights, split, here, mate, walkers, n_o
-    )
     inside = lax.ppermute(nearby, "vec", [(0, 0), (1, 2), (2, 1), (3, 3)])
+    crossing, kept, *sources = other_pieces(
+        own_pack, walk_pack, weights, split, here, mate, walkers, n_o
+    )
     crossed = lax.ppermute(crossing, "vec", [(0, 2), (3, 1), (1, 0), (2, 3)])
     passed = combined(crossing, nearby, came, split.shape[0])
     last = lax.ppermute(passed, "vec", [(0, 1), (1, 3), (2, 0), (3, 2)])

time: 53.9 us -> 54.9 us (1.019)
  waiting for transfers between devices: 23.3 us -> 25.5 us
  Pallas kernels: 9.85 us -> 9.27 us
    ppermute x15 -> x14, waiting for transfers between devices: 13.8 us -> 17.4 us  [swapped(): return lax.ppermute(value, axes, perm)]
    ppermute x1, waiting for transfers between devices: 9.56 us -> 8.03 us  [slot_device(): last = lax.ppermute(passed, 'vec', [(0, 1), (1, 3), (2, 0), (3, 2)])]
    ppermute x1, starting transfers between devices: 3.87 us -> 2.59 us  [slot_device(): crossed = lax.ppermute(crossing, 'vec', [(0, 2), (3, 1), (1, 0), (2, 3)])]
    pallas_call x1, Pallas kernels: 4.29 us -> 3.56 us  [partial_bias_of(): pl.pallas_call(bias_kernel, out_shape=[VMEM((3 * n_walk, n_vec), jnp.floa...]
    ppermute x15 -> x14, starting transfers between devices: 13.4 us -> 13.8 us  [swapped(): return lax.ppermute(value, axes, perm)]
    pallas_call x2 -> x3, Pallas kernels: 2.24 us -> 2.38 us  [the longest x1 1.21 us: first_pieces(): pl.pallas_call(partial(first_kernel, n_o), out_shape=[VMEM((layout(here.s...]
  transfers between devices with their start and end apart: 18 -> 17, of which waited for: 10 -> 10; matrix products, arithmetic and copies ran while one was open for 0% -> 0% of each run, Pallas kernels for 3% -> 2%
where the time goes in v6:
time: 54.9 us; the launch traced here: 54.7 us
  waiting for transfers between devices  25.5 us (46%)
  starting transfers between devices  19.3 us (35%)
  Pallas kernels  9.27 us (17%)
  between operations  0.68 us (1%)
    ppermute x14, waiting for transfers between devices, swapped(): return lax.ppermute(value, axes, perm)  17.4 us
    ppermute x14, starting transfers between devices, swapped(): return lax.ppermute(value, axes, perm)  13.8 us
    ppermute x1, waiting for transfers between devices, slot_device(): last = lax.ppermute(passed, 'vec', [(0, 1), (1, 3), (2, 0), (3, 2)])  8.03 us
    pallas_call x1, Pallas kernels, partial_bias_of(): pl.pallas_call(bias_kernel, out_shape=[VMEM((3 * n_walk, n_vec), jnp.floa...  3.56 us
    ppermute x1, starting transfers between devices, slot_device(): crossed = lax.ppermute(crossing, 'vec', [(0, 2), (3, 1), (1, 0), (2, 3)])  2.59 us
    pallas_call x1, Pallas kernels, taylor(): pl.pallas_call(partial(taylor_kernel, n_o), out_shape=[out, out, VMEM((1,...  2.45 us
    ppermute x1, starting transfers between devices, slot_device(): last = lax.ppermute(passed, 'vec', [(0, 1), (1, 3), (2, 0), (3, 2)])  2.2 us
    pallas_call x1, Pallas kernels, first_pieces(): pl.pallas_call(partial(first_kernel, n_o), out_shape=[VMEM((layout(here.s...  1.21 us
  transfers between devices with their start and end apart: 17, of which 10 were waited for; matrix products, arithmetic and copies ran while one was open for 0% of the time, Pallas kernels for 2%

profile of v6, /device:TPU:0, one launch (start us, length us, event | category | flops | bytes accessed | tf_op | source)
XLA Modules:
  0.0 54.7 jit_solution(15674818256718037450)
XLA Ops:
  0.6 3.6 %bias.1 = (f32[24,8]{1,0:T(8,128)S(1)}, bf16[8,256,512]{2,1,0:T(8,128)(2,1)S(1)}, bf16[8,256,256]{2,1,0:T(8,128)(2,1)S(1)}) custom-call(f32[8,8]{1,0:T(8,128)} %aux_hbm.1, f32[1,8]{1,0:T(1,128)} %bitcast.3, s32[1,8]{1,0:T(1,128)} %bitcast.4, bf16[8,256,128]{2,1,0:T(8,128)(2,1)} %walkers_hbm.3, bf16[8,128,128]{2,1,0:T(8,128)(2,1)} %inv_hbm.1, ...), custom_call_target="tpu_custom_call" | custom-call | tf_op jit(solution)/shard_map/bias/pallas_call | solution.py:128
  4.2 0.6 %collective-permute-start.2 = (bf16[8,256,256]{2,1,0:T(8,128)(2,1)S(1)}, bf16[8,256,256]{2,1,0:T(8,128)(2,1)S(1)}, u32[]{:S(2)}, u32[]{:S(2)}) collective-permute-start(bf16[8,256,256]{2,1,0:T(8,128)(2,1)S(1)} %get-tuple-element.23), channel_id=1, source_target_pairs={{0,1},{1,0},{2,3},{3,2},{4,5},{5,4},{6,7},{7,6},{8,9},{9,8},{10,11... | collective-permute-start | bytes 3145736 | tf_op jit(solution)/shard_map/ppermute | solution.py:516
  4.8 0.1 collective-permute-start
  4.8 2.2 %collective-permute-done.orb_ref = f32[24,8]{1,0:T(8,128)S(1)} collective-permute-done((f32[24,8]{1,0:T(8,128)S(1)}, f32[24,8]{1,0:T(8,128)S(1)}, u32[]{:S(2)}, u32[]{:S(2)}) %collective-permute-start) | collective-permute-done | bytes 800 | tf_op jit(solution)/shard_map/ppermute | solution.py:516
  7.1 2.9 %collective-permute-start.1 = (f32[24,8]{1,0:T(8,128)S(1)}, f32[24,8]{1,0:T(8,128)S(1)}, u32[]{:S(2)}, u32[]{:S(2)}) collective-permute-start(f32[24,8]{1,0:T(8,128)S(1)} %summed_pack.1.own_ref.pack_ref), channel_id=1, source_target_pairs={{0,2},{1,3},{2,0},{3,1},{4,6},{5,7},{6,4},{7,5},{8,10},{9,11},{10,... | collective-permute-start | bytes 2312 | tf_op jit(solution)/shard_map/ppermute | solution.py:516
  9.9 1.7 %collective-permute-done.1.walk_ref = f32[24,8]{1,0:T(8,128)S(1)} collective-permute-done((f32[24,8]{1,0:T(8,128)S(1)}, f32[24,8]{1,0:T(8,128)S(1)}, u32[]{:S(2)}, u32[]{:S(2)}) %collective-permute-start.1) | collective-permute-done | bytes 800 | tf_op jit(solution)/shard_map/ppermute | solution.py:516
  11.6 0.0 collective-permute-done.2.mate_ref
  11.6 1.2 %first_piece.1 = (bf16[1072,128]{1,0:T(8,128)(2,1)S(1)}, bf16[1072,128]{1,0:T(8,128)(2,1)S(1)}, f32[8,8]{1,0:T(8,128)S(1)}, bf16[16,128]{1,0:T(8,128)(2,1)S(1)}, f32[16,1]{1,0:T(8,128)S(1)}) custom-call(f32[24,8]{1,0:T(8,128)S(1)} %summed_pack.1.own_ref.pack_ref, f32[24,8]{1,0:T(8,128)S(1)} %collective-permute-done.1.walk_ref, ...), custom_call_target="tpu_custom_call" | custom-call | tf_op jit(solution)/shard_map/first_piece/pallas_call | solution.py:314
  12.8 2.2 %collective-permute-start.3 = (bf16[1072,128]{1,0:T(8,128)(2,1)S(1)}, bf16[1072,128]{1,0:T(8,128)(2,1)S(1)}, u32[]{:S(2)}, u32[]{:S(2)}) collective-permute-start(bf16[1072,128]{1,0:T(8,128)(2,1)S(1)} %get-tuple-element.28), channel_id=1, source_target_pairs={{0,4},{1,5},{4,0},{5,1},{8,12},{9,13},{12,8},{13,9},{2,6},{3,7},{6... | collective-permute-start | bytes 823304 | tf_op jit(solution)/shard_map/ppermute | solution.py:516
  15.0 1.2 %other_pieces.1 = (bf16[1072,128]{1,0:T(8,128)(2,1)S(1)}, bf16[1072,128]{1,0:T(8,128)(2,1)S(1)}, bf16[256,128]{1,0:T(8,128)(2,1)S(1)}, bf16[256,128]{1,0:T(8,128...) custom-call(f32[24,8]{1,0:T(8,128)S(1)} %summed_pack.1.own_ref.pack_ref, ...), custom_call_target="tpu_custom_call" | custom-call | tf_op jit(solution)/shard_map/other_pieces/pallas_call | solution.py:350
  16.1 2.6 %collective-permute-start.5 = (bf16[1072,128]{1,0:T(8,128)(2,1)S(1)}, bf16[1072,128]{1,0:T(8,128)(2,1)S(1)}, u32[]{:S(2)}, u32[]{:S(2)}) collective-permute-start(bf16[1072,128]{1,0:T(8,128)(2,1)S(1)} %get-tuple-element.30.far_ref), channel_id=1, source_target_pairs={{0,8},{12,4},{4,0},{8,12},{1,9},{13,5},{5,1},{9,13},{2,10},{14,6},... | collective-permute-start | bytes 823304 | tf_op jit(solution)/shard_map/ppermute | solution.py:538
  18.7 0.7 %collective-permute-start.4 = (bf16[1072,128]{1,0:T(8,128)(2,1)S(1)}, bf16[1072,128]{1,0:T(8,128)(2,1)S(1)}, u32[]{:S(2)}, u32[]{:S(2)}) collective-permute-start(bf16[1072,128]{1,0:T(8,128)(2,1)S(1)} %get-tuple-element.29.near_ref), channel_id=1, source_target_pairs={{0,0},{4,8},{8,4},{12,12},{1,1},{5,9},{9,5},{13,13},{2,2},{6,10},{... | collective-permute-start | bytes 823304 | tf_op jit(solution)/shard_map/ppermute | solution.py:534
  19.4 3.0 %collective-permute-done.3.came_ref.first_ref = bf16[1072,128]{1,0:T(8,128)(2,1)S(1)} collective-permute-done((bf16[1072,128]{1,0:T(8,128)(2,1)S(1)}, bf16[1072,128]{1,0:T(8,128)(2,1)S(1)}, u32[]{:S(2)}, u32[]{:S(2)}) %collective-permute-start.3) | collective-permute-done | bytes 274464 | tf_op jit(solution)/shard_map/ppermute | solution.py:516
  22.4 2.2 %collective-permute-start.6 = (bf16[1072,128]{1,0:T(8,128)(2,1)S(1)}, bf16[1072,128]{1,0:T(8,128)(2,1)S(1)}, u32[]{:S(2)}, u32[]{:S(2)}) collective-permute-start(bf16[1072,128]{1,0:T(8,128)(2,1)S(1)} %combine.1), channel_id=1, source_target_pairs={{0,4},{4,12},{8,0},{12,8},{1,5},{5,13},{9,1},{13,9},{2,6},{6,14},{... | collective-permute-start | bytes 823304 | tf_op jit(solution)/shard_map/ppermute | solution.py:540
  24.6 0.0 collective-permute-start.7
  24.6 1.5 %collective-permute-start.8 = (bf16[256,128]{1,0:T(8,128)(2,1)S(1)}, bf16[256,128]{1,0:T(8,128)(2,1)S(1)}, u32[]{:S(2)}, u32[]{:S(2)}) collective-permute-start(bf16[256,128]{1,0:T(8,128)(2,1)S(1)} %get-tuple-element.33), channel_id=1, source_target_pairs={{0,2},{1,3},{2,0},{3,1},{4,6},{5,7},{6,4},{7,5},{8,10},{9,11},{10,... | collective-permute-start | bytes 196616 | tf_op jit(solution)/shard_map/ppermute | solution.py:516
  26.1 0.0 collective-permute-done.7.orb_ref
  26.1 1.0 %collective-permute-start.9 = (bf16[256,128]{1,0:T(8,128)(2,1)S(1)}, bf16[256,128]{1,0:T(8,128)(2,1)S(1)}, u32[]{:S(2)}, u32[]{:S(2)}) collective-permute-start(bf16[256,128]{1,0:T(8,128)(2,1)S(1)} %get-tuple-element.34), channel_id=1, source_target_pairs={{0,3},{1,2},{2,1},{3,0},{4,7},{5,6},{6,5},{7,4},{8,11},{9,10},{10,... | collective-permute-start | bytes 196616 | tf_op jit(solution)/shard_map/ppermute | solution.py:516
  27.1 2.0 %collective-permute-done.8.walk_ref = bf16[256,128]{1,0:T(8,128)(2,1)S(1)} collective-permute-done((bf16[256,128]{1,0:T(8,128)(2,1)S(1)}, bf16[256,128]{1,0:T(8,128)(2,1)S(1)}, u32[]{:S(2)}, u32[]{:S(2)}) %collective-permute-start.8) | collective-permute-done | bytes 65568 | tf_op jit(solution)/shard_map/ppermute | solution.py:516
  29.1 1.0 %collective-permute-done.9.far_ref = bf16[256,128]{1,0:T(8,128)(2,1)S(1)} collective-permute-done((bf16[256,128]{1,0:T(8,128)(2,1)S(1)}, bf16[256,128]{1,0:T(8,128)(2,1)S(1)}, u32[]{:S(2)}, u32[]{:S(2)}) %collective-permute-start.9) | collective-permute-done | bytes 65568 | tf_op jit(solution)/shard_map/ppermute | solution.py:516
  30.1 0.0 collective-permute-done.5.cross_ref
  30.1 0.0 collective-permute-done.4.inside_ref
  30.1 8.0 %collective-permute-done.6.last_ref = bf16[1072,128]{1,0:T(8,128)(2,1)S(1)} collective-permute-done((bf16[1072,128]{1,0:T(8,128)(2,1)S(1)}, bf16[1072,128]{1,0:T(8,128)(2,1)S(1)}, u32[]{:S(2)}, u32[]{:S(2)}) %collective-permute-start.6) | collective-permute-done | bytes 274464 | tf_op jit(solution)/shard_map/ppermute | solution.py:540
  38.2 2.5 %taylor.1 = (bf16[256,128]{1,0:T(8,128)(2,1)S(1)}, bf16[256,128]{1,0:T(8,128)(2,1)S(1)}, f32[1,8]{1,0:T(1,128)S(1)}) custom-call(f32[24,8]{1,0:T(8,128)S(1)} %summed_pack.1.own_ref.pack_ref, f32[16,1]{1,0:T(8,128)S(1)} %get-tuple-element.24.log_ref, bf16[1072,128]{1,0:T(8,128)(2,1)S(1)} %get-tuple-element.27.kept_ref, ...), custom_call_target="tpu_custom_call" | custom-call | tf_op jit(solution)/shard_map/taylor/pallas_call | solution.py:460
  40.6 2.1 %collective-permute-start.15 = (bf16[256,128]{1,0:T(8,128)(2,1)S(1)}, bf16[256,128]{1,0:T(8,128)(2,1)S(1)}, u32[]{:S(2)}, u32[]{:S(2)}) collective-permute-start(bf16[256,128]{1,0:T(8,128)(2,1)S(1)} %get-tuple-element.35.refs_0_), channel_id=1, source_target_pairs={{0,12},{1,13},{4,8},{5,9},{8,4},{9,5},{12,0},{13,1},{2,14},{3,15},... | collective-permute-start | bytes 196616 | tf_op jit(solution)/shard_map/ppermute | solution.py:516
  42.8 0.0 collective-permute-start.13
  42.8 2.3 %collective-permute-start.11 = (bf16[256,128]{1,0:T(8,128)(2,1)S(1)}, bf16[256,128]{1,0:T(8,128)(2,1)S(1)}, u32[]{:S(2)}, u32[]{:S(2)}) collective-permute-start(bf16[256,128]{1,0:T(8,128)(2,1)S(1)} %get-tuple-element.35.refs_0_), channel_id=1, source_target_pairs={{0,4},{1,5},{4,0},{5,1},{8,12},{9,13},{12,8},{13,9},{2,6},{3,7},{6... | collective-permute-start | bytes 196616 | tf_op jit(solution)/shard_map/ppermute | solution.py:516
  45.1 0.0 collective-permute-start.16
  45.1 1.2 %collective-permute-start.14 = (bf16[256,128]{1,0:T(8,128)(2,1)S(1)}, bf16[256,128]{1,0:T(8,128)(2,1)S(1)}, u32[]{:S(2)}, u32[]{:S(2)}) collective-permute-start(bf16[256,128]{1,0:T(8,128)(2,1)S(1)} %get-tuple-element.36), channel_id=1, source_target_pairs={{0,9},{1,8},{4,13},{5,12},{8,1},{9,0},{12,5},{13,4},{2,11},{3,10},... | collective-permute-start | bytes 196616 | tf_op jit(solution)/shard_map/ppermute | solution.py:516
  46.3 1.3 %collective-permute-done.15.refs_6_ = bf16[256,128]{1,0:T(8,128)(2,1)S(1)} collective-permute-done((bf16[256,128]{1,0:T(8,128)(2,1)S(1)}, bf16[256,128]{1,0:T(8,128)(2,1)S(1)}, u32[]{:S(2)}, u32[]{:S(2)}) %collective-permute-start.15) | collective-permute-done | bytes 65568 | tf_op jit(solution)/shard_map/ppermute | solution.py:516
  47.5 0.0 collective-permute-start.12
  47.5 1.8 %collective-permute-done.13.refs_4_ = bf16[256,128]{1,0:T(8,128)(2,1)S(1)} collective-permute-done((bf16[256,128]{1,0:T(8,128)(2,1)S(1)}, bf16[256,128]{1,0:T(8,128)(2,1)S(1)}, u32[]{:S(2)}, u32[]{:S(2)}) %collective-permute-start.13) | collective-permute-done | bytes 65568 | tf_op jit(solution)/shard_map/ppermute | solution.py:516
  49.3 0.0 collective-permute-start.10
  49.3 0.0 collective-permute-done.11.refs_2_
  49.3 2.1 %collective-permute-done.16.refs_7_ = bf16[256,128]{1,0:T(8,128)(2,1)S(1)} collective-permute-done((bf16[256,128]{1,0:T(8,128)(2,1)S(1)}, bf16[256,128]{1,0:T(8,128)(2,1)S(1)}, u32[]{:S(2)}, u32[]{:S(2)}) %collective-permute-start.16) | collective-permute-done | bytes 65568 | tf_op jit(solution)/shard_map/ppermute | solution.py:516
  51.4 2.5 %collective-permute-done.14.refs_5_ = bf16[256,128]{1,0:T(8,128)(2,1)S(1)} collective-permute-done((bf16[256,128]{1,0:T(8,128)(2,1)S(1)}, bf16[256,128]{1,0:T(8,128)(2,1)S(1)}, u32[]{:S(2)}, u32[]{:S(2)}) %collective-permute-start.14) | collective-permute-done | bytes 65568 | tf_op jit(solution)/shard_map/ppermute | solution.py:516
  53.8 0.0 collective-permute-done.12.refs_3_
  53.8 0.0 collective-permute-done.10.refs_1_
  53.8 0.9 %place.1 = (bf16[8,256,128]{2,1,0:T(8,128)(2,1)}, f32[1,8]{1,0:T(1,128)}) custom-call(bf16[256,128]{1,0:T(8,128)(2,1)S(1)} %get-tuple-element.35.refs_0_, bf16[256,128]{1,0:T(8,128)(2,1)S(1)} %collective-permute-done.10.refs_1_, bf16[256,128]{1,0:T(8,128)(2,1)S(1)} %collective-permute-done.11.refs_2_, bf16[256,128]{1,0:T(8,128)(2,1)S(1)} %collective-permute-done.12.refs_3_, ...), custom_call_target="tpu_custom_call" | custom-call | tf_op jit(solution)/shard_map/place/pallas_call | solution.py:497
  (2 shorter events, 0.0 us)
Async XLA Ops:
  4.2 7.4 %collective-permute-start.2 = (bf16[8,256,256]{2,1,0:T(8,128)(2,1)S(1)}, bf16[8,256,256]{2,1,0:T(8,128)(2,1)S(1)}, u32[]{:S(2)}, u32[]{:S(2)}) collective-permute-start(bf16[8,256,256]{2,1,0:T(8,128)(2,1)S(1)} %get-tuple-element.23), channel_id=1, source_target_pairs={{0,1},{1,0},{2,3},{3,2},{4,5},{5,4},{6,7},{7,6},{8,9},{9,8},{10,11... | collective-permute-start | bytes 3145736 | tf_op jit(solution)/shard_map/ppermute | solution.py:516
  4.8 2.3 %collective-permute-start = (f32[24,8]{1,0:T(8,128)S(1)}, f32[24,8]{1,0:T(8,128)S(1)}, u32[]{:S(2)}, u32[]{:S(2)}) collective-permute-start(f32[24,8]{1,0:T(8,128)S(1)} %get-tuple-element.21.own_ref), channel_id=1, source_target_pairs={{0,1},{1,0},{2,3},{3,2},{4,5},{5,4},{6,7},{7,6},{8,9},{9,8},{10,11... | collective-permute-start | bytes 2312 | tf_op jit(solution)/shard_map/ppermute | solution.py:516
  7.1 4.5 %collective-permute-start.1 = (f32[24,8]{1,0:T(8,128)S(1)}, f32[24,8]{1,0:T(8,128)S(1)}, u32[]{:S(2)}, u32[]{:S(2)}) collective-permute-start(f32[24,8]{1,0:T(8,128)S(1)} %summed_pack.1.own_ref.pack_ref), channel_id=1, source_target_pairs={{0,2},{1,3},{2,0},{3,1},{4,6},{5,7},{6,4},{7,5},{8,10},{9,11},{10,... | collective-permute-start | bytes 2312 | tf_op jit(solution)/shard_map/ppermute | solution.py:516
  12.8 9.6 %collective-permute-start.3 = (bf16[1072,128]{1,0:T(8,128)(2,1)S(1)}, bf16[1072,128]{1,0:T(8,128)(2,1)S(1)}, u32[]{:S(2)}, u32[]{:S(2)}) collective-permute-start(bf16[1072,128]{1,0:T(8,128)(2,1)S(1)} %get-tuple-element.28), channel_id=1, source_target_pairs={{0,4},{1,5},{4,0},{5,1},{8,12},{9,13},{12,8},{13,9},{2,6},{3,7},{6... | collective-permute-start | bytes 823304 | tf_op jit(solution)/shard_map/ppermute | solution.py:516
  16.1 14.0 %collective-permute-start.5 = (bf16[1072,128]{1,0:T(8,128)(2,1)S(1)}, bf16[1072,128]{1,0:T(8,128)(2,1)S(1)}, u32[]{:S(2)}, u32[]{:S(2)}) collective-permute-start(bf16[1072,128]{1,0:T(8,128)(2,1)S(1)} %get-tuple-element.30.far_ref), channel_id=1, source_target_pairs={{0,8},{12,4},{4,0},{8,12},{1,9},{13,5},{5,1},{9,13},{2,10},{14,6},... | collective-permute-start | bytes 823304 | tf_op jit(solution)/shard_map/ppermute | solution.py:538
  18.7 11.4 %collective-permute-start.4 = (bf16[1072,128]{1,0:T(8,128)(2,1)S(1)}, bf16[1072,128]{1,0:T(8,128)(2,1)S(1)}, u32[]{:S(2)}, u32[]{:S(2)}) collective-permute-start(bf16[1072,128]{1,0:T(8,128)(2,1)S(1)} %get-tuple-element.29.near_ref), channel_id=1, source_target_pairs={{0,0},{4,8},{8,4},{12,12},{1,1},{5,9},{9,5},{13,13},{2,2},{6,10},{... | collective-permute-start | bytes 823304 | tf_op jit(solution)/shard_map/ppermute | solution.py:534
  22.4 15.8 %collective-permute-start.6 = (bf16[1072,128]{1,0:T(8,128)(2,1)S(1)}, bf16[1072,128]{1,0:T(8,128)(2,1)S(1)}, u32[]{:S(2)}, u32[]{:S(2)}) collective-permute-start(bf16[1072,128]{1,0:T(8,128)(2,1)S(1)} %combine.1), channel_id=1, source_target_pairs={{0,4},{4,12},{8,0},{12,8},{1,5},{5,13},{9,1},{13,9},{2,6},{6,14},{... | collective-permute-start | bytes 823304 | tf_op jit(solution)/shard_map/ppermute | solution.py:540
  24.6 1.5 %collective-permute-start.7 = (bf16[256,128]{1,0:T(8,128)(2,1)S(1)}, bf16[256,128]{1,0:T(8,128)(2,1)S(1)}, u32[]{:S(2)}, u32[]{:S(2)}) collective-permute-start(bf16[256,128]{1,0:T(8,128)(2,1)S(1)} %get-tuple-element.32), channel_id=1, source_target_pairs={{0,1},{1,0},{2,3},{3,2},{4,5},{5,4},{6,7},{7,6},{8,9},{9,8},{10,11... | collective-permute-start | bytes 196616 | tf_op jit(solution)/shard_map/ppermute | solution.py:516
  24.6 4.5 %collective-permute-start.8 = (bf16[256,128]{1,0:T(8,128)(2,1)S(1)}, bf16[256,128]{1,0:T(8,128)(2,1)S(1)}, u32[]{:S(2)}, u32[]{:S(2)}) collective-permute-start(bf16[256,128]{1,0:T(8,128)(2,1)S(1)} %get-tuple-element.33), channel_id=1, source_target_pairs={{0,2},{1,3},{2,0},{3,1},{4,6},{5,7},{6,4},{7,5},{8,10},{9,11},{10,... | collective-permute-start | bytes 196616 | tf_op jit(solution)/shard_map/ppermute | solution.py:516
  26.1 4.0 %collective-permute-start.9 = (bf16[256,128]{1,0:T(8,128)(2,1)S(1)}, bf16[256,128]{1,0:T(8,128)(2,1)S(1)}, u32[]{:S(2)}, u32[]{:S(2)}) collective-permute-start(bf16[256,128]{1,0:T(8,128)(2,1)S(1)} %get-tuple-element.34), channel_id=1, source_target_pairs={{0,3},{1,2},{2,1},{3,0},{4,7},{5,6},{6,5},{7,4},{8,11},{9,10},{10,... | collective-permute-start | bytes 196616 | tf_op jit(solution)/shard_map/ppermute | solution.py:516
  40.6 6.9 %collective-permute-start.15 = (bf16[256,128]{1,0:T(8,128)(2,1)S(1)}, bf16[256,128]{1,0:T(8,128)(2,1)S(1)}, u32[]{:S(2)}, u32[]{:S(2)}) collective-permute-start(bf16[256,128]{1,0:T(8,128)(2,1)S(1)} %get-tuple-element.35.refs_0_), channel_id=1, source_target_pairs={{0,12},{1,13},{4,8},{5,9},{8,4},{9,5},{12,0},{13,1},{2,14},{3,15},... | collective-permute-start | bytes 196616 | tf_op jit(solution)/shard_map/ppermute | solution.py:516
  42.8 6.5 %collective-permute-start.13 = (bf16[256,128]{1,0:T(8,128)(2,1)S(1)}, bf16[256,128]{1,0:T(8,128)(2,1)S(1)}, u32[]{:S(2)}, u32[]{:S(2)}) collective-permute-start(bf16[256,128]{1,0:T(8,128)(2,1)S(1)} %get-tuple-element.35.refs_0_), channel_id=1, source_target_pairs={{0,8},{1,9},{4,12},{5,13},{8,0},{9,1},{12,4},{13,5},{2,10},{3,11},... | collective-permute-start | bytes 196616 | tf_op jit(solution)/shard_map/ppermute | solution.py:516
  42.8 6.5 %collective-permute-start.11 = (bf16[256,128]{1,0:T(8,128)(2,1)S(1)}, bf16[256,128]{1,0:T(8,128)(2,1)S(1)}, u32[]{:S(2)}, u32[]{:S(2)}) collective-permute-start(bf16[256,128]{1,0:T(8,128)(2,1)S(1)} %get-tuple-element.35.refs_0_), channel_id=1, source_target_pairs={{0,4},{1,5},{4,0},{5,1},{8,12},{9,13},{12,8},{13,9},{2,6},{3,7},{6... | collective-permute-start | bytes 196616 | tf_op jit(solution)/shard_map/ppermute | solution.py:516
  45.1 6.3 %collective-permute-start.16 = (bf16[256,128]{1,0:T(8,128)(2,1)S(1)}, bf16[256,128]{1,0:T(8,128)(2,1)S(1)}, u32[]{:S(2)}, u32[]{:S(2)}) collective-permute-start(bf16[256,128]{1,0:T(8,128)(2,1)S(1)} %get-tuple-element.36), channel_id=1, source_target_pairs={{0,13},{1,12},{4,9},{5,8},{8,5},{9,4},{12,1},{13,0},{2,15},{3,14},... | collective-permute-start | bytes 196616 | tf_op jit(solution)/shard_map/ppermute | solution.py:516
  45.1 8.7 %collective-permute-start.14 = (bf16[256,128]{1,0:T(8,128)(2,1)S(1)}, bf16[256,128]{1,0:T(8,128)(2,1)S(1)}, u32[]{:S(2)}, u32[]{:S(2)}) collective-permute-start(bf16[256,128]{1,0:T(8,128)(2,1)S(1)} %get-tuple-element.36), channel_id=1, source_target_pairs={{0,9},{1,8},{4,13},{5,12},{8,1},{9,0},{12,5},{13,4},{2,11},{3,10},... | collective-permute-start | bytes 196616 | tf_op jit(solution)/shard_map/ppermute | solution.py:516
  47.5 6.3 %collective-permute-start.12 = (bf16[256,128]{1,0:T(8,128)(2,1)S(1)}, bf16[256,128]{1,0:T(8,128)(2,1)S(1)}, u32[]{:S(2)}, u32[]{:S(2)}) collective-permute-start(bf16[256,128]{1,0:T(8,128)(2,1)S(1)} %get-tuple-element.36), channel_id=1, source_target_pairs={{0,5},{1,4},{4,1},{5,0},{8,13},{9,12},{12,9},{13,8},{2,7},{3,6},{6... | collective-permute-start | bytes 196616 | tf_op jit(solution)/shard_map/ppermute | solution.py:516
  49.3 4.6 %collective-permute-start.10 = (bf16[256,128]{1,0:T(8,128)(2,1)S(1)}, bf16[256,128]{1,0:T(8,128)(2,1)S(1)}, u32[]{:S(2)}, u32[]{:S(2)}) collective-permute-start(bf16[256,128]{1,0:T(8,128)(2,1)S(1)} %get-tuple-element.36), channel_id=1, source_target_pairs={{0,1},{1,0},{4,5},{5,4},{8,9},{9,8},{12,13},{13,12},{2,3},{3,2},{6... | collective-permute-start | bytes 196616 | tf_op jit(solution)/shard_map/ppermute | solution.py:516

commit v7 on v6

--- a/solution.py
+++ b/solution.py
@@ -12,6 +12,7 @@
 ORDER = 6
 LANE = 128
 VMEM_LIMIT = 24 * 1024 * 1024
+CHUNK = 64
 
 step_root = math.sqrt(0.08)
 
@@ -110,7 +111,14 @@
             vec_copies[g + 1].wait()
             ahead = mm(vec_ref[g + 1], trial)
         quad_ref[g] = vec_ref[g, :, columns]
-        rows = [jnp.sum(green_ref[w] * mixed, axis=0, keepdims=True) for w in range(n_walk)]
+        held = [None] * n_walk
+        for low in range(0, n_rows, CHUNK):
+            part = mixed[low : low + CHUNK]
+            for w in range(n_walk):
+                product = (green_ref[w, pl.ds(low, CHUNK), :] * part).reshape(CHUNK // 8, 8, -1)
+                found = jnp.sum(product, axis=0)
+                held[w] = found if low == 0 else held[w] + found
+        rows = [jnp.sum(value, axis=0, keepdims=True) for value in held]
         column = jnp.sum(jnp.concatenate(rows, axis=0), axis=1, keepdims=True)
         total = total + jnp.where(lane == g, column, 0.0)
     for copy in copies[3:]:
@@ -440,11 +448,12 @@
     term_ref[bottom, :] = jnp.where(here, orb_ref[...], far_ref[...])
     sum_ref[...] = term_ref[...].astype(jnp.float32)
     for degree in range(1, ORDER + 1):
-        product = mm(op_ref[...], term_ref[...])
-        term = (product / degree).astype(jnp.bfloat16)
-        sum_ref[...] += term.astype(jnp.float32)
-        if degree < ORDER:
-            term_ref[...] = term
+        halves = [mm(op_ref[half, :], term_ref[...]) for half in (top, bottom)]
+        for half, product in zip((top, bottom), halves):
+            term = (product * (1.0 / degree)).astype(jnp.bfloat16)
+            sum_ref[half, :] += term.astype(jnp.float32)
+            if degree < ORDER:
+                term_ref[half, :] = term
     mine_ref[...] = sum_ref[top, :].astype(jnp.bfloat16)
     other_ref[...] = sum_ref[bottom, :].astype(jnp.bfloat16)
 

time: 54.9 us -> 54.4 us (level)
  no operation moved by 1% of the time
where the time goes in v7:
time: 54.4 us; the launch traced here: 54.2 us
  waiting for transfers between devices  25.4 us (47%)
  starting transfers between devices  19.3 us (35%)
  Pallas kernels  8.77 us (16%)
  between operations  0.68 us (1%)
    ppermute x14, waiting for transfers between devices, swapped(): return lax.ppermute(value, axes, perm)  17.4 us
    ppermute x14, starting transfers between devices, swapped(): return lax.ppermute(value, axes, perm)  13.8 us
    ppermute x1, waiting for transfers between devices, slot_device(): last = lax.ppermute(passed, 'vec', [(0, 1), (1, 3), (2, 0), (3, 2)])  8.03 us
    pallas_call x1, Pallas kernels, partial_bias_of(): pl.pallas_call(bias_kernel, out_shape=[VMEM((3 * n_walk, n_vec), jnp.floa...  3.54 us
    ppermute x1, starting transfers between devices, slot_device(): crossed = lax.ppermute(crossing, 'vec', [(0, 2), (3, 1), (1, 0), (2, 3)])  2.59 us
    ppermute x1, starting transfers between devices, slot_device(): last = lax.ppermute(passed, 'vec', [(0, 1), (1, 3), (2, 0), (3, 2)])  2.2 us
    pallas_call x1, Pallas kernels, taylor(): pl.pallas_call(partial(taylor_kernel, n_o), out_shape=[out, out, VMEM((1,...  1.97 us
    pallas_call x1, Pallas kernels, first_pieces(): pl.pallas_call(partial(first_kernel, n_o), out_shape=[VMEM((layout(here.s...  1.21 us
  transfers between devices with their start and end apart: 17, of which 10 were waited for; matrix products, arithmetic and copies ran while one was open for 0% of the time, Pallas kernels for 2%

profile of v7, /device:TPU:0, one launch (start us, length us, event | category | flops | bytes accessed | tf_op | source)
XLA Modules:
  0.0 54.2 jit_solution(13450748058336777205)
XLA Ops:
  0.6 3.5 %bias.1 = (f32[24,8]{1,0:T(8,128)S(1)}, bf16[8,256,512]{2,1,0:T(8,128)(2,1)S(1)}, bf16[8,256,256]{2,1,0:T(8,128)(2,1)S(1)}) custom-call(f32[8,8]{1,0:T(8,128)} %aux_hbm.1, f32[1,8]{1,0:T(1,128)} %bitcast.3, s32[1,8]{1,0:T(1,128)} %bitcast.4, bf16[8,256,128]{2,1,0:T(8,128)(2,1)} %walkers_hbm.3, bf16[8,128,128]{2,1,0:T(8,128)(2,1)} %inv_hbm.1, ...), custom_call_target="tpu_custom_call" | custom-call | tf_op jit(solution)/shard_map/bias/pallas_call | solution.py:136
  4.2 0.6 %collective-permute-start.2 = (bf16[8,256,256]{2,1,0:T(8,128)(2,1)S(1)}, bf16[8,256,256]{2,1,0:T(8,128)(2,1)S(1)}, u32[]{:S(2)}, u32[]{:S(2)}) collective-permute-start(bf16[8,256,256]{2,1,0:T(8,128)(2,1)S(1)} %get-tuple-element.23), channel_id=1, source_target_pairs={{0,1},{1,0},{2,3},{3,2},{4,5},{5,4},{6,7},{7,6},{8,9},{9,8},{10,11... | collective-permute-start | bytes 3145736 | tf_op jit(solution)/shard_map/ppermute | solution.py:525
  4.7 0.1 collective-permute-start
  4.8 2.2 %collective-permute-done.orb_ref = f32[24,8]{1,0:T(8,128)S(1)} collective-permute-done((f32[24,8]{1,0:T(8,128)S(1)}, f32[24,8]{1,0:T(8,128)S(1)}, u32[]{:S(2)}, u32[]{:S(2)}) %collective-permute-start) | collective-permute-done | bytes 800 | tf_op jit(solution)/shard_map/ppermute | solution.py:525
  7.0 2.9 %collective-permute-start.1 = (f32[24,8]{1,0:T(8,128)S(1)}, f32[24,8]{1,0:T(8,128)S(1)}, u32[]{:S(2)}, u32[]{:S(2)}) collective-permute-start(f32[24,8]{1,0:T(8,128)S(1)} %summed_pack.1.own_ref.pack_ref), channel_id=1, source_target_pairs={{0,2},{1,3},{2,0},{3,1},{4,6},{5,7},{6,4},{7,5},{8,10},{9,11},{10,... | collective-permute-start | bytes 2312 | tf_op jit(solution)/shard_map/ppermute | solution.py:525
  9.9 1.7 %collective-permute-done.1.walk_ref = f32[24,8]{1,0:T(8,128)S(1)} collective-permute-done((f32[24,8]{1,0:T(8,128)S(1)}, f32[24,8]{1,0:T(8,128)S(1)}, u32[]{:S(2)}, u32[]{:S(2)}) %collective-permute-start.1) | collective-permute-done | bytes 800 | tf_op jit(solution)/shard_map/ppermute | solution.py:525
  11.6 0.0 collective-permute-done.2.mate_ref
  11.6 1.2 %first_piece.1 = (bf16[1072,128]{1,0:T(8,128)(2,1)S(1)}, bf16[1072,128]{1,0:T(8,128)(2,1)S(1)}, f32[8,8]{1,0:T(8,128)S(1)}, bf16[16,128]{1,0:T(8,128)(2,1)S(1)}, f32[16,1]{1,0:T(8,128)S(1)}) custom-call(f32[24,8]{1,0:T(8,128)S(1)} %summed_pack.1.own_ref.pack_ref, f32[24,8]{1,0:T(8,128)S(1)} %collective-permute-done.1.walk_ref, ...), custom_call_target="tpu_custom_call" | custom-call | tf_op jit(solution)/shard_map/first_piece/pallas_call | solution.py:322
  12.8 2.2 %collective-permute-start.3 = (bf16[1072,128]{1,0:T(8,128)(2,1)S(1)}, bf16[1072,128]{1,0:T(8,128)(2,1)S(1)}, u32[]{:S(2)}, u32[]{:S(2)}) collective-permute-start(bf16[1072,128]{1,0:T(8,128)(2,1)S(1)} %get-tuple-element.28), channel_id=1, source_target_pairs={{0,4},{1,5},{4,0},{5,1},{8,12},{9,13},{12,8},{13,9},{2,6},{3,7},{6... | collective-permute-start | bytes 823304 | tf_op jit(solution)/shard_map/ppermute | solution.py:525
  15.0 1.2 %other_pieces.1 = (bf16[1072,128]{1,0:T(8,128)(2,1)S(1)}, bf16[1072,128]{1,0:T(8,128)(2,1)S(1)}, bf16[256,128]{1,0:T(8,128)(2,1)S(1)}, bf16[256,128]{1,0:T(8,128...) custom-call(f32[24,8]{1,0:T(8,128)S(1)} %summed_pack.1.own_ref.pack_ref, ...), custom_call_target="tpu_custom_call" | custom-call | tf_op jit(solution)/shard_map/other_pieces/pallas_call | solution.py:358
  16.1 2.6 %collective-permute-start.5 = (bf16[1072,128]{1,0:T(8,128)(2,1)S(1)}, bf16[1072,128]{1,0:T(8,128)(2,1)S(1)}, u32[]{:S(2)}, u32[]{:S(2)}) collective-permute-start(bf16[1072,128]{1,0:T(8,128)(2,1)S(1)} %get-tuple-element.30.far_ref), channel_id=1, source_target_pairs={{0,8},{12,4},{4,0},{8,12},{1,9},{13,5},{5,1},{9,13},{2,10},{14,6},... | collective-permute-start | bytes 823304 | tf_op jit(solution)/shard_map/ppermute | solution.py:547
  18.7 0.7 %collective-permute-start.4 = (bf16[1072,128]{1,0:T(8,128)(2,1)S(1)}, bf16[1072,128]{1,0:T(8,128)(2,1)S(1)}, u32[]{:S(2)}, u32[]{:S(2)}) collective-permute-start(bf16[1072,128]{1,0:T(8,128)(2,1)S(1)} %get-tuple-element.29.near_ref), channel_id=1, source_target_pairs={{0,0},{4,8},{8,4},{12,12},{1,1},{5,9},{9,5},{13,13},{2,2},{6,10},{... | collective-permute-start | bytes 823304 | tf_op jit(solution)/shard_map/ppermute | solution.py:543
  19.4 3.0 %collective-permute-done.3.came_ref.first_ref = bf16[1072,128]{1,0:T(8,128)(2,1)S(1)} collective-permute-done((bf16[1072,128]{1,0:T(8,128)(2,1)S(1)}, bf16[1072,128]{1,0:T(8,128)(2,1)S(1)}, u32[]{:S(2)}, u32[]{:S(2)}) %collective-permute-start.3) | collective-permute-done | bytes 274464 | tf_op jit(solution)/shard_map/ppermute | solution.py:525
  22.4 2.2 %collective-permute-start.6 = (bf16[1072,128]{1,0:T(8,128)(2,1)S(1)}, bf16[1072,128]{1,0:T(8,128)(2,1)S(1)}, u32[]{:S(2)}, u32[]{:S(2)}) collective-permute-start(bf16[1072,128]{1,0:T(8,128)(2,1)S(1)} %combine.1), channel_id=1, source_target_pairs={{0,4},{4,12},{8,0},{12,8},{1,5},{5,13},{9,1},{13,9},{2,6},{6,14},{... | collective-permute-start | bytes 823304 | tf_op jit(solution)/shard_map/ppermute | solution.py:549
  24.6 0.0 collective-permute-start.7
  24.6 1.5 %collective-permute-start.8 = (bf16[256,128]{1,0:T(8,128)(2,1)S(1)}, bf16[256,128]{1,0:T(8,128)(2,1)S(1)}, u32[]{:S(2)}, u32[]{:S(2)}) collective-permute-start(bf16[256,128]{1,0:T(8,128)(2,1)S(1)} %get-tuple-element.33), channel_id=1, source_target_pairs={{0,2},{1,3},{2,0},{3,1},{4,6},{5,7},{6,4},{7,5},{8,10},{9,11},{10,... | collective-permute-start | bytes 196616 | tf_op jit(solution)/shard_map/ppermute | solution.py:525
  26.1 0.0 collective-permute-done.7.orb_ref
  26.1 1.0 %collective-permute-start.9 = (bf16[256,128]{1,0:T(8,128)(2,1)S(1)}, bf16[256,128]{1,0:T(8,128)(2,1)S(1)}, u32[]{:S(2)}, u32[]{:S(2)}) collective-permute-start(bf16[256,128]{1,0:T(8,128)(2,1)S(1)} %get-tuple-element.34), channel_id=1, source_target_pairs={{0,3},{1,2},{2,1},{3,0},{4,7},{5,6},{6,5},{7,4},{8,11},{9,10},{10,... | collective-permute-start | bytes 196616 | tf_op jit(solution)/shard_map/ppermute | solution.py:525
  27.1 2.0 %collective-permute-done.8.walk_ref = bf16[256,128]{1,0:T(8,128)(2,1)S(1)} collective-permute-done((bf16[256,128]{1,0:T(8,128)(2,1)S(1)}, bf16[256,128]{1,0:T(8,128)(2,1)S(1)}, u32[]{:S(2)}, u32[]{:S(2)}) %collective-permute-start.8) | collective-permute-done | bytes 65568 | tf_op jit(solution)/shard_map/ppermute | solution.py:525
  29.1 1.0 %collective-permute-done.9.far_ref = bf16[256,128]{1,0:T(8,128)(2,1)S(1)} collective-permute-done((bf16[256,128]{1,0:T(8,128)(2,1)S(1)}, bf16[256,128]{1,0:T(8,128)(2,1)S(1)}, u32[]{:S(2)}, u32[]{:S(2)}) %collective-permute-start.9) | collective-permute-done | bytes 65568 | tf_op jit(solution)/shard_map/ppermute | solution.py:525
  30.1 0.0 collective-permute-done.5.cross_ref
  30.1 0.0 collective-permute-done.4.inside_ref
  30.1 8.0 %collective-permute-done.6.last_ref = bf16[1072,128]{1,0:T(8,128)(2,1)S(1)} collective-permute-done((bf16[1072,128]{1,0:T(8,128)(2,1)S(1)}, bf16[1072,128]{1,0:T(8,128)(2,1)S(1)}, u32[]{:S(2)}, u32[]{:S(2)}) %collective-permute-start.6) | collective-permute-done | bytes 274464 | tf_op jit(solution)/shard_map/ppermute | solution.py:549
  38.2 2.0 %taylor.1 = (bf16[256,128]{1,0:T(8,128)(2,1)S(1)}, bf16[256,128]{1,0:T(8,128)(2,1)S(1)}, f32[1,8]{1,0:T(1,128)S(1)}) custom-call(f32[24,8]{1,0:T(8,128)S(1)} %summed_pack.1.own_ref.pack_ref, f32[16,1]{1,0:T(8,128)S(1)} %get-tuple-element.24.log_ref, bf16[1072,128]{1,0:T(8,128)(2,1)S(1)} %get-tuple-element.27.kept_ref, ...), custom_call_target="tpu_custom_call" | custom-call | tf_op jit(solution)/shard_map/taylor/pallas_call | solution.py:469
  40.1 2.1 %collective-permute-start.15 = (bf16[256,128]{1,0:T(8,128)(2,1)S(1)}, bf16[256,128]{1,0:T(8,128)(2,1)S(1)}, u32[]{:S(2)}, u32[]{:S(2)}) collective-permute-start(bf16[256,128]{1,0:T(8,128)(2,1)S(1)} %get-tuple-element.35.refs_0_), channel_id=1, source_target_pairs={{0,12},{1,13},{4,8},{5,9},{8,4},{9,5},{12,0},{13,1},{2,14},{3,15},... | collective-permute-start | bytes 196616 | tf_op jit(solution)/shard_map/ppermute | solution.py:525
  42.3 0.0 collective-permute-start.13
  42.3 2.3 %collective-permute-start.11 = (bf16[256,128]{1,0:T(8,128)(2,1)S(1)}, bf16[256,128]{1,0:T(8,128)(2,1)S(1)}, u32[]{:S(2)}, u32[]{:S(2)}) collective-permute-start(bf16[256,128]{1,0:T(8,128)(2,1)S(1)} %get-tuple-element.35.refs_0_), channel_id=1, source_target_pairs={{0,4},{1,5},{4,0},{5,1},{8,12},{9,13},{12,8},{13,9},{2,6},{3,7},{6... | collective-permute-start | bytes 196616 | tf_op jit(solution)/shard_map/ppermute | solution.py:525
  44.6 0.0 collective-permute-start.16
  44.6 1.2 %collective-permute-start.14 = (bf16[256,128]{1,0:T(8,128)(2,1)S(1)}, bf16[256,128]{1,0:T(8,128)(2,1)S(1)}, u32[]{:S(2)}, u32[]{:S(2)}) collective-permute-start(bf16[256,128]{1,0:T(8,128)(2,1)S(1)} %get-tuple-element.36), channel_id=1, source_target_pairs={{0,9},{1,8},{4,13},{5,12},{8,1},{9,0},{12,5},{13,4},{2,11},{3,10},... | collective-permute-start | bytes 196616 | tf_op jit(solution)/shard_map/ppermute | solution.py:525
  45.8 1.2 %collective-permute-done.15.refs_6_ = bf16[256,128]{1,0:T(8,128)(2,1)S(1)} collective-permute-done((bf16[256,128]{1,0:T(8,128)(2,1)S(1)}, bf16[256,128]{1,0:T(8,128)(2,1)S(1)}, u32[]{:S(2)}, u32[]{:S(2)}) %collective-permute-start.15) | collective-permute-done | bytes 65568 | tf_op jit(solution)/shard_map/ppermute | solution.py:525
  47.0 0.0 collective-permute-start.12
  47.0 1.8 %collective-permute-done.13.refs_4_ = bf16[256,128]{1,0:T(8,128)(2,1)S(1)} collective-permute-done((bf16[256,128]{1,0:T(8,128)(2,1)S(1)}, bf16[256,128]{1,0:T(8,128)(2,1)S(1)}, u32[]{:S(2)}, u32[]{:S(2)}) %collective-permute-start.13) | collective-permute-done | bytes 65568 | tf_op jit(solution)/shard_map/ppermute | solution.py:525
  48.8 0.0 collective-permute-start.10
  48.8 0.0 collective-permute-done.11.refs_2_
  48.8 2.1 %collective-permute-done.16.refs_7_ = bf16[256,128]{1,0:T(8,128)(2,1)S(1)} collective-permute-done((bf16[256,128]{1,0:T(8,128)(2,1)S(1)}, bf16[256,128]{1,0:T(8,128)(2,1)S(1)}, u32[]{:S(2)}, u32[]{:S(2)}) %collective-permute-start.16) | collective-permute-done | bytes 65568 | tf_op jit(solution)/shard_map/ppermute | solution.py:525
  50.9 2.5 %collective-permute-done.14.refs_5_ = bf16[256,128]{1,0:T(8,128)(2,1)S(1)} collective-permute-done((bf16[256,128]{1,0:T(8,128)(2,1)S(1)}, bf16[256,128]{1,0:T(8,128)(2,1)S(1)}, u32[]{:S(2)}, u32[]{:S(2)}) %collective-permute-start.14) | collective-permute-done | bytes 65568 | tf_op jit(solution)/shard_map/ppermute | solution.py:525
  53.3 0.0 collective-permute-done.12.refs_3_
  53.3 0.0 collective-permute-done.10.refs_1_
  53.3 0.9 %place.1 = (bf16[8,256,128]{2,1,0:T(8,128)(2,1)}, f32[1,8]{1,0:T(1,128)}) custom-call(bf16[256,128]{1,0:T(8,128)(2,1)S(1)} %get-tuple-element.35.refs_0_, bf16[256,128]{1,0:T(8,128)(2,1)S(1)} %collective-permute-done.10.refs_1_, bf16[256,128]{1,0:T(8,128)(2,1)S(1)} %collective-permute-done.11.refs_2_, bf16[256,128]{1,0:T(8,128)(2,1)S(1)} %collective-permute-done.12.refs_3_, ...), custom_call_target="tpu_custom_call" | custom-call | tf_op jit(solution)/shard_map/place/pallas_call | solution.py:506
  (2 shorter events, 0.0 us)
Async XLA Ops:
  4.2 7.4 %collective-permute-start.2 = (bf16[8,256,256]{2,1,0:T(8,128)(2,1)S(1)}, bf16[8,256,256]{2,1,0:T(8,128)(2,1)S(1)}, u32[]{:S(2)}, u32[]{:S(2)}) collective-permute-start(bf16[8,256,256]{2,1,0:T(8,128)(2,1)S(1)} %get-tuple-element.23), channel_id=1, source_target_pairs={{0,1},{1,0},{2,3},{3,2},{4,5},{5,4},{6,7},{7,6},{8,9},{9,8},{10,11... | collective-permute-start | bytes 3145736 | tf_op jit(solution)/shard_map/ppermute | solution.py:525
  4.7 2.3 %collective-permute-start = (f32[24,8]{1,0:T(8,128)S(1)}, f32[24,8]{1,0:T(8,128)S(1)}, u32[]{:S(2)}, u32[]{:S(2)}) collective-permute-start(f32[24,8]{1,0:T(8,128)S(1)} %get-tuple-element.21.own_ref), channel_id=1, source_target_pairs={{0,1},{1,0},{2,3},{3,2},{4,5},{5,4},{6,7},{7,6},{8,9},{9,8},{10,11... | collective-permute-start | bytes 2312 | tf_op jit(solution)/shard_map/ppermute | solution.py:525
  7.0 4.5 %collective-permute-start.1 = (f32[24,8]{1,0:T(8,128)S(1)}, f32[24,8]{1,0:T(8,128)S(1)}, u32[]{:S(2)}, u32[]{:S(2)}) collective-permute-start(f32[24,8]{1,0:T(8,128)S(1)} %summed_pack.1.own_ref.pack_ref), channel_id=1, source_target_pairs={{0,2},{1,3},{2,0},{3,1},{4,6},{5,7},{6,4},{7,5},{8,10},{9,11},{10,... | collective-permute-start | bytes 2312 | tf_op jit(solution)/shard_map/ppermute | solution.py:525
  12.8 9.6 %collective-permute-start.3 = (bf16[1072,128]{1,0:T(8,128)(2,1)S(1)}, bf16[1072,128]{1,0:T(8,128)(2,1)S(1)}, u32[]{:S(2)}, u32[]{:S(2)}) collective-permute-start(bf16[1072,128]{1,0:T(8,128)(2,1)S(1)} %get-tuple-element.28), channel_id=1, source_target_pairs={{0,4},{1,5},{4,0},{5,1},{8,12},{9,13},{12,8},{13,9},{2,6},{3,7},{6... | collective-permute-start | bytes 823304 | tf_op jit(solution)/shard_map/ppermute | solution.py:525
  16.1 14.0 %collective-permute-start.5 = (bf16[1072,128]{1,0:T(8,128)(2,1)S(1)}, bf16[1072,128]{1,0:T(8,128)(2,1)S(1)}, u32[]{:S(2)}, u32[]{:S(2)}) collective-permute-start(bf16[1072,128]{1,0:T(8,128)(2,1)S(1)} %get-tuple-element.30.far_ref), channel_id=1, source_target_pairs={{0,8},{12,4},{4,0},{8,12},{1,9},{13,5},{5,1},{9,13},{2,10},{14,6},... | collective-permute-start | bytes 823304 | tf_op jit(solution)/shard_map/ppermute | solution.py:547
  18.7 11.4 %collective-permute-start.4 = (bf16[1072,128]{1,0:T(8,128)(2,1)S(1)}, bf16[1072,128]{1,0:T(8,128)(2,1)S(1)}, u32[]{:S(2)}, u32[]{:S(2)}) collective-permute-start(bf16[1072,128]{1,0:T(8,128)(2,1)S(1)} %get-tuple-element.29.near_ref), channel_id=1, source_target_pairs={{0,0},{4,8},{8,4},{12,12},{1,1},{5,9},{9,5},{13,13},{2,2},{6,10},{... | collective-permute-start | bytes 823304 | tf_op jit(solution)/shard_map/ppermute | solution.py:543
  22.4 15.8 %collective-permute-start.6 = (bf16[1072,128]{1,0:T(8,128)(2,1)S(1)}, bf16[1072,128]{1,0:T(8,128)(2,1)S(1)}, u32[]{:S(2)}, u32[]{:S(2)}) collective-permute-start(bf16[1072,128]{1,0:T(8,128)(2,1)S(1)} %combine.1), channel_id=1, source_target_pairs={{0,4},{4,12},{8,0},{12,8},{1,5},{5,13},{9,1},{13,9},{2,6},{6,14},{... | collective-permute-start | bytes 823304 | tf_op jit(solution)/shard_map/ppermute | solution.py:549
  24.6 1.5 %collective-permute-start.7 = (bf16[256,128]{1,0:T(8,128)(2,1)S(1)}, bf16[256,128]{1,0:T(8,128)(2,1)S(1)}, u32[]{:S(2)}, u32[]{:S(2)}) collective-permute-start(bf16[256,128]{1,0:T(8,128)(2,1)S(1)} %get-tuple-element.32), channel_id=1, source_target_pairs={{0,1},{1,0},{2,3},{3,2},{4,5},{5,4},{6,7},{7,6},{8,9},{9,8},{10,11... | collective-permute-start | bytes 196616 | tf_op jit(solution)/shard_map/ppermute | solution.py:525
  24.6 4.5 %collective-permute-start.8 = (bf16[256,128]{1,0:T(8,128)(2,1)S(1)}, bf16[256,128]{1,0:T(8,128)(2,1)S(1)}, u32[]{:S(2)}, u32[]{:S(2)}) collective-permute-start(bf16[256,128]{1,0:T(8,128)(2,1)S(1)} %get-tuple-element.33), channel_id=1, source_target_pairs={{0,2},{1,3},{2,0},{3,1},{4,6},{5,7},{6,4},{7,5},{8,10},{9,11},{10,... | collective-permute-start | bytes 196616 | tf_op jit(solution)/shard_map/ppermute | solution.py:525
  26.1 4.0 %collective-permute-start.9 = (bf16[256,128]{1,0:T(8,128)(2,1)S(1)}, bf16[256,128]{1,0:T(8,128)(2,1)S(1)}, u32[]{:S(2)}, u32[]{:S(2)}) collective-permute-start(bf16[256,128]{1,0:T(8,128)(2,1)S(1)} %get-tuple-element.34), channel_id=1, source_target_pairs={{0,3},{1,2},{2,1},{3,0},{4,7},{5,6},{6,5},{7,4},{8,11},{9,10},{10,... | collective-permute-start | bytes 196616 | tf_op jit(solution)/shard_map/ppermute | solution.py:525
  40.1 6.9 %collective-permute-start.15 = (bf16[256,128]{1,0:T(8,128)(2,1)S(1)}, bf16[256,128]{1,0:T(8,128)(2,1)S(1)}, u32[]{:S(2)}, u32[]{:S(2)}) collective-permute-start(bf16[256,128]{1,0:T(8,128)(2,1)S(1)} %get-tuple-element.35.refs_0_), channel_id=1, source_target_pairs={{0,12},{1,13},{4,8},{5,9},{8,4},{9,5},{12,0},{13,1},{2,14},{3,15},... | collective-permute-start | bytes 196616 | tf_op jit(solution)/shard_map/ppermute | solution.py:525
  42.3 6.5 %collective-permute-start.13 = (bf16[256,128]{1,0:T(8,128)(2,1)S(1)}, bf16[256,128]{1,0:T(8,128)(2,1)S(1)}, u32[]{:S(2)}, u32[]{:S(2)}) collective-permute-start(bf16[256,128]{1,0:T(8,128)(2,1)S(1)} %get-tuple-element.35.refs_0_), channel_id=1, source_target_pairs={{0,8},{1,9},{4,12},{5,13},{8,0},{9,1},{12,4},{13,5},{2,10},{3,11},... | collective-permute-start | bytes 196616 | tf_op jit(solution)/shard_map/ppermute | solution.py:525
  42.3 6.5 %collective-permute-start.11 = (bf16[256,128]{1,0:T(8,128)(2,1)S(1)}, bf16[256,128]{1,0:T(8,128)(2,1)S(1)}, u32[]{:S(2)}, u32[]{:S(2)}) collective-permute-start(bf16[256,128]{1,0:T(8,128)(2,1)S(1)} %get-tuple-element.35.refs_0_), channel_id=1, source_target_pairs={{0,4},{1,5},{4,0},{5,1},{8,12},{9,13},{12,8},{13,9},{2,6},{3,7},{6... | collective-permute-start | bytes 196616 | tf_op jit(solution)/shard_map/ppermute | solution.py:525
  44.6 6.3 %collective-permute-start.16 = (bf16[256,128]{1,0:T(8,128)(2,1)S(1)}, bf16[256,128]{1,0:T(8,128)(2,1)S(1)}, u32[]{:S(2)}, u32[]{:S(2)}) collective-permute-start(bf16[256,128]{1,0:T(8,128)(2,1)S(1)} %get-tuple-element.36), channel_id=1, source_target_pairs={{0,13},{1,12},{4,9},{5,8},{8,5},{9,4},{12,1},{13,0},{2,15},{3,14},... | collective-permute-start | bytes 196616 | tf_op jit(solution)/shard_map/ppermute | solution.py:525
  44.6 8.7 %collective-permute-start.14 = (bf16[256,128]{1,0:T(8,128)(2,1)S(1)}, bf16[256,128]{1,0:T(8,128)(2,1)S(1)}, u32[]{:S(2)}, u32[]{:S(2)}) collective-permute-start(bf16[256,128]{1,0:T(8,128)(2,1)S(1)} %get-tuple-element.36), channel_id=1, source_target_pairs={{0,9},{1,8},{4,13},{5,12},{8,1},{9,0},{12,5},{13,4},{2,11},{3,10},... | collective-permute-start | bytes 196616 | tf_op jit(solution)/shard_map/ppermute | solution.py:525
  47.0 6.3 %collective-permute-start.12 = (bf16[256,128]{1,0:T(8,128)(2,1)S(1)}, bf16[256,128]{1,0:T(8,128)(2,1)S(1)}, u32[]{:S(2)}, u32[]{:S(2)}) collective-permute-start(bf16[256,128]{1,0:T(8,128)(2,1)S(1)} %get-tuple-element.36), channel_id=1, source_target_pairs={{0,5},{1,4},{4,1},{5,0},{8,13},{9,12},{12,9},{13,8},{2,7},{3,6},{6... | collective-permute-start | bytes 196616 | tf_op jit(solution)/shard_map/ppermute | solution.py:525
  48.8 4.5 %collective-permute-start.10 = (bf16[256,128]{1,0:T(8,128)(2,1)S(1)}, bf16[256,128]{1,0:T(8,128)(2,1)S(1)}, u32[]{:S(2)}, u32[]{:S(2)}) collective-permute-start(bf16[256,128]{1,0:T(8,128)(2,1)S(1)} %get-tuple-element.36), channel_id=1, source_target_pairs={{0,1},{1,0},{4,5},{5,4},{8,9},{9,8},{12,13},{13,12},{2,3},{3,2},{6... | collective-permute-start | bytes 196616 | tf_op jit(solution)/shard_map/ppermute | solution.py:525

commit v8 on v7

--- a/solution.py
+++ b/solution.py
@@ -481,12 +481,9 @@
     )(*on_chip(pack, log_column, *arrived, *candidates))
 
 
-def place_kernel(steps, n_o, *refs):
-    n_line = len(steps)
-    pieces, weights_ref = refs[:n_line], refs[n_line]
-    out_ref, weights_out, sems = refs[n_line + 1 :]
+def slot_copies(steps, n_o, pieces, out_ref, sems):
     z, o = lax.axis_index("vec"), lax.axis_index("orb")
-    copies = [
+    return [
         pltpu.make_async_copy(
             pieces[k],
             out_ref.at[jnp.bitwise_xor(z, dz) * n_o + jnp.bitwise_xor(o, flip)],
@@ -494,27 +491,53 @@
         )
         for k, (dz, flip) in enumerate(steps)
     ]
-    copies.append(pltpu.make_async_copy(weights_ref, weights_out, sems.at[n_line]))
+
+
+def run_copies(copies):
     for copy in copies:
         copy.start()
     for copy in copies:
         copy.wait()
 
 
-def put_in_place(steps, pieces, weights, n_o):
-    n_line = len(pieces)
-    return pl.pallas_call(
-        partial(place_kernel, steps, n_o),
-        out_shape=[
-            jax.ShapeDtypeStruct((n_line,) + pieces[0].shape, pieces[0].dtype),
-            jax.ShapeDtypeStruct(weights.shape, weights.dtype),
-        ],
-        in_specs=[in_vmem()] * (n_line + 1),
+def early_place_kernel(steps, n_o, *refs):
+    count = len(steps)
+    weights_ref, out_ref, weights_out, sems = refs[count:]
+    copies = slot_copies(steps, n_o, refs[:count], out_ref, sems)
+    run_copies(copies + [pltpu.make_async_copy(weights_ref, weights_out, sems.at[count])])
+
+
+def late_place_kernel(steps, n_o, *refs):
+    count = len(steps)
+    _, out_ref, sems = refs[count:]
+    run_copies(slot_copies(steps, n_o, refs[:count], out_ref, sems))
+
+
+def put_in_place(steps, pieces, late, weights, n_o):
+    out = jax.ShapeDtypeStruct((len(pieces),) + pieces[0].shape, pieces[0].dtype)
+    first = [k for k, step in enumerate(steps) if step not in late]
+    last = [k for k, step in enumerate(steps) if step in late]
+    limits = pltpu.CompilerParams(vmem_limit_bytes=VMEM_LIMIT)
+    held, weights_out = pl.pallas_call(
+        partial(early_place_kernel, [steps[k] for k in first], n_o),
+        out_shape=[out, jax.ShapeDtypeStruct(weights.shape, weights.dtype)],
+        in_specs=[in_vmem()] * (len(first) + 1),
         out_specs=[in_hbm()] * 2,
-        scratch_shapes=[pltpu.SemaphoreType.DMA((n_line + 1,))],
-        compiler_params=pltpu.CompilerParams(vmem_limit_bytes=VMEM_LIMIT),
-        name="place",
-    )(*on_chip(*pieces, weights))
+        scratch_shapes=[pltpu.SemaphoreType.DMA((len(first) + 1,))],
+        compiler_params=limits,
+        name="early_place",
+    )(*on_chip(*[pieces[k] for k in first], weights))
+    walkers_out = pl.pallas_call(
+        partial(late_place_kernel, [steps[k] for k in last], n_o),
+        out_shape=out,
+        in_specs=[in_vmem()] * len(last) + [in_hbm()],
+        out_specs=in_hbm(),
+        scratch_shapes=[pltpu.SemaphoreType.DMA((len(last),))],
+        input_output_aliases={len(last): 0},
+        compiler_params=limits,
+        name="late_place",
+    )(*on_chip(*[pieces[k] for k in last]), held)
+    return walkers_out, weights_out
 
 
 def swapped(value, axes, sizes, masks):
@@ -558,7 +581,7 @@
     for dz, flip in steps:
         half = mine if flip == 0 else other
         landed.append(half if (dz, flip) == (0, 0) else line(half, masks=(dz, flip)))
-    walkers_out, weights_out = put_in_place(steps, landed, slot_weights, n_o)
+    walkers_out, weights_out = put_in_place(steps, landed, ((2, 0), (2, 1), (1, 0), (1, 1), (0, 1)), slot_weights, n_o)
     return walkers_out, weights_out[0]
 
 

time: 54.4 us -> 54.2 us (level)
  waiting for transfers between devices: 25.4 us -> 22.3 us
  starting transfers between devices: 19.3 us -> 21.6 us
  Pallas kernels: 8.77 us -> 9.38 us
    ppermute x14, waiting for transfers between devices: 17.4 us -> 14.3 us  [swapped(): return lax.ppermute(value, axes, perm)]
    ppermute x14, starting transfers between devices: 13.8 us -> 16.1 us  [swapped(): return lax.ppermute(value, axes, perm)]
    pallas_call x1 -> x2, Pallas kernels: 0.86 us -> 1.46 us  [the longest x1 0.76 us: put_in_place(): pl.pallas_call(partial(late_place_kernel, [steps[k] for k in last], n_o),...]
  transfers between devices with their start and end apart: 17 -> 17, of which waited for: 10 -> 9; matrix products, arithmetic and copies ran while one was open for 0% -> 0% of each run, Pallas kernels for 2% -> 4%
where the time goes in v8:
time: 54.2 us; the launch traced here: 54 us
  waiting for transfers between devices  22.3 us (41%)
  starting transfers between devices  21.6 us (40%)
  Pallas kernels  9.38 us (17%)
  between operations  0.69 us (1%)
    ppermute x14, starting transfers between devices, swapped(): return lax.ppermute(value, axes, perm)  16.1 us
    ppermute x14, waiting for transfers between devices, swapped(): return lax.ppermute(value, axes, perm)  14.3 us
    ppermute x1, waiting for transfers between devices, slot_device(): last = lax.ppermute(passed, 'vec', [(0, 1), (1, 3), (2, 0), (3, 2)])  8.03 us
    pallas_call x1, Pallas kernels, partial_bias_of(): pl.pallas_call(bias_kernel, out_shape=[VMEM((3 * n_walk, n_vec), jnp.floa...  3.54 us
    ppermute x1, starting transfers between devices, slot_device(): crossed = lax.ppermute(crossing, 'vec', [(0, 2), (3, 1), (1, 0), (2, 3)])  2.59 us
    ppermute x1, starting transfers between devices, slot_device(): last = lax.ppermute(passed, 'vec', [(0, 1), (1, 3), (2, 0), (3, 2)])  2.2 us
    pallas_call x1, Pallas kernels, taylor(): pl.pallas_call(partial(taylor_kernel, n_o), out_shape=[out, out, VMEM((1,...  1.97 us
    pallas_call x1, Pallas kernels, first_pieces(): pl.pallas_call(partial(first_kernel, n_o), out_shape=[VMEM((layout(here.s...  1.21 us
  transfers between devices with their start and end apart: 17, of which 9 were waited for; matrix products, arithmetic and copies ran while one was open for 0% of the time, Pallas kernels for 4%

profile of v8, /device:TPU:0, one launch (start us, length us, event | category | flops | bytes accessed | tf_op | source)
XLA Modules:
  0.0 54.0 jit_solution(10742439393154777498)
XLA Ops:
  0.6 3.5 %bias.1 = (f32[24,8]{1,0:T(8,128)S(1)}, bf16[8,256,512]{2,1,0:T(8,128)(2,1)S(1)}, bf16[8,256,256]{2,1,0:T(8,128)(2,1)S(1)}) custom-call(f32[8,8]{1,0:T(8,128)} %aux_hbm.1, f32[1,8]{1,0:T(1,128)} %bitcast.3, s32[1,8]{1,0:T(1,128)} %bitcast.4, bf16[8,256,128]{2,1,0:T(8,128)(2,1)} %walkers_hbm.3, bf16[8,128,128]{2,1,0:T(8,128)(2,1)} %inv_hbm.1, ...), custom_call_target="tpu_custom_call" | custom-call | tf_op jit(solution)/shard_map/bias/pallas_call | solution.py:136
  4.2 0.6 %collective-permute-start.2 = (bf16[8,256,256]{2,1,0:T(8,128)(2,1)S(1)}, bf16[8,256,256]{2,1,0:T(8,128)(2,1)S(1)}, u32[]{:S(2)}, u32[]{:S(2)}) collective-permute-start(bf16[8,256,256]{2,1,0:T(8,128)(2,1)S(1)} %get-tuple-element.23), channel_id=1, source_target_pairs={{0,1},{1,0},{2,3},{3,2},{4,5},{5,4},{6,7},{7,6},{8,9},{9,8},{10,11... | collective-permute-start | bytes 3145736 | tf_op jit(solution)/shard_map/ppermute | solution.py:548
  4.7 0.1 collective-permute-start
  4.8 2.2 %collective-permute-done.orb_ref = f32[24,8]{1,0:T(8,128)S(1)} collective-permute-done((f32[24,8]{1,0:T(8,128)S(1)}, f32[24,8]{1,0:T(8,128)S(1)}, u32[]{:S(2)}, u32[]{:S(2)}) %collective-permute-start) | collective-permute-done | bytes 800 | tf_op jit(solution)/shard_map/ppermute | solution.py:548
  7.0 2.9 %collective-permute-start.1 = (f32[24,8]{1,0:T(8,128)S(1)}, f32[24,8]{1,0:T(8,128)S(1)}, u32[]{:S(2)}, u32[]{:S(2)}) collective-permute-start(f32[24,8]{1,0:T(8,128)S(1)} %summed_pack.1.own_ref.pack_ref), channel_id=1, source_target_pairs={{0,2},{1,3},{2,0},{3,1},{4,6},{5,7},{6,4},{7,5},{8,10},{9,11},{10,... | collective-permute-start | bytes 2312 | tf_op jit(solution)/shard_map/ppermute | solution.py:548
  9.9 1.7 %collective-permute-done.1.walk_ref = f32[24,8]{1,0:T(8,128)S(1)} collective-permute-done((f32[24,8]{1,0:T(8,128)S(1)}, f32[24,8]{1,0:T(8,128)S(1)}, u32[]{:S(2)}, u32[]{:S(2)}) %collective-permute-start.1) | collective-permute-done | bytes 800 | tf_op jit(solution)/shard_map/ppermute | solution.py:548
  11.6 0.0 collective-permute-done.2.mate_ref
  11.6 1.2 %first_piece.1 = (bf16[1072,128]{1,0:T(8,128)(2,1)S(1)}, bf16[1072,128]{1,0:T(8,128)(2,1)S(1)}, f32[8,8]{1,0:T(8,128)S(1)}, bf16[16,128]{1,0:T(8,128)(2,1)S(1)}, f32[16,1]{1,0:T(8,128)S(1)}) custom-call(f32[24,8]{1,0:T(8,128)S(1)} %summed_pack.1.own_ref.pack_ref, f32[24,8]{1,0:T(8,128)S(1)} %collective-permute-done.1.walk_ref, ...), custom_call_target="tpu_custom_call" | custom-call | tf_op jit(solution)/shard_map/first_piece/pallas_call | solution.py:322
  12.8 2.2 %collective-permute-start.3 = (bf16[1072,128]{1,0:T(8,128)(2,1)S(1)}, bf16[1072,128]{1,0:T(8,128)(2,1)S(1)}, u32[]{:S(2)}, u32[]{:S(2)}) collective-permute-start(bf16[1072,128]{1,0:T(8,128)(2,1)S(1)} %get-tuple-element.28), channel_id=1, source_target_pairs={{0,4},{1,5},{4,0},{5,1},{8,12},{9,13},{12,8},{13,9},{2,6},{3,7},{6... | collective-permute-start | bytes 823304 | tf_op jit(solution)/shard_map/ppermute | solution.py:548
  15.0 1.2 %other_pieces.1 = (bf16[1072,128]{1,0:T(8,128)(2,1)S(1)}, bf16[1072,128]{1,0:T(8,128)(2,1)S(1)}, bf16[256,128]{1,0:T(8,128)(2,1)S(1)}, bf16[256,128]{1,0:T(8,128...) custom-call(f32[24,8]{1,0:T(8,128)S(1)} %summed_pack.1.own_ref.pack_ref, ...), custom_call_target="tpu_custom_call" | custom-call | tf_op jit(solution)/shard_map/other_pieces/pallas_call | solution.py:358
  16.1 2.6 %collective-permute-start.5 = (bf16[1072,128]{1,0:T(8,128)(2,1)S(1)}, bf16[1072,128]{1,0:T(8,128)(2,1)S(1)}, u32[]{:S(2)}, u32[]{:S(2)}) collective-permute-start(bf16[1072,128]{1,0:T(8,128)(2,1)S(1)} %get-tuple-element.30.far_ref), channel_id=1, source_target_pairs={{0,8},{12,4},{4,0},{8,12},{1,9},{13,5},{5,1},{9,13},{2,10},{14,6},... | collective-permute-start | bytes 823304 | tf_op jit(solution)/shard_map/ppermute | solution.py:570
  18.7 0.7 %collective-permute-start.4 = (bf16[1072,128]{1,0:T(8,128)(2,1)S(1)}, bf16[1072,128]{1,0:T(8,128)(2,1)S(1)}, u32[]{:S(2)}, u32[]{:S(2)}) collective-permute-start(bf16[1072,128]{1,0:T(8,128)(2,1)S(1)} %get-tuple-element.29.near_ref), channel_id=1, source_target_pairs={{0,0},{4,8},{8,4},{12,12},{1,1},{5,9},{9,5},{13,13},{2,2},{6,10},{... | collective-permute-start | bytes 823304 | tf_op jit(solution)/shard_map/ppermute | solution.py:566
  19.4 3.0 %collective-permute-done.3.came_ref.first_ref = bf16[1072,128]{1,0:T(8,128)(2,1)S(1)} collective-permute-done((bf16[1072,128]{1,0:T(8,128)(2,1)S(1)}, bf16[1072,128]{1,0:T(8,128)(2,1)S(1)}, u32[]{:S(2)}, u32[]{:S(2)}) %collective-permute-start.3) | collective-permute-done | bytes 274464 | tf_op jit(solution)/shard_map/ppermute | solution.py:548
  22.4 2.2 %collective-permute-start.6 = (bf16[1072,128]{1,0:T(8,128)(2,1)S(1)}, bf16[1072,128]{1,0:T(8,128)(2,1)S(1)}, u32[]{:S(2)}, u32[]{:S(2)}) collective-permute-start(bf16[1072,128]{1,0:T(8,128)(2,1)S(1)} %combine.1), channel_id=1, source_target_pairs={{0,4},{4,12},{8,0},{12,8},{1,5},{5,13},{9,1},{13,9},{2,6},{6,14},{... | collective-permute-start | bytes 823304 | tf_op jit(solution)/shard_map/ppermute | solution.py:572
  24.6 0.0 collective-permute-start.7
  24.6 1.5 %collective-permute-start.8 = (bf16[256,128]{1,0:T(8,128)(2,1)S(1)}, bf16[256,128]{1,0:T(8,128)(2,1)S(1)}, u32[]{:S(2)}, u32[]{:S(2)}) collective-permute-start(bf16[256,128]{1,0:T(8,128)(2,1)S(1)} %get-tuple-element.33), channel_id=1, source_target_pairs={{0,2},{1,3},{2,0},{3,1},{4,6},{5,7},{6,4},{7,5},{8,10},{9,11},{10,... | collective-permute-start | bytes 196616 | tf_op jit(solution)/shard_map/ppermute | solution.py:548
  26.1 0.0 collective-permute-done.7.orb_ref
  26.1 1.0 %collective-permute-start.9 = (bf16[256,128]{1,0:T(8,128)(2,1)S(1)}, bf16[256,128]{1,0:T(8,128)(2,1)S(1)}, u32[]{:S(2)}, u32[]{:S(2)}) collective-permute-start(bf16[256,128]{1,0:T(8,128)(2,1)S(1)} %get-tuple-element.34), channel_id=1, source_target_pairs={{0,3},{1,2},{2,1},{3,0},{4,7},{5,6},{6,5},{7,4},{8,11},{9,10},{10,... | collective-permute-start | bytes 196616 | tf_op jit(solution)/shard_map/ppermute | solution.py:548
  27.1 2.0 %collective-permute-done.8.walk_ref = bf16[256,128]{1,0:T(8,128)(2,1)S(1)} collective-permute-done((bf16[256,128]{1,0:T(8,128)(2,1)S(1)}, bf16[256,128]{1,0:T(8,128)(2,1)S(1)}, u32[]{:S(2)}, u32[]{:S(2)}) %collective-permute-start.8) | collective-permute-done | bytes 65568 | tf_op jit(solution)/shard_map/ppermute | solution.py:548
  29.1 1.0 %collective-permute-done.9.far_ref = bf16[256,128]{1,0:T(8,128)(2,1)S(1)} collective-permute-done((bf16[256,128]{1,0:T(8,128)(2,1)S(1)}, bf16[256,128]{1,0:T(8,128)(2,1)S(1)}, u32[]{:S(2)}, u32[]{:S(2)}) %collective-permute-start.9) | collective-permute-done | bytes 65568 | tf_op jit(solution)/shard_map/ppermute | solution.py:548
  30.1 0.0 collective-permute-done.5.cross_ref
  30.1 0.0 collective-permute-done.4.inside_ref
  30.1 8.0 %collective-permute-done.6.last_ref = bf16[1072,128]{1,0:T(8,128)(2,1)S(1)} collective-permute-done((bf16[1072,128]{1,0:T(8,128)(2,1)S(1)}, bf16[1072,128]{1,0:T(8,128)(2,1)S(1)}, u32[]{:S(2)}, u32[]{:S(2)}) %collective-permute-start.6) | collective-permute-done | bytes 274464 | tf_op jit(solution)/shard_map/ppermute | solution.py:572
  38.2 2.0 %taylor.1 = (bf16[256,128]{1,0:T(8,128)(2,1)S(1)}, bf16[256,128]{1,0:T(8,128)(2,1)S(1)}, f32[1,8]{1,0:T(1,128)S(1)}) custom-call(f32[24,8]{1,0:T(8,128)S(1)} %summed_pack.1.own_ref.pack_ref, f32[16,1]{1,0:T(8,128)S(1)} %get-tuple-element.24.log_ref, bf16[1072,128]{1,0:T(8,128)(2,1)S(1)} %get-tuple-element.27.kept_ref, ...), custom_call_target="tpu_custom_call" | custom-call | tf_op jit(solution)/shard_map/taylor/pallas_call | solution.py:469
  40.1 0.6 %collective-permute-start.16 = (bf16[256,128]{1,0:T(8,128)(2,1)S(1)}, bf16[256,128]{1,0:T(8,128)(2,1)S(1)}, u32[]{:S(2)}, u32[]{:S(2)}) collective-permute-start(bf16[256,128]{1,0:T(8,128)(2,1)S(1)} %get-tuple-element.35), channel_id=1, source_target_pairs={{0,13},{1,12},{4,9},{5,8},{8,5},{9,4},{12,1},{13,0},{2,15},{3,14},... | collective-permute-start | bytes 196616 | tf_op jit(solution)/shard_map/ppermute | solution.py:548
  40.7 1.6 %collective-permute-start.15 = (bf16[256,128]{1,0:T(8,128)(2,1)S(1)}, bf16[256,128]{1,0:T(8,128)(2,1)S(1)}, u32[]{:S(2)}, u32[]{:S(2)}) collective-permute-start(bf16[256,128]{1,0:T(8,128)(2,1)S(1)} %get-tuple-element.36.refs_0_), channel_id=1, source_target_pairs={{0,12},{1,13},{4,8},{5,9},{8,4},{9,5},{12,0},{13,1},{2,14},{3,15},... | collective-permute-start | bytes 196616 | tf_op jit(solution)/shard_map/ppermute | solution.py:548
  42.3 0.0 collective-permute-start.14
  42.4 2.5 %collective-permute-start.12 = (bf16[256,128]{1,0:T(8,128)(2,1)S(1)}, bf16[256,128]{1,0:T(8,128)(2,1)S(1)}, u32[]{:S(2)}, u32[]{:S(2)}) collective-permute-start(bf16[256,128]{1,0:T(8,128)(2,1)S(1)} %get-tuple-element.35), channel_id=1, source_target_pairs={{0,5},{1,4},{4,1},{5,0},{8,13},{9,12},{12,9},{13,8},{2,7},{3,6},{6... | collective-permute-start | bytes 196616 | tf_op jit(solution)/shard_map/ppermute | solution.py:548
  44.8 1.4 %collective-permute-start.10 = (bf16[256,128]{1,0:T(8,128)(2,1)S(1)}, bf16[256,128]{1,0:T(8,128)(2,1)S(1)}, u32[]{:S(2)}, u32[]{:S(2)}) collective-permute-start(bf16[256,128]{1,0:T(8,128)(2,1)S(1)} %get-tuple-element.35), channel_id=1, source_target_pairs={{0,1},{1,0},{4,5},{5,4},{8,9},{9,8},{12,13},{13,12},{2,3},{3,2},{6... | collective-permute-start | bytes 196616 | tf_op jit(solution)/shard_map/ppermute | solution.py:548
  46.2 0.0 collective-permute-done.16.refs_2_
  46.2 0.2 collective-permute-start.13
  46.5 0.4 collective-permute-done.15.refs_1_
  46.9 1.7 %collective-permute-start.11 = (bf16[256,128]{1,0:T(8,128)(2,1)S(1)}, bf16[256,128]{1,0:T(8,128)(2,1)S(1)}, u32[]{:S(2)}, u32[]{:S(2)}) collective-permute-start(bf16[256,128]{1,0:T(8,128)(2,1)S(1)} %get-tuple-element.36.refs_0_), channel_id=1, source_target_pairs={{0,4},{1,5},{4,0},{5,1},{8,12},{9,13},{12,8},{13,9},{2,6},{3,7},{6... | collective-permute-start | bytes 196616 | tf_op jit(solution)/shard_map/ppermute | solution.py:548
  48.5 0.7 %early_place.1 = (bf16[8,256,128]{2,1,0:T(8,128)(2,1)}, f32[1,8]{1,0:T(1,128)}) custom-call(bf16[256,128]{1,0:T(8,128)(2,1)S(1)} %get-tuple-element.36.refs_0_, bf16[256,128]{1,0:T(8,128)(2,1)S(1)} %collective-permute-done.15.refs_1_, bf16[256,128]{1,0:T(8,128)(2,1)S(1)} %collective-permute-done.16.refs_2_, f32[1,8]{1,0:T(1,128)S(1)} %get-tuple-element.37.refs_3_), custom_call_target="tpu_custom_call" | custom-call | tf_op jit(solution)/shard_map/early_place/pallas_call | solution.py:521
  49.2 1.3 %collective-permute-done.14.refs_4_ = bf16[256,128]{1,0:T(8,128)(2,1)S(1)} collective-permute-done((bf16[256,128]{1,0:T(8,128)(2,1)S(1)}, bf16[256,128]{1,0:T(8,128)(2,1)S(1)}, u32[]{:S(2)}, u32[]{:S(2)}) %collective-permute-start.14) | collective-permute-done | bytes 65568 | tf_op jit(solution)/shard_map/ppermute | solution.py:548
  50.5 0.0 collective-permute-done.12.refs_2_
  50.5 0.0 collective-permute-done.10.refs_0_
  50.5 2.7 %collective-permute-done.13.refs_3_ = bf16[256,128]{1,0:T(8,128)(2,1)S(1)} collective-permute-done((bf16[256,128]{1,0:T(8,128)(2,1)S(1)}, bf16[256,128]{1,0:T(8,128)(2,1)S(1)}, u32[]{:S(2)}, u32[]{:S(2)}) %collective-permute-start.13) | collective-permute-done | bytes 65568 | tf_op jit(solution)/shard_map/ppermute | solution.py:548
  53.2 0.0 collective-permute-done.11.refs_1_
  53.2 0.8 %late_place.1 = bf16[8,256,128]{2,1,0:T(8,128)(2,1)} custom-call(bf16[256,128]{1,0:T(8,128)(2,1)S(1)} %collective-permute-done.10.refs_0_, bf16[256,128]{1,0:T(8,128)(2,1)S(1)} %collective-permute-done.11.refs_1_, bf16[256,128]{1,0:T(8,128)(2,1)S(1)} %collective-permute-done.12.refs_2_, ...), custom_call_target="tpu_custom_call", output_to_operand_aliasing={{}: (5, {})} | custom-call | tf_op jit(solution)/shard_map/late_place/pallas_call | solution.py:530
  (2 shorter events, 0.0 us)
Async XLA Ops:
  4.2 7.4 %collective-permute-start.2 = (bf16[8,256,256]{2,1,0:T(8,128)(2,1)S(1)}, bf16[8,256,256]{2,1,0:T(8,128)(2,1)S(1)}, u32[]{:S(2)}, u32[]{:S(2)}) collective-permute-start(bf16[8,256,256]{2,1,0:T(8,128)(2,1)S(1)} %get-tuple-element.23), channel_id=1, source_target_pairs={{0,1},{1,0},{2,3},{3,2},{4,5},{5,4},{6,7},{7,6},{8,9},{9,8},{10,11... | collective-permute-start | bytes 3145736 | tf_op jit(solution)/shard_map/ppermute | solution.py:548
  4.7 2.3 %collective-permute-start = (f32[24,8]{1,0:T(8,128)S(1)}, f32[24,8]{1,0:T(8,128)S(1)}, u32[]{:S(2)}, u32[]{:S(2)}) collective-permute-start(f32[24,8]{1,0:T(8,128)S(1)} %get-tuple-element.21.own_ref), channel_id=1, source_target_pairs={{0,1},{1,0},{2,3},{3,2},{4,5},{5,4},{6,7},{7,6},{8,9},{9,8},{10,11... | collective-permute-start | bytes 2312 | tf_op jit(solution)/shard_map/ppermute | solution.py:548
  7.0 4.5 %collective-permute-start.1 = (f32[24,8]{1,0:T(8,128)S(1)}, f32[24,8]{1,0:T(8,128)S(1)}, u32[]{:S(2)}, u32[]{:S(2)}) collective-permute-start(f32[24,8]{1,0:T(8,128)S(1)} %summed_pack.1.own_ref.pack_ref), channel_id=1, source_target_pairs={{0,2},{1,3},{2,0},{3,1},{4,6},{5,7},{6,4},{7,5},{8,10},{9,11},{10,... | collective-permute-start | bytes 2312 | tf_op jit(solution)/shard_map/ppermute | solution.py:548
  12.8 9.6 %collective-permute-start.3 = (bf16[1072,128]{1,0:T(8,128)(2,1)S(1)}, bf16[1072,128]{1,0:T(8,128)(2,1)S(1)}, u32[]{:S(2)}, u32[]{:S(2)}) collective-permute-start(bf16[1072,128]{1,0:T(8,128)(2,1)S(1)} %get-tuple-element.28), channel_id=1, source_target_pairs={{0,4},{1,5},{4,0},{5,1},{8,12},{9,13},{12,8},{13,9},{2,6},{3,7},{6... | collective-permute-start | bytes 823304 | tf_op jit(solution)/shard_map/ppermute | solution.py:548
  16.1 14.0 %collective-permute-start.5 = (bf16[1072,128]{1,0:T(8,128)(2,1)S(1)}, bf16[1072,128]{1,0:T(8,128)(2,1)S(1)}, u32[]{:S(2)}, u32[]{:S(2)}) collective-permute-start(bf16[1072,128]{1,0:T(8,128)(2,1)S(1)} %get-tuple-element.30.far_ref), channel_id=1, source_target_pairs={{0,8},{12,4},{4,0},{8,12},{1,9},{13,5},{5,1},{9,13},{2,10},{14,6},... | collective-permute-start | bytes 823304 | tf_op jit(solution)/shard_map/ppermute | solution.py:570
  18.7 11.4 %collective-permute-start.4 = (bf16[1072,128]{1,0:T(8,128)(2,1)S(1)}, bf16[1072,128]{1,0:T(8,128)(2,1)S(1)}, u32[]{:S(2)}, u32[]{:S(2)}) collective-permute-start(bf16[1072,128]{1,0:T(8,128)(2,1)S(1)} %get-tuple-element.29.near_ref), channel_id=1, source_target_pairs={{0,0},{4,8},{8,4},{12,12},{1,1},{5,9},{9,5},{13,13},{2,2},{6,10},{... | collective-permute-start | bytes 823304 | tf_op jit(solution)/shard_map/ppermute | solution.py:566
  22.4 15.8 %collective-permute-start.6 = (bf16[1072,128]{1,0:T(8,128)(2,1)S(1)}, bf16[1072,128]{1,0:T(8,128)(2,1)S(1)}, u32[]{:S(2)}, u32[]{:S(2)}) collective-permute-start(bf16[1072,128]{1,0:T(8,128)(2,1)S(1)} %combine.1), channel_id=1, source_target_pairs={{0,4},{4,12},{8,0},{12,8},{1,5},{5,13},{9,1},{13,9},{2,6},{6,14},{... | collective-permute-start | bytes 823304 | tf_op jit(solution)/shard_map/ppermute | solution.py:572
  24.6 1.5 %collective-permute-start.7 = (bf16[256,128]{1,0:T(8,128)(2,1)S(1)}, bf16[256,128]{1,0:T(8,128)(2,1)S(1)}, u32[]{:S(2)}, u32[]{:S(2)}) collective-permute-start(bf16[256,128]{1,0:T(8,128)(2,1)S(1)} %get-tuple-element.32), channel_id=1, source_target_pairs={{0,1},{1,0},{2,3},{3,2},{4,5},{5,4},{6,7},{7,6},{8,9},{9,8},{10,11... | collective-permute-start | bytes 196616 | tf_op jit(solution)/shard_map/ppermute | solution.py:548
  24.6 4.5 %collective-permute-start.8 = (bf16[256,128]{1,0:T(8,128)(2,1)S(1)}, bf16[256,128]{1,0:T(8,128)(2,1)S(1)}, u32[]{:S(2)}, u32[]{:S(2)}) collective-permute-start(bf16[256,128]{1,0:T(8,128)(2,1)S(1)} %get-tuple-element.33), channel_id=1, source_target_pairs={{0,2},{1,3},{2,0},{3,1},{4,6},{5,7},{6,4},{7,5},{8,10},{9,11},{10,... | collective-permute-start | bytes 196616 | tf_op jit(solution)/shard_map/ppermute | solution.py:548
  26.1 4.0 %collective-permute-start.9 = (bf16[256,128]{1,0:T(8,128)(2,1)S(1)}, bf16[256,128]{1,0:T(8,128)(2,1)S(1)}, u32[]{:S(2)}, u32[]{:S(2)}) collective-permute-start(bf16[256,128]{1,0:T(8,128)(2,1)S(1)} %get-tuple-element.34), channel_id=1, source_target_pairs={{0,3},{1,2},{2,1},{3,0},{4,7},{5,6},{6,5},{7,4},{8,11},{9,10},{10,... | collective-permute-start | bytes 196616 | tf_op jit(solution)/shard_map/ppermute | solution.py:548
  40.1 6.1 %collective-permute-start.16 = (bf16[256,128]{1,0:T(8,128)(2,1)S(1)}, bf16[256,128]{1,0:T(8,128)(2,1)S(1)}, u32[]{:S(2)}, u32[]{:S(2)}) collective-permute-start(bf16[256,128]{1,0:T(8,128)(2,1)S(1)} %get-tuple-element.35), channel_id=1, source_target_pairs={{0,13},{1,12},{4,9},{5,8},{8,5},{9,4},{12,1},{13,0},{2,15},{3,14},... | collective-permute-start | bytes 196616 | tf_op jit(solution)/shard_map/ppermute | solution.py:548
  40.7 6.2 %collective-permute-start.15 = (bf16[256,128]{1,0:T(8,128)(2,1)S(1)}, bf16[256,128]{1,0:T(8,128)(2,1)S(1)}, u32[]{:S(2)}, u32[]{:S(2)}) collective-permute-start(bf16[256,128]{1,0:T(8,128)(2,1)S(1)} %get-tuple-element.36.refs_0_), channel_id=1, source_target_pairs={{0,12},{1,13},{4,8},{5,9},{8,4},{9,5},{12,0},{13,1},{2,14},{3,15},... | collective-permute-start | bytes 196616 | tf_op jit(solution)/shard_map/ppermute | solution.py:548
  42.3 8.2 %collective-permute-start.14 = (bf16[256,128]{1,0:T(8,128)(2,1)S(1)}, bf16[256,128]{1,0:T(8,128)(2,1)S(1)}, u32[]{:S(2)}, u32[]{:S(2)}) collective-permute-start(bf16[256,128]{1,0:T(8,128)(2,1)S(1)} %get-tuple-element.35), channel_id=1, source_target_pairs={{0,9},{1,8},{4,13},{5,12},{8,1},{9,0},{12,5},{13,4},{2,11},{3,10},... | collective-permute-start | bytes 196616 | tf_op jit(solution)/shard_map/ppermute | solution.py:548
  42.4 8.2 %collective-permute-start.12 = (bf16[256,128]{1,0:T(8,128)(2,1)S(1)}, bf16[256,128]{1,0:T(8,128)(2,1)S(1)}, u32[]{:S(2)}, u32[]{:S(2)}) collective-permute-start(bf16[256,128]{1,0:T(8,128)(2,1)S(1)} %get-tuple-element.35), channel_id=1, source_target_pairs={{0,5},{1,4},{4,1},{5,0},{8,13},{9,12},{12,9},{13,8},{2,7},{3,6},{6... | collective-permute-start | bytes 196616 | tf_op jit(solution)/shard_map/ppermute | solution.py:548
  44.8 5.7 %collective-permute-start.10 = (bf16[256,128]{1,0:T(8,128)(2,1)S(1)}, bf16[256,128]{1,0:T(8,128)(2,1)S(1)}, u32[]{:S(2)}, u32[]{:S(2)}) collective-permute-start(bf16[256,128]{1,0:T(8,128)(2,1)S(1)} %get-tuple-element.35), channel_id=1, source_target_pairs={{0,1},{1,0},{4,5},{5,4},{8,9},{9,8},{12,13},{13,12},{2,3},{3,2},{6... | collective-permute-start | bytes 196616 | tf_op jit(solution)/shard_map/ppermute | solution.py:548
  46.2 7.0 %collective-permute-start.13 = (bf16[256,128]{1,0:T(8,128)(2,1)S(1)}, bf16[256,128]{1,0:T(8,128)(2,1)S(1)}, u32[]{:S(2)}, u32[]{:S(2)}) collective-permute-start(bf16[256,128]{1,0:T(8,128)(2,1)S(1)} %get-tuple-element.36.refs_0_), channel_id=1, source_target_pairs={{0,8},{1,9},{4,12},{5,13},{8,0},{9,1},{12,4},{13,5},{2,10},{3,11},... | collective-permute-start | bytes 196616 | tf_op jit(solution)/shard_map/ppermute | solution.py:548
  46.9 6.4 %collective-permute-start.11 = (bf16[256,128]{1,0:T(8,128)(2,1)S(1)}, bf16[256,128]{1,0:T(8,128)(2,1)S(1)}, u32[]{:S(2)}, u32[]{:S(2)}) collective-permute-start(bf16[256,128]{1,0:T(8,128)(2,1)S(1)} %get-tuple-element.36.refs_0_), channel_id=1, source_target_pairs={{0,4},{1,5},{4,0},{5,1},{8,12},{9,13},{12,8},{13,9},{2,6},{3,7},{6... | collective-permute-start | bytes 196616 | tf_op jit(solution)/shard_map/ppermute | solution.py:548
